TPU v7x, 256 devices: a whole 4x4x8 slice. The times are simulated.
256 devices in a mesh: blk: 64 (over x, z, y_hi), col: 4 (over y_lo, core).
Axes of the slice: x: 4, y: 4 (y_hi: 2, y_lo: 2; y = y_hi * 2 + y_lo), z: 8, core: 2. Of those that a mesh axis runs over, the one named last changes fastest.
Arguments:
- points: bfloat16 [32768, 128], P(('blk', 'col')), may hold values from -4.5 to 4.5
- targets: float32 [32768, 32], P(('blk', 'col')), may hold values from -6 to 6
- pivots: int32 [2, 256], replicated, may hold values from 0 to 32767, as said below
Outputs:
- factor: bfloat16 [32768, 512], P(('blk', 'col'))
- solution: float32 [32768, 32], P(('blk', 'col'))
- residual: float32 [32768, 32], P(('blk', 'col'))
Inputs may be any that keep to these rules, and one draw needn't show every extreme that they name: `pivots`: the 512 indices are distinct; 0 and 32767 are among them.
All inputs are finite; a program needn't handle non-finite values.
Results may differ from a plain program's by a relative error of at most 0.012.
Values may be sent and summed in bfloat16 or wider, within the bound.
No kernel may reach another device: no remote copies, remote signals or barrier semaphores. Data moves between devices by JAX's collectives and lax.ppermute only.
A program may use at most 64 MiB of HBM per device.

v0:
```python
import functools

import jax
import jax.numpy as jnp
from jax import lax
from jax.experimental import pallas as pl
from jax.experimental.pallas import tpu as pltpu
from jax.sharding import Mesh, PartitionSpec as P

ITERS = 3
NOISE = 0.5
JITTER = 0.05
HIGHEST = lax.Precision.HIGHEST
INTERPRET = False
GROUP = 8
STRIDE = 8
BLOCK = 128
F32 = jnp.float32
BF16 = jnp.bfloat16

U = ("z",)
CHIPS = ("x", "yh", "yl")
ALL = ("x", "z", "yh", "yl", "c")


def swap(blocks, axes):
    return lax.all_to_all(blocks, axes, 0, 0, tiled=False)


def share(block, axes):
    count = lax.axis_size(axes)
    return swap(jnp.broadcast_to(block[None], (count,) + block.shape), axes)


def partner(values):
    return lax.ppermute(values, "c", [(0, 1), (1, 0)])


def core_first(mine, other):
    first = lax.axis_index("c") == 0
    return jnp.concatenate([jnp.where(first, mine, other), jnp.where(first, other, mine)], axis=0)


def half(values, at):
    count = values.shape[0] // 2
    return lax.dynamic_slice_in_dim(values, at * count, count, 0)


def three_parts(values):
    high = lax.reduce_precision(values, 8, 7)
    rest = values - high
    middle = lax.reduce_precision(rest, 8, 7)
    low = rest - middle
    return [part.astype(BF16) for part in (high, middle, low)]


def dot_nt(left, right, precision=None):
    return lax.dot_general(
        left, right, (((1,), (1,)), ((), ())), precision=precision, preferred_element_type=F32
    )


def dot_nn(left, right, precision=None):
    return lax.dot_general(
        left, right, (((1,), (0,)), ((), ())), precision=precision, preferred_element_type=F32
    )


def split(values):
    high = values.astype(BF16)
    rest = values - high.astype(F32)
    middle = rest.astype(BF16)
    return high, middle, (rest - middle.astype(F32)).astype(BF16)


def extended(rows, left):
    wide = rows.astype(F32)
    lane = lax.broadcasted_iota(jnp.int32, wide.shape, 1)
    parts = split(jnp.sum(wide * wide, axis=1, keepdims=True) * (-1.0 / 64.0))
    first, ones = (0, 3) if left else (3, 0)
    tail = jnp.where((lane >= ones) & (lane < ones + 3), 1.0, 0.0)
    for k in range(3):
        tail = jnp.where(lane == first + k, parts[k].astype(F32), tail)
    head = (wide * 0.03125).astype(BF16) if left else rows
    return jnp.concatenate([head, tail.astype(BF16)], axis=1)


def stacked_dot(dot, values, wide):
    count = values.shape[0]
    parts = jnp.concatenate(split(values), axis=0)
    a = dot(parts, wide[0])
    b = dot(parts[:2 * count], wide[1])
    c = dot(parts[:count], wide[2])
    return a[:count] + ((a[count:2 * count] + b[:count]) + (a[2 * count:] + b[count:] + c))


def eliminate(groups):
    order = len(groups) * GROUP
    lane = lax.broadcasted_iota(jnp.int32, (GROUP, order), 1)
    sub = lax.broadcasted_iota(jnp.int32, (GROUP, order), 0)
    groups = list(groups)
    for first in range(0, order, STRIDE):
        at = first // GROUP
        cols = [None] * len(groups)
        for g in range(at, len(groups)):
            cols[g] = [
                jnp.broadcast_to(groups[g][:, first + j:first + j + 1], (GROUP, order))
                for j in range(STRIDE)
            ]
        home = groups[at]
        own = cols[at]
        rows, inverses, steps = [], [], []
        for j in range(STRIDE):
            r = first % GROUP + j
            inverse = 1.0 / jnp.broadcast_to(own[j][r:r + 1, :], (GROUP, order))
            mult = jnp.where(sub > r, own[j] * inverse, 0.0)
            steps.append(
                [
                    jnp.broadcast_to(own[l][r:r + 1, :], (GROUP, order))
                    for l in range(j + 1, STRIDE)
                ]
            )
            for l in range(j + 1, STRIDE):
                own[l] = own[l] - mult * steps[j][l - j - 1]
            row = jnp.where(
                lane == first + j, 1.0, jnp.broadcast_to(home[r:r + 1, :], (GROUP, order))
            )
            home = jnp.where((lane == first + j) & (sub > r), 0.0, home) - mult * row
            rows.append(jnp.where((lane > first + j) & (lane < first + STRIDE), 0.0, row))
            inverses.append(inverse)
        groups[at] = home
        for g in range(at + 1, len(groups)):
            col = cols[g]
            value = jnp.where((lane >= first) & (lane < first + STRIDE), 0.0, groups[g])
            for j in range(STRIDE):
                mult = col[j] * inverses[j]
                for l in range(j + 1, STRIDE):
                    col[l] = col[l] - mult * steps[j][l - j - 1]
                value = value - mult * rows[j]
            groups[g] = value
    return groups


def inverse_of_block(diag):
    if INTERPRET:
        return jnp.linalg.inv(jnp.linalg.cholesky(diag))
    groups = eliminate([diag[g:g + GROUP, :] for g in range(0, BLOCK, GROUP)])
    done = jnp.concatenate(groups, axis=0)
    row = lax.broadcasted_iota(jnp.int32, (BLOCK, BLOCK), 0)
    col = lax.broadcasted_iota(jnp.int32, (BLOCK, BLOCK), 1)
    pivots = jnp.sum(jnp.where(row == col, done, 0.0), axis=1, keepdims=True)
    unit = jnp.where(col < row, done, jnp.where(col == row, 1.0, 0.0))
    return unit * lax.rsqrt(pivots)


def inverse_factor(work_ref):
    order = work_ref.shape[0]

    def stage(j, carry):
        start = pl.multiple_of(j * BLOCK, BLOCK)
        here = pl.ds(start, BLOCK)
        below = lax.broadcasted_iota(jnp.int32, (order, BLOCK), 0) >= start + BLOCK
        local = inverse_of_block(work_ref[here, here])
        work_ref[here, :] = dot_nn(local, work_ref[here, :], HIGHEST)
        low = jnp.where(below, dot_nt(work_ref[:, here], local, HIGHEST), 0.0)
        work_ref[here, here] = local
        strip = work_ref[here, :]
        work_ref[:, here] = jnp.where(below, 0.0, work_ref[:, here])
        work_ref[...] = work_ref[...] - dot_nn(low, strip, HIGHEST)
        return carry

    lax.fori_loop(0, order // BLOCK, stage, 0)
    row = lax.broadcasted_iota(jnp.int32, (order, order), 0)
    col = lax.broadcasted_iota(jnp.int32, (order, order), 1)
    return jnp.where(col <= row, work_ref[...], 0.0)


def unit_matrix(order, scale):
    row = lax.broadcasted_iota(jnp.int32, (order, order), 0)
    col = lax.broadcasted_iota(jnp.int32, (order, order), 1)
    return jnp.where(row == col, scale, 0.0)


def joined(ref):
    return jnp.concatenate([ref[i] for i in range(ref.shape[0])], axis=1)


def setup_body(
    picked_ref, keys_ref, rows_ref, targets_ref,
    high_ref, mid_ref, low_ref, key_ref, row_ref, out_ref, work_ref, pack_ref,
):
    piv = picked_ref.shape[0]
    chunks = out_ref.shape[0]
    picked = picked_ref[...]
    right = extended(picked, False)
    work_ref[...] = jnp.exp(dot_nt(extended(picked, True), right)) + unit_matrix(piv, JITTER)
    key_ref[...] = extended(keys_ref[...], True)

    def rows_step(i, carry):
        here = pl.ds(pl.multiple_of(i * 256, 256), 256)
        row_ref[here, :] = extended(rows_ref[here, :], False)
        return carry

    lax.fori_loop(0, rows_ref.shape[0] // 256, rows_step, 0)
    inverse = inverse_factor(work_ref)
    wide = dot_nt(jnp.exp(dot_nt(key_ref[...], right)), inverse, HIGHEST)
    parts = split(wide)
    high_ref[...] = parts[0]
    mid_ref[...] = parts[1]
    low_ref[...] = parts[2]
    at = 0
    for i in range(piv // BLOCK):
        strip = lax.dot_general(
            wide[:, i * BLOCK:(i + 1) * BLOCK], wide[:, :(i + 1) * BLOCK],
            (((0,), (0,)), ((), ())), precision=HIGHEST, preferred_element_type=F32,
        )
        for j in range(i + 1):
            pack_ref[at:at + BLOCK, :] = strip[:, j * BLOCK:(j + 1) * BLOCK]
            at += BLOCK
    targets = joined(targets_ref)
    proj = dot_nn(targets, wide, HIGHEST)
    squares = jnp.broadcast_to(
        jnp.sum(targets * targets, axis=1, keepdims=True), (proj.shape[0], BLOCK)
    )
    part = at // chunks
    per = proj.shape[0] // chunks
    split_by = piv // BLOCK
    for i in range(chunks):
        out_ref[i, 0:part, :] = pack_ref[i * part:(i + 1) * part, :]
        for p in range(per):
            row = i * per + p
            for k in range(split_by):
                out_ref[i, part + p * split_by + k, :] = proj[row, k * BLOCK:(k + 1) * BLOCK]
            out_ref[i, part + per * split_by + p, :] = squares[row, :]


def gram_solve(proj, inverse):
    return stacked_dot(dot_nn, stacked_dot(dot_nt, proj, inverse), inverse)


def product(direction, key_ref, row_ref, out_ref):
    keys = key_ref.shape[0]
    count = direction.shape[0]
    parts = jnp.concatenate(split(direction), axis=0)
    chunk = 256

    def rows_step(i, carry):
        rows = row_ref[pl.ds(pl.multiple_of(i * chunk, chunk), chunk), :]
        total = jnp.zeros((count, chunk), F32)
        for start in range(0, keys, chunk):
            values = jnp.exp(dot_nt(key_ref[start:start + chunk, :], rows))
            high = values.astype(BF16)
            low = (values - high.astype(F32)).astype(BF16)
            a = dot_nn(parts[:, start:start + chunk], high)
            b = dot_nn(parts[:2 * count, start:start + chunk], low)
            total = total + (
                a[:count] + ((a[count:2 * count] + b[:count]) + (a[2 * count:] + b[count:]))
            )
        for k in range(chunk // BLOCK):
            out_ref[i * (chunk // BLOCK) + k] = total[:, k * BLOCK:(k + 1) * BLOCK]
        return carry

    lax.fori_loop(0, row_ref.shape[0] // chunk, rows_step, 0)


def next_direction(residual, coef, wide):
    return (residual - stacked_dot(dot_nt, coef, wide)) * (1.0 / NOISE)


def begin_body(
    packed_ref, res_ref, high_ref, mid_ref, low_ref, key_ref, row_ref,
    inv_high, inv_mid, inv_low, proj_ref, dir_ref, inner_ref, sq_ref, out_ref, work_ref, pack_ref,
):
    piv = work_ref.shape[0]
    chunks = packed_ref.shape[0]
    split_by = piv // BLOCK
    part = split_by * (split_by + 1) // 2 * BLOCK // chunks
    per = proj_ref.shape[0] // chunks
    for i in range(chunks):
        pack_ref[i * part:(i + 1) * part, :] = packed_ref[i, 0:part, :]
        for p in range(per):
            row = i * per + p
            for k in range(split_by):
                proj_ref[row, k * BLOCK:(k + 1) * BLOCK] = packed_ref[i, part + p * split_by + k, :]
            sq_ref[row, :] = packed_ref[i, part + per * split_by + p, :]
    at = 0
    for i in range(split_by):
        for j in range(i + 1):
            piece = pack_ref[at:at + BLOCK, :]
            work_ref[i * BLOCK:(i + 1) * BLOCK, j * BLOCK:(j + 1) * BLOCK] = piece
            if j < i:
                work_ref[j * BLOCK:(j + 1) * BLOCK, i * BLOCK:(i + 1) * BLOCK] = piece.T
            at += BLOCK
    work_ref[...] = work_ref[...] + unit_matrix(piv, NOISE)
    inverse = inverse_factor(work_ref)
    inverse = split(inverse)
    inv_high[...] = inverse[0]
    inv_mid[...] = inverse[1]
    inv_low[...] = inverse[2]
    proj = proj_ref[...]
    coef = gram_solve(proj, inverse)
    inner_ref[...] = (sq_ref[...] - jnp.sum(proj * coef, axis=1, keepdims=True)) * (1.0 / NOISE)
    direction = next_direction(joined(res_ref), coef, (high_ref[...], mid_ref[...], low_ref[...]))
    for i in range(dir_ref.shape[0]):
        dir_ref[i] = direction[:, i * BLOCK:(i + 1) * BLOCK]
    product(direction, key_ref, row_ref, out_ref)


def project_body(image_ref, res_ref, dir_ref, high_ref, mid_ref, low_ref, out_ref):
    image = joined(image_ref)
    residual = joined(res_ref)
    direction = joined(dir_ref)
    piv = high_ref.shape[1]
    out_ref[:, :piv] = stacked_dot(dot_nn, image, (high_ref[...], mid_ref[...], low_ref[...]))
    curve = jnp.sum(direction * image, axis=1, keepdims=True)
    cross = jnp.sum(residual * image, axis=1, keepdims=True)
    own = jnp.sum(image * image, axis=1, keepdims=True)
    lane = lax.broadcasted_iota(jnp.int32, (image.shape[0], BLOCK), 1)
    out_ref[:, piv:] = jnp.where(lane == 0, curve, jnp.where(lane == 1, cross, own))


def advance_body(
    packed_ref, image_ref, res_ref, dir_ref, sol_ref, proj_ref, inner_ref, sq_ref,
    inv_high, inv_mid, inv_low, high_ref, mid_ref, low_ref, key_ref, row_ref,
    new_res, new_dir, new_sol, new_proj, new_inner, new_sq, out_ref,
):
    piv = proj_ref.shape[1]
    total = packed_ref[0]
    for i in range(1, packed_ref.shape[0]):
        total = total + packed_ref[i]
    inner = inner_ref[:, 0:1]
    alpha = inner / total[:, piv:piv + 1]
    squares = (
        sq_ref[:, 0:1] - 2.0 * alpha * total[:, piv + 1:piv + 2]
        + alpha * alpha * total[:, piv + 2:piv + 3]
    )
    proj = proj_ref[...] - alpha * total[:, :piv]
    coef = gram_solve(proj, (inv_high[...], inv_mid[...], inv_low[...]))
    inner_next = (squares - jnp.sum(proj * coef, axis=1, keepdims=True)) * (1.0 / NOISE)
    beta = inner_next / inner
    new_proj[...] = proj
    new_inner[...] = jnp.broadcast_to(inner_next, new_inner.shape)
    new_sq[...] = jnp.broadcast_to(squares, new_sq.shape)
    direction = joined(dir_ref)
    residual = joined(res_ref) - alpha * joined(image_ref)
    solution = joined(sol_ref) + alpha * direction
    direction = (
        next_direction(residual, coef, (high_ref[...], mid_ref[...], low_ref[...]))
        + beta * direction
    )
    for i in range(new_dir.shape[0]):
        new_res[i] = residual[:, i * BLOCK:(i + 1) * BLOCK]
        new_dir[i] = direction[:, i * BLOCK:(i + 1) * BLOCK]
        new_sol[i] = solution[:, i * BLOCK:(i + 1) * BLOCK]
    product(direction, key_ref, row_ref, out_ref)


def call(body, name, outs, scratch, *args):
    return pl.pallas_call(
        body,
        out_shape=[jax.ShapeDtypeStruct(shape, dtype) for shape, dtype in outs],
        scratch_shapes=scratch,
        compiler_params=pltpu.CompilerParams(vmem_limit_bytes=48 << 20),
        interpret=INTERPRET,
        name=name,
    )(*args)


def per_device(points, targets, pivots):
    own = points.shape[0]
    columns = targets.shape[1]
    u_size, chips = lax.axis_size(U), lax.axis_size(CHIPS)
    u_at, core = lax.axis_index(U), lax.axis_index("c")
    v_size = 2 * chips
    flat_pivots = pivots.reshape(-1)
    piv = flat_pivots.shape[0]
    part = piv // v_size
    per = columns // v_size

    packed = share(jnp.concatenate([points] + three_parts(targets.T), axis=0), U)
    key_points = packed[:, :own].reshape(u_size * own, -1)
    parts = packed[:, own:].astype(F32).reshape(u_size, 3, columns, own)
    residual = parts[:, 0] + parts[:, 1] + parts[:, 2]

    place = jnp.zeros((), jnp.int32)
    for axis in ALL:
        here = jnp.arange(u_size, dtype=jnp.int32) if axis in U else lax.axis_index(axis)
        place = place * lax.axis_size(axis) + here
    key_ids = (place[:, None] * own + jnp.arange(own, dtype=jnp.int32)[None, :]).reshape(1, -1)

    owned = (flat_pivots[:, None] == key_ids).astype(BF16)
    held = jnp.dot(owned, key_points, preferred_element_type=F32).astype(BF16)
    held = half(held, core) + partner(half(held, 1 - core))
    packed = swap(
        jnp.concatenate(
            [
                jnp.broadcast_to(points[None], (chips,) + points.shape),
                held.reshape(chips, part, -1),
            ],
            axis=1,
        ),
        CHIPS,
    )
    picked = jnp.sum(packed[:, own:].astype(F32), axis=0).astype(BF16)
    picked = share(picked, CHIPS)
    picked = core_first(picked, partner(picked)).reshape(piv, -1)
    row_points = packed[:, :own].reshape(chips * own, -1)
    row_points = jnp.concatenate([row_points, partner(row_points)], axis=0)

    keys, rows = key_points.shape[0], row_points.shape[0]
    lower = piv // BLOCK * (piv // BLOCK + 1) // 2 * BLOCK
    height = (lower // v_size + per * (piv // BLOCK + 1) + 7) // 8 * 8
    work = [pltpu.VMEM((piv, piv), F32), pltpu.VMEM((lower, BLOCK), F32)]
    *wide, key_left, row_right, packed = call(
        setup_body, "setup_factor",
        [((keys, piv), BF16)] * 3
        + [((keys, 2 * BLOCK), BF16), ((rows, 2 * BLOCK), BF16), ((v_size, height, BLOCK), F32)],
        work, picked, key_points, row_points, residual,
    )
    factor = lax.dynamic_slice_in_dim(wide[0], u_at * own, own, 0)
    packed = jnp.sum(swap(half(packed, core) + partner(half(packed, 1 - core)), CHIPS), axis=0)
    packed = share(packed, CHIPS)
    packed = core_first(packed, partner(packed))

    state = ((u_size, columns, own), F32)
    scalar = ((columns, BLOCK), F32)
    partial_shape = ((v_size, columns, own), F32)
    *inverse, projection, direction, inner, squares, partial = call(
        begin_body, "begin",
        [((piv, piv), BF16)] * 3
        + [((columns, piv), F32), state, scalar, scalar, partial_shape],
        work, packed, residual, *wide, key_left, row_right,
    )
    solution_now = jnp.zeros(state[0], F32)
    for step in range(ITERS):
        direction_own = lax.dynamic_index_in_dim(direction, u_at, 0, keepdims=False)
        blocks = partial[:chips] + partner(partial[chips:])
        image_own = jnp.sum(swap(blocks, CHIPS), axis=0) + NOISE * direction_own
        if step + 1 == ITERS:
            break
        image = share(image_own, U)
        packed = call(
            project_body, "project", [((columns, piv + BLOCK), F32)], [],
            image, residual, direction, *wide,
        )[0]
        packed = packed + partner(packed)
        packed = packed + lax.ppermute(packed, CHIPS[2], [(0, 1), (1, 0)])
        packed = share(packed, CHIPS[:2])
        residual, direction, solution_now, projection, inner, squares, partial = call(
            advance_body, "advance",
            [state, state, state, ((columns, piv), F32), scalar, scalar, partial_shape], [],
            packed, image, residual, direction, solution_now, projection, inner, squares,
            *inverse, *wide, key_left, row_right,
        )
    curve = jnp.sum(direction_own * image_own, axis=1)
    curve = jnp.zeros((1, BLOCK), F32).at[0, :columns].set(curve)
    curve = jnp.sum(share(curve, ALL), axis=0)
    alpha = inner[:, :1] / curve[0, :columns, None]
    solution_own = lax.dynamic_index_in_dim(solution_now, u_at, 0, keepdims=False)
    residual_own = lax.dynamic_index_in_dim(residual, u_at, 0, keepdims=False)
    solution_own = solution_own + alpha * direction_own
    residual_own = residual_own - alpha * image_own
    return (factor, solution_own.T, residual_own.T)


def solution(mesh):
    sizes = (4, 8, 2, 2, 2) if mesh.devices.size == 256 else (2, 2, 1, 2, 2)
    grid = Mesh(mesh.devices.reshape(sizes), ALL)
    return jax.shard_map(
        per_device,
        mesh=grid,
        in_specs=(P(ALL, None), P(ALL, None), P()),
        out_specs=(P(ALL, None), P(ALL, None), P(ALL, None)),
        check_vma=False,
    )
```

profile of v0, /device:TPU:1, one launch (start us, length us, event | category | flops | bytes accessed | tf_op | source)
XLA Modules:
  0.0 339.3 jit_solution(10980389197731291604)
XLA Ops:
  3.0 9.0 %all-to-all-start = ((bf16[8,224,128]{2,1,0:T(8,128)(2,1)}), bf16[8,224,128]{2,1,0:T(8,128)(2,1)S(1)}, u32[]{:S(2)}, u32[]{:S(2)}) async-start(bf16[8,224,128]{2,1,0:T(8,128)(2,1)} %broadcast_in_dim.27), calls=%async_computation | async-start | bytes 917504 | tf_op jit(solution)/shard_map/all_to_all | solution.py:27
  12.8 15.7 %all-to-all-done = bf16[8,224,128]{2,1,0:T(8,128)(2,1)S(1)} async-done(((bf16[8,224,128]{2,1,0:T(8,128)(2,1)}), bf16[8,224,128]{2,1,0:T(8,128)(2,1)S(1)}, u32[]{:S(2)}, u32[]{:S(2)}) %all-to-all-start) | async-done | bytes 458784 | tf_op jit(solution)/shard_map/all_to_all | solution.py:27
  30.7 18.1 %all_to_all.65 = bf16[16,144,128]{2,1,0:T(8,128)(2,1)S(1)} all-to-all(bf16[16,144,128]{2,1,0:T(8,128)(2,1)S(1)} %pad_maximum_fusion.2), channel_id=1, replica_groups=mesh['x'=4,'z'=8,'yh'=2,'yl'=2,'c'=2] {'x','yh','yl'}, dimensions={0} | all-to-all | bytes 1179648 | tf_op jit(solution)/shard_map/all_to_all | solution.py:27
  49.5 3.5 %all-to-all-start.2 = ((bf16[16,16,128]{2,1,0:T(8,128)(2,1)}), bf16[16,16,128]{2,1,0:T(8,128)(2,1)S(1)}, u32[]{:S(2)}, u32[]{:S(2)}) async-start(bf16[16,16,128]{2,1,0:T(8,128)(2,1)} %broadcast_in_dim.28), calls=%async_computation.2 | async-start | bytes 131072 | tf_op jit(solution)/shard_map/all_to_all | solution.py:27
  53.1 1.8 collective-permute-start.2
  54.9 4.6 %all-to-all-done.2 = bf16[16,16,128]{2,1,0:T(8,128)(2,1)S(1)} async-done(((bf16[16,16,128]{2,1,0:T(8,128)(2,1)}), bf16[16,16,128]{2,1,0:T(8,128)(2,1)S(1)}, u32[]{:S(2)}, u32[]{:S(2)}) %all-to-all-start.2) | async-done | bytes 65568 | tf_op jit(solution)/shard_map/all_to_all | solution.py:27
  59.4 2.8 collective-permute-start.1
  63.3 35.2 %setup_factor.1 = (bf16[1024,512]{1,0:T(8,128)(2,1)S(1)}, bf16[1024,512]{1,0:T(8,128)(2,1)S(1)}, bf16[1024,512]{1,0:T(8,128)(2,1)S(1)}, bf16[1024,256]{1,0:T(8,1...) custom-call(bf16[512,128]{1,0:T(8,128)(2,1)S(1)} %bitcast.80, bf16[1024,128]{1,0:T(8,128)(2,1)S(1)} %bitcast.79, ...), custom_call_target="tpu_custom_call" | custom-call | tf_op jit(solution)/shard_map/setup_factor/pallas_call | solution.py:359
  101.5 1.6 collective-permute-done.3
  104.1 12.2 %all_to_all.66 = f32[16,48,128]{2,1,0:T(8,128)S(1)} all-to-all(f32[16,48,128]{2,1,0:T(8,128)S(1)} %dynamic-slice_add_fusion), channel_id=1, replica_groups=mesh['x'=4,'z'=8,'yh'=2,'yl'=2,'c'=2] {'x','yh','yl'}, dimensions={0} | all-to-all | bytes 786432 | tf_op jit(solution)/shard_map/all_to_all | solution.py:27
  116.4 11.3 %all_to_all.67 = f32[16,48,128]{2,1,0:T(8,128)S(1)} all-to-all(f32[16,48,128]{2,1,0:T(8,128)S(1)} %broadcast_in_dim.29), channel_id=1, replica_groups=mesh['x'=4,'z'=8,'yh'=2,'yl'=2,'c'=2] {'x','yh','yl'}, dimensions={0} | all-to-all | bytes 786432 | tf_op jit(solution)/shard_map/all_to_all | solution.py:27
  127.7 2.9 collective-permute-start.4
  132.1 38.8 %begin.1 = (bf16[512,512]{1,0:T(8,128)(2,1)S(1)}, bf16[512,512]{1,0:T(8,128)(2,1)S(1)}, bf16[512,512]{1,0:T(8,128)(2,1)S(1)}, f32[32,512]{1,0:T(8,128)S(1)}, f32...) custom-call(f32[32,48,128]{2,1,0:T(8,128)S(1)} %pad_maximum_fusion.1.packed_, ...), custom_call_target="tpu_custom_call" | custom-call | tf_op jit(solution)/shard_map/begin/pallas_call | solution.py:359
  176.4 4.2 %all-to-all-start.5 = ((f32[16,32,128]{2,1,0:T(8,128)}), f32[16,32,128]{2,1,0:T(8,128)}, u32[]{:S(2)}, u32[]{:S(2)}) async-start(f32[16,32,128]{2,1,0:T(8,128)} %slice_add_fusion.2), calls=%async_computation.5 | async-start | bytes 524288 | tf_op jit(solution)/shard_map/all_to_all | solution.py:27
  180.6 7.7 %all-to-all-done.5 = f32[16,32,128]{2,1,0:T(8,128)} async-done(((f32[16,32,128]{2,1,0:T(8,128)}), f32[16,32,128]{2,1,0:T(8,128)}, u32[]{:S(2)}, u32[]{:S(2)}) %all-to-all-start.5) | async-done | bytes 262176 | tf_op jit(solution)/shard_map/all_to_all | solution.py:27
  189.3 10.3 %all_to_all.68.image_ref = f32[8,32,128]{2,1,0:T(8,128)S(1)} all-to-all(f32[8,32,128]{2,1,0:T(8,128)S(1)} %broadcast_in_dim.31), channel_id=1, replica_groups=mesh['x'=4,'z'=8,'yh'=2,'yl'=2,'c'=2] {'z'}, dimensions={0} | all-to-all | bytes 262144 | tf_op jit(solution)/shard_map/all_to_all | solution.py:27
  200.3 3.0 collective-permute-start.6
  204.5 3.5 %collective-permute-done.7 = f32[32,640]{1,0:T(8,128)S(1)} collective-permute-done((f32[32,640]{1,0:T(8,128)S(1)}, f32[32,640]{1,0:T(8,128)S(1)}, u32[]{:S(2)}, u32[]{:S(2)}) %collective-permute-start.7) | collective-permute-done | bytes 81952 | tf_op jit(solution)/shard_map/ppermute | solution.py:447
  208.1 13.9 %all_to_all.69.packed_ref = f32[8,32,640]{2,1,0:T(8,128)S(1)} all-to-all(f32[8,32,640]{2,1,0:T(8,128)S(1)} %broadcast_in_dim.32), channel_id=1, replica_groups=mesh['x'=4,'z'=8,'yh'=2,'yl'=2,'c'=2] {'x','yh'}, dimensions={0} | all-to-all | bytes 1310720 | tf_op jit(solution)/shard_map/all_to_all | solution.py:27
  222.1 14.5 %advance.2 = (f32[8,32,128]{2,1,0:T(8,128)S(1)}, f32[8,32,128]{2,1,0:T(8,128)S(1)}, f32[8,32,128]{2,1,0:T(8,128)S(1)}, f32[32,512]{1,0:T(8,128)S(1)}, f32[32,128...) custom-call(f32[8,32,640]{2,1,0:T(8,128)S(1)} %all_to_all.69.packed_ref, ...), custom_call_target="tpu_custom_call" | custom-call | tf_op jit(solution)/shard_map/advance/pallas_call | solution.py:359
  237.2 3.3 collective-permute-start.8
  241.7 11.0 %all_to_all.70 = f32[16,32,128]{2,1,0:T(8,128)} all-to-all(f32[16,32,128]{2,1,0:T(8,128)S(1)} %slice_add_fusion.1), channel_id=1, replica_groups=mesh['x'=4,'z'=8,'yh'=2,'yl'=2,'c'=2] {'x','yh','yl'}, dimensions={0} | all-to-all | bytes 524288 | tf_op jit(solution)/shard_map/all_to_all | solution.py:27
  253.7 10.3 %all_to_all.71.image_ref = f32[8,32,128]{2,1,0:T(8,128)S(1)} all-to-all(f32[8,32,128]{2,1,0:T(8,128)S(1)} %broadcast_in_dim.35), channel_id=1, replica_groups=mesh['x'=4,'z'=8,'yh'=2,'yl'=2,'c'=2] {'z'}, dimensions={0} | all-to-all | bytes 262144 | tf_op jit(solution)/shard_map/all_to_all | solution.py:27
  264.7 3.0 collective-permute-start.9
  268.8 3.5 %collective-permute-done.10 = f32[32,640]{1,0:T(8,128)S(1)} collective-permute-done((f32[32,640]{1,0:T(8,128)S(1)}, f32[32,640]{1,0:T(8,128)S(1)}, u32[]{:S(2)}, u32[]{:S(2)}) %collective-permute-start.10) | collective-permute-done | bytes 81952 | tf_op jit(solution)/shard_map/ppermute | solution.py:447
  272.4 13.9 %all_to_all.72.packed_ref = f32[8,32,640]{2,1,0:T(8,128)S(1)} all-to-all(f32[8,32,640]{2,1,0:T(8,128)S(1)} %broadcast_in_dim.36), channel_id=1, replica_groups=mesh['x'=4,'z'=8,'yh'=2,'yl'=2,'c'=2] {'x','yh'}, dimensions={0} | all-to-all | bytes 1310720 | tf_op jit(solution)/shard_map/all_to_all | solution.py:27
  286.4 14.5 %advance.3 = (f32[8,32,128]{2,1,0:T(8,128)S(1)}, f32[8,32,128]{2,1,0:T(8,128)S(1)}, f32[8,32,128]{2,1,0:T(8,128)S(1)}, f32[32,512]{1,0:T(8,128)}, f32[32,128]{1,...) custom-call(f32[8,32,640]{2,1,0:T(8,128)S(1)} %all_to_all.72.packed_ref, ...), custom_call_target="tpu_custom_call" | custom-call | tf_op jit(solution)/shard_map/advance/pallas_call | solution.py:359
  301.0 3.0 collective-permute-start.11
  305.8 3.5 %all-to-all-start.11 = ((f32[16,32,128]{2,1,0:T(8,128)}), f32[16,32,128]{2,1,0:T(8,128)S(1)}, u32[]{:S(2)}, u32[]{:S(2)}) async-start(f32[16,32,128]{2,1,0:T(8,128)} %slice_add_fusion), calls=%async_computation.11 | async-start | bytes 524288 | tf_op jit(solution)/shard_map/all_to_all | solution.py:27
  310.0 7.0 %all-to-all-done.11 = f32[16,32,128]{2,1,0:T(8,128)S(1)} async-done(((f32[16,32,128]{2,1,0:T(8,128)}), f32[16,32,128]{2,1,0:T(8,128)S(1)}, u32[]{:S(2)}, u32[]{:S(2)}) %all-to-all-start.11) | async-done | bytes 262176 | tf_op jit(solution)/shard_map/all_to_all | solution.py:27
  318.6 6.7 %all-to-all-start.12 = ((f32[256,1,128]{2,1,0:T(1,128)}), f32[256,1,128]{2,1,0:T(1,128)S(1)}, u32[]{:S(2)}, u32[]{:S(2)}) async-start(f32[256,1,128]{2,1,0:T(1,128)} %broadcast_in_dim.38), calls=%async_computation.12 | async-start | bytes 262144 | tf_op jit(solution)/shard_map/all_to_all | solution.py:27
  326.0 12.3 %all-to-all-done.12 = f32[256,1,128]{2,1,0:T(1,128)S(1)} async-done(((f32[256,1,128]{2,1,0:T(1,128)}), f32[256,1,128]{2,1,0:T(1,128)S(1)}, u32[]{:S(2)}, u32[]{:S(2)}) %all-to-all-start.12) | async-done | bytes 131104 | tf_op jit(solution)/shard_map/all_to_all | solution.py:27
  (136 shorter events, 31.5 us)
Async XLA Ops:
  0.6 30.0 %copy-start.30 = (bf16[128,128]{1,0:T(8,128)(2,1)S(1)}, bf16[128,128]{1,0:T(8,128)(2,1)}, u32[]{:S(2)}) copy-start(bf16[128,128]{1,0:T(8,128)(2,1)} %param.5) | copy-start | bytes 98308
  3.0 25.5 %all-to-all-start = ((bf16[8,224,128]{2,1,0:T(8,128)(2,1)}), bf16[8,224,128]{2,1,0:T(8,128)(2,1)S(1)}, u32[]{:S(2)}, u32[]{:S(2)}) async-start(bf16[8,224,128]{2,1,0:T(8,128)(2,1)} %broadcast_in_dim.27), calls=%async_computation | async-start | bytes 917504 | tf_op jit(solution)/shard_map/all_to_all | solution.py:27
  29.0 1.6 collective-permute-start
  49.5 10.0 %all-to-all-start.2 = ((bf16[16,16,128]{2,1,0:T(8,128)(2,1)}), bf16[16,16,128]{2,1,0:T(8,128)(2,1)S(1)}, u32[]{:S(2)}, u32[]{:S(2)}) async-start(bf16[16,16,128]{2,1,0:T(8,128)(2,1)} %broadcast_in_dim.28), calls=%async_computation.2 | async-start | bytes 131072 | tf_op jit(solution)/shard_map/all_to_all | solution.py:27
  53.1 10.1 %collective-permute-start.2 = (bf16[2048,128]{1,0:T(8,128)(2,1)S(1)}, bf16[2048,128]{1,0:T(8,128)(2,1)S(1)}, u32[]{:S(2)}, u32[]{:S(2)}) collective-permute-start(bf16[2048,128]{1,0:T(8,128)(2,1)S(1)} %bitcast.81), channel_id=1, source_target_pairs={{0,1},{1,0},{2,3},{3,2},{4,5},{5,4},{6,7},{7,6},{8,9},{9,8},{10,11... | collective-permute-start | bytes 1572872 | tf_op jit(solution)/shard_map/ppermute | solution.py:36
  59.4 3.7 %collective-permute-start.1 = (bf16[16,16,128]{2,1,0:T(8,128)(2,1)S(1)}, bf16[16,16,128]{2,1,0:T(8,128)(2,1)S(1)}, u32[]{:S(2)}, u32[]{:S(2)}) collective-permute-start(bf16[16,16,128]{2,1,0:T(8,128)(2,1)S(1)} %all-to-all-done.2), channel_id=1, source_target_pairs={{0,1},{1,0},{2,3},{3,2},{4,5},{5,4},{6,7},{7,6},{8,9},{9,8},{10,11... | collective-permute-start | bytes 196616 | tf_op jit(solution)/shard_map/ppermute | solution.py:36
  99.5 32.6 %copy-start.5 = (bf16[1024,256]{1,0:T(8,128)(2,1)}, bf16[1024,256]{1,0:T(8,128)(2,1)S(1)}, u32[]{:S(2)}) copy-start(bf16[1024,256]{1,0:T(8,128)(2,1)S(1)} %get-tuple-element.45.key_ref) | copy-start | bytes 1572868
  99.5 100.1 %copy-start = (bf16[1024,512]{1,0:T(8,128)(2,1)}, bf16[1024,512]{1,0:T(8,128)(2,1)S(1)}, u32[]{:S(2)}) copy-start(bf16[1024,512]{1,0:T(8,128)(2,1)S(1)} %get-tuple-element.43.mid_ref) | copy-start | bytes 3145732
  101.1 1.9 collective-permute-start.3
  127.7 4.2 %collective-permute-start.4 = (f32[16,48,128]{2,1,0:T(8,128)S(1)}, f32[16,48,128]{2,1,0:T(8,128)S(1)}, u32[]{:S(2)}, u32[]{:S(2)}) collective-permute-start(f32[16,48,128]{2,1,0:T(8,128)S(1)} %all_to_all.67), channel_id=1, source_target_pairs={{0,1},{1,0},{2,3},{3,2},{4,5},{5,4},{6,7},{7,6},{8,9},{9,8},{10,11... | collective-permute-start | bytes 1179656 | tf_op jit(solution)/shard_map/ppermute | solution.py:36
  174.0 26.3 %copy-start.24 = (f32[32,128]{1,0:T(8,128)}, f32[32,128]{1,0:T(8,128)S(1)}, u32[]{:S(2)}) copy-start(f32[32,128]{1,0:T(8,128)S(1)} %get-tuple-element.51.sq_ref) | copy-start | bytes 49156
  174.0 25.7 %copy-start.3 = (bf16[1024,512]{1,0:T(8,128)(2,1)S(1)}, bf16[1024,512]{1,0:T(8,128)(2,1)}, u32[]{:S(2)}) copy-start(bf16[1024,512]{1,0:T(8,128)(2,1)} %copy-done.2) | copy-start | bytes 3145732
  174.0 1.6 collective-permute-start.5
  176.4 11.9 %all-to-all-start.5 = ((f32[16,32,128]{2,1,0:T(8,128)}), f32[16,32,128]{2,1,0:T(8,128)}, u32[]{:S(2)}, u32[]{:S(2)}) async-start(f32[16,32,128]{2,1,0:T(8,128)} %slice_add_fusion.2), calls=%async_computation.5 | async-start | bytes 524288 | tf_op jit(solution)/shard_map/all_to_all | solution.py:27
  200.3 3.9 %collective-permute-start.6 = (f32[32,640]{1,0:T(8,128)S(1)}, f32[32,640]{1,0:T(8,128)S(1)}, u32[]{:S(2)}, u32[]{:S(2)}) collective-permute-start(f32[32,640]{1,0:T(8,128)S(1)} %project.2), channel_id=1, source_target_pairs={{0,1},{1,0},{2,3},{3,2},{4,5},{5,4},{6,7},{7,6},{8,9},{9,8},{10,11... | collective-permute-start | bytes 245768 | tf_op jit(solution)/shard_map/ppermute | solution.py:36
  204.2 3.8 %collective-permute-start.7 = (f32[32,640]{1,0:T(8,128)S(1)}, f32[32,640]{1,0:T(8,128)S(1)}, u32[]{:S(2)}, u32[]{:S(2)}) collective-permute-start(f32[32,640]{1,0:T(8,128)S(1)} %add.162), channel_id=1, source_target_pairs={{0,2},{2,0},{1,3},{3,1},{4,6},{6,4},{5,7},{7,5},{8,10},{10,8},{9,1... | collective-permute-start | bytes 245768 | tf_op jit(solution)/shard_map/ppermute | solution.py:447
  237.2 26.8 %copy-start.1 = (bf16[1024,512]{1,0:T(8,128)(2,1)S(1)}, bf16[1024,512]{1,0:T(8,128)(2,1)}, u32[]{:S(2)}) copy-start(bf16[1024,512]{1,0:T(8,128)(2,1)} %copy-done) | copy-start | bytes 3145732
  237.2 26.8 %copy-start.4 = (bf16[1024,512]{1,0:T(8,128)(2,1)S(1)}, bf16[1024,512]{1,0:T(8,128)(2,1)}, u32[]{:S(2)}) copy-start(bf16[1024,512]{1,0:T(8,128)(2,1)} %copy-done.2) | copy-start | bytes 3145732
  237.2 4.4 %collective-permute-start.8 = (f32[16,32,128]{2,1,0:T(8,128)S(1)}, f32[16,32,128]{2,1,0:T(8,128)S(1)}, u32[]{:S(2)}, u32[]{:S(2)}) collective-permute-start(f32[16,32,128]{2,1,0:T(8,128)S(1)} %slice.71), channel_id=1, source_target_pairs={{0,1},{1,0},{2,3},{3,2},{4,5},{5,4},{6,7},{7,6},{8,9},{9,8},{10,11... | collective-permute-start | bytes 786440 | tf_op jit(solution)/shard_map/ppermute | solution.py:36
  264.6 21.7 %copy-start.7 = (bf16[1024,256]{1,0:T(8,128)(2,1)S(1)}, bf16[1024,256]{1,0:T(8,128)(2,1)}, u32[]{:S(2)}) copy-start(bf16[1024,256]{1,0:T(8,128)(2,1)} %copy-done.5) | copy-start | bytes 1572868
  264.6 21.7 %copy-start.10 = (bf16[512,512]{1,0:T(8,128)(2,1)S(1)}, bf16[512,512]{1,0:T(8,128)(2,1)}, u32[]{:S(2)}) copy-start(bf16[512,512]{1,0:T(8,128)(2,1)} %copy-done.8) | copy-start | bytes 1572868
  264.6 21.7 %copy-start.13 = (bf16[512,512]{1,0:T(8,128)(2,1)S(1)}, bf16[512,512]{1,0:T(8,128)(2,1)}, u32[]{:S(2)}) copy-start(bf16[512,512]{1,0:T(8,128)(2,1)} %copy-done.11) | copy-start | bytes 1572868
  264.6 21.7 %copy-start.16 = (bf16[512,512]{1,0:T(8,128)(2,1)S(1)}, bf16[512,512]{1,0:T(8,128)(2,1)}, u32[]{:S(2)}) copy-start(bf16[512,512]{1,0:T(8,128)(2,1)} %copy-done.14) | copy-start | bytes 1572868
  264.7 21.7 %copy-start.19 = (f32[8,32,128]{2,1,0:T(8,128)S(1)}, f32[8,32,128]{2,1,0:T(8,128)}, u32[]{:S(2)}) copy-start(f32[8,32,128]{2,1,0:T(8,128)} %copy-done.18) | copy-start | bytes 393220
  264.7 21.7 %copy-start.23 = (f32[32,512]{1,0:T(8,128)S(1)}, f32[32,512]{1,0:T(8,128)}, u32[]{:S(2)}) copy-start(f32[32,512]{1,0:T(8,128)} %copy-done.22) | copy-start | bytes 196612
  264.7 21.7 %copy-start.27 = (f32[32,128]{1,0:T(8,128)S(1)}, f32[32,128]{1,0:T(8,128)}, u32[]{:S(2)}) copy-start(f32[32,128]{1,0:T(8,128)} %copy-done.26) | copy-start | bytes 49156
  264.7 21.7 %copy-start.29 = (f32[32,128]{1,0:T(8,128)S(1)}, f32[32,128]{1,0:T(8,128)}, u32[]{:S(2)}) copy-start(f32[32,128]{1,0:T(8,128)} %copy-done.28) | copy-start | bytes 49156
  264.7 3.9 %collective-permute-start.9 = (f32[32,640]{1,0:T(8,128)S(1)}, f32[32,640]{1,0:T(8,128)S(1)}, u32[]{:S(2)}, u32[]{:S(2)}) collective-permute-start(f32[32,640]{1,0:T(8,128)S(1)} %project.3), channel_id=1, source_target_pairs={{0,1},{1,0},{2,3},{3,2},{4,5},{5,4},{6,7},{7,6},{8,9},{9,8},{10,11... | collective-permute-start | bytes 245768 | tf_op jit(solution)/shard_map/ppermute | solution.py:36
  268.6 3.8 %collective-permute-start.10 = (f32[32,640]{1,0:T(8,128)S(1)}, f32[32,640]{1,0:T(8,128)S(1)}, u32[]{:S(2)}, u32[]{:S(2)}) collective-permute-start(f32[32,640]{1,0:T(8,128)S(1)} %add.166), channel_id=1, source_target_pairs={{0,2},{2,0},{1,3},{3,1},{4,6},{6,4},{5,7},{7,5},{8,10},{10,8},{9,1... | collective-permute-start | bytes 245768 | tf_op jit(solution)/shard_map/ppermute | solution.py:447
  301.0 4.2 %collective-permute-start.11 = (f32[16,32,128]{2,1,0:T(8,128)S(1)}, f32[16,32,128]{2,1,0:T(8,128)S(1)}, u32[]{:S(2)}, u32[]{:S(2)}) collective-permute-start(f32[16,32,128]{2,1,0:T(8,128)S(1)} %slice.74), channel_id=1, source_target_pairs={{0,1},{1,0},{2,3},{3,2},{4,5},{5,4},{6,7},{7,6},{8,9},{9,8},{10,11... | collective-permute-start | bytes 786440 | tf_op jit(solution)/shard_map/ppermute | solution.py:36
  305.8 11.2 %all-to-all-start.11 = ((f32[16,32,128]{2,1,0:T(8,128)}), f32[16,32,128]{2,1,0:T(8,128)S(1)}, u32[]{:S(2)}, u32[]{:S(2)}) async-start(f32[16,32,128]{2,1,0:T(8,128)} %slice_add_fusion), calls=%async_computation.11 | async-start | bytes 524288 | tf_op jit(solution)/shard_map/all_to_all | solution.py:27
  318.6 19.7 %all-to-all-start.12 = ((f32[256,1,128]{2,1,0:T(1,128)}), f32[256,1,128]{2,1,0:T(1,128)S(1)}, u32[]{:S(2)}, u32[]{:S(2)}) async-start(f32[256,1,128]{2,1,0:T(1,128)} %broadcast_in_dim.38), calls=%async_computation.12 | async-start | bytes 262144 | tf_op jit(solution)/shard_map/all_to_all | solution.py:27
  (16 other events, 146.6 us)
where the time goes:
time: 340 us; the launch traced here: 339 us
  Pallas kernels  104 us (31%)
  blocking collectives  101 us (30%)
  waiting for transfers between devices  64.4 us (19%)
  starting transfers between devices  48.6 us (14%)
  local copies, waits for them, and re-layouts  10.5 us (3%)
  other arithmetic  8.82 us (3%)
    pallas_call x6, Pallas kernels, call(): pl.pallas_call(body, out_shape=[jax.ShapeDtypeStruct(shape, dtype) for sh...  104 us
    all_to_all x8, blocking collectives, swap(): return lax.all_to_all(blocks, axes, 0, 0, tiled=False)  101 us
    all_to_all x5, waiting for transfers between devices, swap(): return lax.all_to_all(blocks, axes, 0, 0, tiled=False)  47.3 us
    all_to_all x5, starting transfers between devices, swap(): return lax.all_to_all(blocks, axes, 0, 0, tiled=False)  27 us
    ppermute x10, starting transfers between devices, partner(): return lax.ppermute(values, 'c', [(0, 1), (1, 0)])  21.2 us
    ppermute x10, waiting for transfers between devices, partner(): return lax.ppermute(values, 'c', [(0, 1), (1, 0)])  10 us
    ppermute x2, waiting for transfers between devices, per_device(): packed = packed + lax.ppermute(packed, CHIPS[2], [(0, 1), (1, 0)])  7.08 us
  transfers between devices with their start and end apart: 17, of which 16 were waited for; matrix products, arithmetic and copies ran while one was open for 1% of the time, Pallas kernels for 0%

commit v1 on v0

--- a/solution.py
+++ b/solution.py
@@ -32,8 +32,13 @@
     return swap(jnp.broadcast_to(block[None], (count,) + block.shape), axes)
 
 
+def other_of_two(values, axis):
+    count = lax.axis_size(axis)
+    return lax.ppermute(values, axis, [(i, (i + 1) % count) for i in range(count)])
+
+
 def partner(values):
-    return lax.ppermute(values, "c", [(0, 1), (1, 0)])
+    return other_of_two(values, "c")
 
 
 def core_first(mine, other):
@@ -63,6 +68,12 @@
 def dot_nn(left, right, precision=None):
     return lax.dot_general(
         left, right, (((1,), (0,)), ((), ())), precision=precision, preferred_element_type=F32
+    )
+
+
+def dot_tn(left, right, precision=None):
+    return lax.dot_general(
+        left, right, (((0,), (0,)), ((), ())), precision=precision, preferred_element_type=F32
     )
 
 
@@ -159,14 +170,26 @@
     def stage(j, carry):
         start = pl.multiple_of(j * BLOCK, BLOCK)
         here = pl.ds(start, BLOCK)
+        local = inverse_of_block(work_ref[here, here])
+        strip = dot_nn(local, work_ref[here, :], HIGHEST)
+        lane = lax.broadcasted_iota(jnp.int32, strip.shape, 1)
+        upper = split(jnp.where(lane >= start + BLOCK, strip, 0.0))
+        work_ref[here, :] = strip
+        work_ref[here, here] = local
+        strip = split(work_ref[here, :])
         below = lax.broadcasted_iota(jnp.int32, (order, BLOCK), 0) >= start + BLOCK
-        local = inverse_of_block(work_ref[here, here])
-        work_ref[here, :] = dot_nn(local, work_ref[here, :], HIGHEST)
-        low = jnp.where(below, dot_nt(work_ref[:, here], local, HIGHEST), 0.0)
-        work_ref[here, here] = local
-        strip = work_ref[here, :]
         work_ref[:, here] = jnp.where(below, 0.0, work_ref[:, here])
-        work_ref[...] = work_ref[...] - dot_nn(low, strip, HIGHEST)
+        high_mid = jnp.concatenate(upper[:2], axis=0)
+        work_ref[...] = work_ref[...] - (
+            dot_tn(high_mid, jnp.concatenate([strip[0], strip[0]], axis=0))
+            + (
+                dot_tn(high_mid, jnp.concatenate([strip[1], strip[1]], axis=0))
+                + dot_tn(
+                    jnp.concatenate([upper[0], upper[2]], axis=0),
+                    jnp.concatenate([strip[2], strip[0]], axis=0),
+                )
+            )
+        )
         return carry
 
     lax.fori_loop(0, order // BLOCK, stage, 0)
@@ -185,24 +208,25 @@
     return jnp.concatenate([ref[i] for i in range(ref.shape[0])], axis=1)
 
 
-def setup_body(
-    picked_ref, keys_ref, rows_ref, targets_ref,
-    high_ref, mid_ref, low_ref, key_ref, row_ref, out_ref, work_ref, pack_ref,
-):
-    piv = picked_ref.shape[0]
-    chunks = out_ref.shape[0]
+def pivots_body(picked_ref, inv_ref, right_ref, work_ref):
     picked = picked_ref[...]
     right = extended(picked, False)
-    work_ref[...] = jnp.exp(dot_nt(extended(picked, True), right)) + unit_matrix(piv, JITTER)
+    right_ref[...] = right
+    work_ref[...] = (
+        jnp.exp(dot_nt(extended(picked, True), right)) + unit_matrix(picked.shape[0], JITTER)
+    )
+    inv_ref[...] = inverse_factor(work_ref)
+
+
+def setup_body(
+    inv_ref, right_ref, keys_ref, targets_ref,
+    high_ref, mid_ref, low_ref, key_ref, out_ref, pack_ref,
+):
+    piv = inv_ref.shape[0]
+    chunks = out_ref.shape[0]
+    right = right_ref[...]
+    inverse = inv_ref[...]
     key_ref[...] = extended(keys_ref[...], True)
-
-    def rows_step(i, carry):
-        here = pl.ds(pl.multiple_of(i * 256, 256), 256)
-        row_ref[here, :] = extended(rows_ref[here, :], False)
-        return carry
-
-    lax.fori_loop(0, rows_ref.shape[0] // 256, rows_step, 0)
-    inverse = inverse_factor(work_ref)
     wide = dot_nt(jnp.exp(dot_nt(key_ref[...], right)), inverse, HIGHEST)
     parts = split(wide)
     high_ref[...] = parts[0]
@@ -210,18 +234,14 @@
     low_ref[...] = parts[2]
     at = 0
     for i in range(piv // BLOCK):
-        strip = lax.dot_general(
-            wide[:, i * BLOCK:(i + 1) * BLOCK], wide[:, :(i + 1) * BLOCK],
-            (((0,), (0,)), ((), ())), precision=HIGHEST, preferred_element_type=F32,
+        strip = dot_tn(
+            wide[:, i * BLOCK:(i + 1) * BLOCK], wide[:, :(i + 1) * BLOCK], HIGHEST
         )
         for j in range(i + 1):
             pack_ref[at:at + BLOCK, :] = strip[:, j * BLOCK:(j + 1) * BLOCK]
             at += BLOCK
     targets = joined(targets_ref)
     proj = dot_nn(targets, wide, HIGHEST)
-    squares = jnp.broadcast_to(
-        jnp.sum(targets * targets, axis=1, keepdims=True), (proj.shape[0], BLOCK)
-    )
     part = at // chunks
     per = proj.shape[0] // chunks
     split_by = piv // BLOCK
@@ -231,7 +251,6 @@
             row = i * per + p
             for k in range(split_by):
                 out_ref[i, part + p * split_by + k, :] = proj[row, k * BLOCK:(k + 1) * BLOCK]
-            out_ref[i, part + per * split_by + p, :] = squares[row, :]
 
 
 def gram_solve(proj, inverse):
@@ -244,8 +263,8 @@
     parts = jnp.concatenate(split(direction), axis=0)
     chunk = 256
 
-    def rows_step(i, carry):
-        rows = row_ref[pl.ds(pl.multiple_of(i * chunk, chunk), chunk), :]
+    for first in range(0, row_ref.shape[0], chunk):
+        rows = row_ref[first:first + chunk, :]
         total = jnp.zeros((count, chunk), F32)
         for start in range(0, keys, chunk):
             values = jnp.exp(dot_nt(key_ref[start:start + chunk, :], rows))
@@ -257,20 +276,14 @@
                 a[:count] + ((a[count:2 * count] + b[:count]) + (a[2 * count:] + b[count:]))
             )
         for k in range(chunk // BLOCK):
-            out_ref[i * (chunk // BLOCK) + k] = total[:, k * BLOCK:(k + 1) * BLOCK]
-        return carry
-
-    lax.fori_loop(0, row_ref.shape[0] // chunk, rows_step, 0)
+            out_ref[first // BLOCK + k] = total[:, k * BLOCK:(k + 1) * BLOCK]
 
 
 def next_direction(residual, coef, wide):
     return (residual - stacked_dot(dot_nt, coef, wide)) * (1.0 / NOISE)
 
 
-def begin_body(
-    packed_ref, res_ref, high_ref, mid_ref, low_ref, key_ref, row_ref,
-    inv_high, inv_mid, inv_low, proj_ref, dir_ref, inner_ref, sq_ref, out_ref, work_ref, pack_ref,
-):
+def gram_body(packed_ref, inv_high, inv_mid, inv_low, proj_ref, work_ref, pack_ref):
     piv = work_ref.shape[0]
     chunks = packed_ref.shape[0]
     split_by = piv // BLOCK
@@ -282,7 +295,6 @@
             row = i * per + p
             for k in range(split_by):
                 proj_ref[row, k * BLOCK:(k + 1) * BLOCK] = packed_ref[i, part + p * split_by + k, :]
-            sq_ref[row, :] = packed_ref[i, part + per * split_by + p, :]
     at = 0
     for i in range(split_by):
         for j in range(i + 1):
@@ -297,9 +309,18 @@
     inv_high[...] = inverse[0]
     inv_mid[...] = inverse[1]
     inv_low[...] = inverse[2]
-    proj = proj_ref[...]
-    coef = gram_solve(proj, inverse)
-    inner_ref[...] = (sq_ref[...] - jnp.sum(proj * coef, axis=1, keepdims=True)) * (1.0 / NOISE)
+
+
+def begin_body(
+    proj_ref, inv_high, inv_mid, inv_low, res_ref, high_ref, mid_ref, low_ref, key_ref,
+    points_ref, dir_ref, row_ref, out_ref,
+):
+    chips = points_ref.shape[0]
+    for i in range(chips):
+        for k in range(2):
+            at = (k * chips + i) * BLOCK
+            row_ref[at:at + BLOCK, :] = extended(points_ref[i, k * BLOCK:(k + 1) * BLOCK, :], False)
+    coef = gram_solve(proj_ref[...], (inv_high[...], inv_mid[...], inv_low[...]))
     direction = next_direction(joined(res_ref), coef, (high_ref[...], mid_ref[...], low_ref[...]))
     for i in range(dir_ref.shape[0]):
         dir_ref[i] = direction[:, i * BLOCK:(i + 1) * BLOCK]
@@ -315,23 +336,24 @@
     curve = jnp.sum(direction * image, axis=1, keepdims=True)
     cross = jnp.sum(residual * image, axis=1, keepdims=True)
     own = jnp.sum(image * image, axis=1, keepdims=True)
+    along = jnp.sum(direction * residual, axis=1, keepdims=True)
+    squares = jnp.sum(residual * residual, axis=1, keepdims=True)
     lane = lax.broadcasted_iota(jnp.int32, (image.shape[0], BLOCK), 1)
-    out_ref[:, piv:] = jnp.where(lane == 0, curve, jnp.where(lane == 1, cross, own))
+    sums = jnp.where(lane == 0, curve, jnp.where(lane == 1, cross, own))
+    out_ref[:, piv:] = jnp.where(lane == 3, along, jnp.where(lane == 4, squares, sums))
 
 
 def advance_body(
-    packed_ref, image_ref, res_ref, dir_ref, sol_ref, proj_ref, inner_ref, sq_ref,
+    packed_ref, image_ref, res_ref, dir_ref, sol_ref, proj_ref,
     inv_high, inv_mid, inv_low, high_ref, mid_ref, low_ref, key_ref, row_ref,
-    new_res, new_dir, new_sol, new_proj, new_inner, new_sq, out_ref,
+    new_res, new_dir, new_sol, new_proj, out_ref,
 ):
     piv = proj_ref.shape[1]
-    total = packed_ref[0]
-    for i in range(1, packed_ref.shape[0]):
-        total = total + packed_ref[i]
-    inner = inner_ref[:, 0:1]
+    total = packed_ref[...]
+    inner = total[:, piv + 3:piv + 4]
     alpha = inner / total[:, piv:piv + 1]
     squares = (
-        sq_ref[:, 0:1] - 2.0 * alpha * total[:, piv + 1:piv + 2]
+        total[:, piv + 4:piv + 5] - 2.0 * alpha * total[:, piv + 1:piv + 2]
         + alpha * alpha * total[:, piv + 2:piv + 3]
     )
     proj = proj_ref[...] - alpha * total[:, :piv]
@@ -339,8 +361,6 @@
     inner_next = (squares - jnp.sum(proj * coef, axis=1, keepdims=True)) * (1.0 / NOISE)
     beta = inner_next / inner
     new_proj[...] = proj
-    new_inner[...] = jnp.broadcast_to(inner_next, new_inner.shape)
-    new_sq[...] = jnp.broadcast_to(squares, new_sq.shape)
     direction = joined(dir_ref)
     residual = joined(res_ref) - alpha * joined(image_ref)
     solution = joined(sol_ref) + alpha * direction
@@ -355,12 +375,15 @@
     product(direction, key_ref, row_ref, out_ref)
 
 
-def call(body, name, outs, scratch, *args):
+def call(body, name, outs, scratch, *args, seconds=10e-6):
     return pl.pallas_call(
         body,
         out_shape=[jax.ShapeDtypeStruct(shape, dtype) for shape, dtype in outs],
         scratch_shapes=scratch,
         compiler_params=pltpu.CompilerParams(vmem_limit_bytes=48 << 20),
+        cost_estimate=pl.CostEstimate(
+            flops=int(seconds * 1e15), bytes_accessed=int(seconds * 3e12), transcendentals=0
+        ),
         interpret=INTERPRET,
         name=name,
     )(*args)
@@ -377,45 +400,39 @@
     part = piv // v_size
     per = columns // v_size
 
+    place = jnp.zeros((), jnp.int32)
+    for axis in ALL:
+        place = place * lax.axis_size(axis) + lax.axis_index(axis)
+    own_ids = place * own + jnp.arange(own, dtype=jnp.int32)
+    owned = (flat_pivots[:, None] == own_ids[None, :]).astype(BF16)
+    held = jnp.dot(owned, points, preferred_element_type=F32).astype(BF16)
+    held = half(held, core) + partner(half(held, 1 - core))
+    picked = swap(held.reshape(chips, part, -1), CHIPS)
+    picked = jnp.sum(picked.astype(F32), axis=0).astype(BF16)
+    picked = jnp.sum(share(picked, U).astype(F32), axis=0).astype(BF16)
+    picked = share(picked, CHIPS)
+    picked = core_first(picked, partner(picked)).reshape(piv, -1)
+
+    both_points = jnp.concatenate([points, partner(points)], axis=0)
+    points, targets, picked = lax.optimization_barrier((points, targets, picked))
     packed = share(jnp.concatenate([points] + three_parts(targets.T), axis=0), U)
     key_points = packed[:, :own].reshape(u_size * own, -1)
     parts = packed[:, own:].astype(F32).reshape(u_size, 3, columns, own)
     residual = parts[:, 0] + parts[:, 1] + parts[:, 2]
-
-    place = jnp.zeros((), jnp.int32)
-    for axis in ALL:
-        here = jnp.arange(u_size, dtype=jnp.int32) if axis in U else lax.axis_index(axis)
-        place = place * lax.axis_size(axis) + here
-    key_ids = (place[:, None] * own + jnp.arange(own, dtype=jnp.int32)[None, :]).reshape(1, -1)
-
-    owned = (flat_pivots[:, None] == key_ids).astype(BF16)
-    held = jnp.dot(owned, key_points, preferred_element_type=F32).astype(BF16)
-    held = half(held, core) + partner(half(held, 1 - core))
-    packed = swap(
-        jnp.concatenate(
-            [
-                jnp.broadcast_to(points[None], (chips,) + points.shape),
-                held.reshape(chips, part, -1),
-            ],
-            axis=1,
-        ),
-        CHIPS,
-    )
-    picked = jnp.sum(packed[:, own:].astype(F32), axis=0).astype(BF16)
-    picked = share(picked, CHIPS)
-    picked = core_first(picked, partner(picked)).reshape(piv, -1)
-    row_points = packed[:, :own].reshape(chips * own, -1)
-    row_points = jnp.concatenate([row_points, partner(row_points)], axis=0)
-
-    keys, rows = key_points.shape[0], row_points.shape[0]
+    piv_inverse, piv_right = call(
+        pivots_body, "pivots_factor", [((piv, piv), F32), ((piv, 2 * BLOCK), BF16)],
+        [pltpu.VMEM((piv, piv), F32)], picked, seconds=22e-6,
+    )
+
+    keys = key_points.shape[0]
     lower = piv // BLOCK * (piv // BLOCK + 1) // 2 * BLOCK
-    height = (lower // v_size + per * (piv // BLOCK + 1) + 7) // 8 * 8
+    height = (lower // v_size + per * (piv // BLOCK) + 7) // 8 * 8
     work = [pltpu.VMEM((piv, piv), F32), pltpu.VMEM((lower, BLOCK), F32)]
-    *wide, key_left, row_right, packed = call(
+    *wide, key_left, packed = call(
         setup_body, "setup_factor",
         [((keys, piv), BF16)] * 3
-        + [((keys, 2 * BLOCK), BF16), ((rows, 2 * BLOCK), BF16), ((v_size, height, BLOCK), F32)],
-        work, picked, key_points, row_points, residual,
+        + [((keys, 2 * BLOCK), BF16), ((v_size, height, BLOCK), F32)],
+        work[1:], piv_inverse, piv_right, key_points, residual,
     )
     factor = lax.dynamic_slice_in_dim(wide[0], u_at * own, own, 0)
     packed = jnp.sum(swap(half(packed, core) + partner(half(packed, 1 - core)), CHIPS), axis=0)
@@ -423,13 +440,16 @@
     packed = core_first(packed, partner(packed))
 
     state = ((u_size, columns, own), F32)
-    scalar = ((columns, BLOCK), F32)
     partial_shape = ((v_size, columns, own), F32)
-    *inverse, projection, direction, inner, squares, partial = call(
-        begin_body, "begin",
-        [((piv, piv), BF16)] * 3
-        + [((columns, piv), F32), state, scalar, scalar, partial_shape],
-        work, packed, residual, *wide, key_left, row_right,
+    both_points, packed = lax.optimization_barrier((both_points, packed))
+    row_points = share(both_points, CHIPS)
+    *inverse, projection = call(
+        gram_body, "gram_factor", [((piv, piv), BF16)] * 3 + [((columns, piv), F32)], work, packed,
+        seconds=22e-6,
+    )
+    direction, row_right, partial = call(
+        begin_body, "begin", [state, ((v_size * own, 2 * BLOCK), BF16), partial_shape], [],
+        projection, *inverse, residual, *wide, key_left, row_points,
     )
     solution_now = jnp.zeros(state[0], F32)
     for step in range(ITERS):
@@ -443,28 +463,34 @@
             project_body, "project", [((columns, piv + BLOCK), F32)], [],
             image, residual, direction, *wide,
         )[0]
-        packed = packed + partner(packed)
-        packed = packed + lax.ppermute(packed, CHIPS[2], [(0, 1), (1, 0)])
-        packed = share(packed, CHIPS[:2])
-        residual, direction, solution_now, projection, inner, squares, partial = call(
+        packed = half(packed, core) + partner(half(packed, 1 - core))
+        packed = packed + other_of_two(packed, CHIPS[1])
+        packed = jnp.sum(share(packed, (CHIPS[0], CHIPS[2])), axis=0)
+        packed = core_first(packed, partner(packed))
+        residual, direction, solution_now, projection, partial = call(
             advance_body, "advance",
-            [state, state, state, ((columns, piv), F32), scalar, scalar, partial_shape], [],
-            packed, image, residual, direction, solution_now, projection, inner, squares,
+            [state, state, state, ((columns, piv), F32), partial_shape], [],
+            packed, image, residual, direction, solution_now, projection,
             *inverse, *wide, key_left, row_right,
         )
-    curve = jnp.sum(direction_own * image_own, axis=1)
-    curve = jnp.zeros((1, BLOCK), F32).at[0, :columns].set(curve)
-    curve = jnp.sum(share(curve, ALL), axis=0)
-    alpha = inner[:, :1] / curve[0, :columns, None]
     solution_own = lax.dynamic_index_in_dim(solution_now, u_at, 0, keepdims=False)
     residual_own = lax.dynamic_index_in_dim(residual, u_at, 0, keepdims=False)
+    sums = jnp.concatenate(
+        [
+            jnp.sum(direction_own * image_own, axis=1),
+            jnp.sum(direction_own * residual_own, axis=1),
+            jnp.zeros((BLOCK - 2 * columns,), F32),
+        ]
+    )
+    sums = jnp.sum(share(sums[None], ALL), axis=(0, 1))
+    alpha = (sums[columns:2 * columns] / sums[:columns])[:, None]
     solution_own = solution_own + alpha * direction_own
     residual_own = residual_own - alpha * image_own
     return (factor, solution_own.T, residual_own.T)
 
 
 def solution(mesh):
-    sizes = (4, 8, 2, 2, 2) if mesh.devices.size == 256 else (2, 2, 1, 2, 2)
+    sizes = (4, 8, 2, 2, 2) if mesh.devices.size == 256 else (1, 2, 2, 2, 2)
     grid = Mesh(mesh.devices.reshape(sizes), ALL)
     return jax.shard_map(
         per_device,

time: 340 us -> 332 us (0.976); the launches traced: 339 us -> 328 us
  waiting for transfers between devices: 64.4 us -> 38.1 us
  Pallas kernels: 104 us -> 78.4 us
  blocking collectives: 101 us -> 125 us
  local copies, waits for them, and re-layouts: 10.5 us -> 27.8 us
    all_to_all x5 -> x4, waiting for transfers between devices: 47.3 us -> 19.9 us  [swap(): return lax.all_to_all(blocks, axes, 0, 0, tiled=False)]
    pallas_call x6 -> x8, Pallas kernels: 104 us -> 78.4 us  [call(): pl.pallas_call(body, out_shape=[jax.ShapeDtypeStruct(shape, dtype) for sh...]
    all_to_all x8 -> x11, blocking collectives: 101 us -> 125 us  [swap(): return lax.all_to_all(blocks, axes, 0, 0, tiled=False)]
    unnamed x63 -> x57, local copies, waits for them, and re-layouts: 6.37 us -> 23.3 us
    ppermute x12 -> x14, starting transfers between devices: 21.6 us -> 26.9 us  [other_of_two(): lax.ppermute(values, axis, [(i, (i + 1) % count) for i in range(count)])]
    all_to_all x5 -> x4, starting transfers between devices: 27 us -> 22.2 us  [swap(): return lax.all_to_all(blocks, axes, 0, 0, tiled=False)]
    ppermute x12 -> x14, waiting for transfers between devices: 17.1 us -> 18.3 us  [other_of_two(): lax.ppermute(values, axis, [(i, (i + 1) % count) for i in range(count)])]
  transfers between devices with their start and end apart: 17 -> 18, of which waited for: 16 -> 15; matrix products, arithmetic and copies ran while one was open for 1% -> 0% of each run, Pallas kernels for 0% -> 13%
where the time goes in v1:
time: 332 us; the launch traced here: 328 us
  blocking collectives  125 us (38%)
  Pallas kernels  78.4 us (24%)
  starting transfers between devices  49.1 us (15%)
  waiting for transfers between devices  38.1 us (11%)
  local copies, waits for them, and re-layouts  27.8 us (8%)
  other arithmetic  6.78 us (2%)
    all_to_all x11, blocking collectives, swap(): return lax.all_to_all(blocks, axes, 0, 0, tiled=False)  125 us
    pallas_call x8, Pallas kernels, call(): pl.pallas_call(body, out_shape=[jax.ShapeDtypeStruct(shape, dtype) for sh...  78.4 us
    ppermute x14, starting transfers between devices, other_of_two(): lax.ppermute(values, axis, [(i, (i + 1) % count) for i in range(count)])  26.9 us
    unnamed x57, local copies, waits for them, and re-layouts  23.3 us
    all_to_all x4, starting transfers between devices, swap(): return lax.all_to_all(blocks, axes, 0, 0, tiled=False)  22.2 us
    all_to_all x4, waiting for transfers between devices, swap(): return lax.all_to_all(blocks, axes, 0, 0, tiled=False)  19.9 us
    ppermute x14, waiting for transfers between devices, other_of_two(): lax.ppermute(values, axis, [(i, (i + 1) % count) for i in range(count)])  18.3 us
  transfers between devices with their start and end apart: 18, of which 15 were waited for; matrix products, arithmetic and copies ran while one was open for 0% of the time, Pallas kernels for 13%

profile of v1, /device:TPU:1, one launch (start us, length us, event | category | flops | bytes accessed | tf_op | source)
XLA Modules:
  0.0 327.7 jit_solution(13392648684585029979)
XLA Ops:
  2.4 3.3 %collective-permute-start = (bf16[256,128]{1,0:T(8,128)(2,1)S(1)}, bf16[256,128]{1,0:T(8,128)(2,1)S(1)}, u32[]{:S(2)}, u32[]{:S(2)}) collective-permute-start(bf16[256,128]{1,0:T(8,128)(2,1)S(1)} %constant_dynamic-slice_fusion.4), channel_id=1, source_target_pairs={{0,1},{1,0},{2,3},{3,2},{4,5},{5,4},{6,7},{7,6},{8,9},{9,8},{10,11... | collective-permute-start | bytes 196616 | tf_op jit(solution)/shard_map/ppermute | solution.py:37
  6.6 11.3 %all_to_all.75 = bf16[16,16,128]{2,1,0:T(8,128)(2,1)S(1)} all-to-all(bf16[16,16,128]{2,1,0:T(8,128)(2,1)S(1)} %bitcast.80), channel_id=1, replica_groups=mesh['x'=4,'z'=8,'yh'=2,'yl'=2,'c'=2] {'x','yh','yl'}, dimensions={0} | all-to-all | bytes 131072 | tf_op jit(solution)/shard_map/all_to_all | solution.py:27
  18.0 14.9 %all_to_all.76 = bf16[8,16,128]{2,1,0:T(8,128)(2,1)S(1)} all-to-all(bf16[8,16,128]{2,1,0:T(8,128)(2,1)S(1)} %broadcast_in_dim.28), channel_id=1, replica_groups=mesh['x'=4,'z'=8,'yh'=2,'yl'=2,'c'=2] {'z'}, dimensions={0} | all-to-all | bytes 65536 | tf_op jit(solution)/shard_map/all_to_all | solution.py:27
  32.9 9.8 %all_to_all.77 = bf16[16,16,128]{2,1,0:T(8,128)(2,1)S(1)} all-to-all(bf16[16,16,128]{2,1,0:T(8,128)(2,1)S(1)} %broadcast_in_dim.29), channel_id=1, replica_groups=mesh['x'=4,'z'=8,'yh'=2,'yl'=2,'c'=2] {'x','yh','yl'}, dimensions={0} | all-to-all | bytes 131072 | tf_op jit(solution)/shard_map/all_to_all | solution.py:27
  42.7 4.3 %collective-permute-start.1 = (bf16[16,16,128]{2,1,0:T(8,128)(2,1)S(1)}, bf16[16,16,128]{2,1,0:T(8,128)(2,1)S(1)}, u32[]{:S(2)}, u32[]{:S(2)}) collective-permute-start(bf16[16,16,128]{2,1,0:T(8,128)(2,1)S(1)} %all_to_all.77), channel_id=1, source_target_pairs={{0,1},{1,0},{2,3},{3,2},{4,5},{5,4},{6,7},{7,6},{8,9},{9,8},{10,11... | collective-permute-start | bytes 196616 | tf_op jit(solution)/shard_map/ppermute | solution.py:37
  50.3 3.6 %all-to-all-start.3 = ((bf16[8,224,128]{2,1,0:T(8,128)(2,1)}), bf16[8,224,128]{2,1,0:T(8,128)(2,1)S(1)}, u32[]{:S(2)}, u32[]{:S(2)}) async-start(bf16[8,224,128]{2,1,0:T(8,128)(2,1)} %broadcast_in_dim.30), calls=%async_computation.3 | async-start | bytes 917504 | tf_op jit(solution)/shard_map/all_to_all | solution.py:27
  53.9 21.4 %pivots_factor.1 = (f32[512,512]{1,0:T(8,128)S(1)}, bf16[512,256]{1,0:T(8,128)(2,1)S(1)}) custom-call(bf16[512,128]{1,0:T(8,128)(2,1)S(1)} %bitcast.77), custom_call_target="tpu_custom_call" | custom-call | flops 22000001024 | bytes 66000000 | tf_op jit(solution)/shard_map/pivots_factor/pallas_call | solution.py:379
  79.4 7.9 %setup_factor.1 = (bf16[1024,512]{1,0:T(8,128)(2,1)S(1)}, bf16[1024,512]{1,0:T(8,128)(2,1)S(1)}, bf16[1024,512]{1,0:T(8,128)(2,1)S(1)}, bf16[1024,256]{1,0:T(8,128)(2,1)S(1)}, f32[32,48,128]{2,1,0:T(8,128)S(1)}) custom-call(f32[512,512]{1,0:T(8,128)S(1)} %copy-done.5, bf16[512,256]{1,0:T(8,128)(2,1)S(1)} %copy-done.19, bf16[1024,128]{1,0:T(8,128)(2,1)S(1)} %bitcast.76, ...), custom_call_target="tpu_custom_call" | custom-call | flops 10000000000 | bytes 30000000 | tf_op jit(solution)/shard_map/setup_factor/pallas_call | solution.py:379
  92.2 12.2 %all_to_all.78 = f32[16,48,128]{2,1,0:T(8,128)S(1)} all-to-all(f32[16,48,128]{2,1,0:T(8,128)S(1)} %dynamic-slice_add_fusion), channel_id=1, replica_groups=mesh['x'=4,'z'=8,'yh'=2,'yl'=2,'c'=2] {'x','yh','yl'}, dimensions={0} | all-to-all | bytes 786432 | tf_op jit(solution)/shard_map/all_to_all | solution.py:27
  104.5 11.3 %all_to_all.79 = f32[16,48,128]{2,1,0:T(8,128)S(1)} all-to-all(f32[16,48,128]{2,1,0:T(8,128)S(1)} %broadcast_in_dim.31), channel_id=1, replica_groups=mesh['x'=4,'z'=8,'yh'=2,'yl'=2,'c'=2] {'x','yh','yl'}, dimensions={0} | all-to-all | bytes 786432 | tf_op jit(solution)/shard_map/all_to_all | solution.py:27
  115.8 2.9 collective-permute-start.4
  121.4 4.7 %all-to-all-start.6 = ((bf16[16,256,128]{2,1,0:T(8,128)(2,1)}), bf16[16,256,128]{2,1,0:T(8,128)(2,1)}, u32[]{:S(2)}, u32[]{:S(2)}) async-start(bf16[16,256,128]{2,1,0:T(8,128)(2,1)} %broadcast_in_dim.32), calls=%async_computation.6 | async-start | bytes 2097152 | tf_op jit(solution)/shard_map/all_to_all | solution.py:27
  126.1 21.3 %gram_factor.1 = (bf16[512,512]{1,0:T(8,128)(2,1)S(1)}, bf16[512,512]{1,0:T(8,128)(2,1)S(1)}, bf16[512,512]{1,0:T(8,128)(2,1)S(1)}, f32[32,512]{1,0:T(8,128)S(1)}) custom-call(f32[32,48,128]{2,1,0:T(8,128)S(1)} %pad_maximum_fusion.packed_ref), custom_call_target="tpu_custom_call" | custom-call | flops 22000001024 | bytes 66000000 | tf_op jit(solution)/shard_map/gram_factor/pallas_call | solution.py:379
  155.7 8.8 %begin.1 = (f32[8,32,128]{2,1,0:T(8,128)S(1)}, bf16[4096,256]{1,0:T(8,128)(2,1)}, f32[32,32,128]{2,1,0:T(8,128)S(1)}) custom-call(f32[32,512]{1,0:T(8,128)S(1)} %copy-done.23, bf16[512,512]{1,0:T(8,128)(2,1)S(1)} %copy-done.7, bf16[512,512]{1,0:T(8,128)(2,1)S(1)} %copy-done.11, bf16[512,512]{1,0:T(8,128)(2,1)S(1)} %copy-done.15, ...), custom_call_target="tpu_custom_call" | custom-call | flops 10000000000 | bytes 30000000 | tf_op jit(solution)/shard_map/begin/pallas_call | solution.py:379
  166.8 7.0 %all-to-all-start.7 = ((f32[16,32,128]{2,1,0:T(8,128)}), f32[16,32,128]{2,1,0:T(8,128)S(1)}, u32[]{:S(2)}, u32[]{:S(2)}) async-start(f32[16,32,128]{2,1,0:T(8,128)} %slice_add_fusion.2), calls=%async_computation.7 | async-start | bytes 524288 | tf_op jit(solution)/shard_map/all_to_all | solution.py:27
  173.8 7.6 %all-to-all-done.7 = f32[16,32,128]{2,1,0:T(8,128)S(1)} async-done(((f32[16,32,128]{2,1,0:T(8,128)}), f32[16,32,128]{2,1,0:T(8,128)S(1)}, u32[]{:S(2)}, u32[]{:S(2)}) %all-to-all-start.7) | async-done | bytes 262176 | tf_op jit(solution)/shard_map/all_to_all | solution.py:27
  181.4 14.7 %all_to_all.80.image_ref = f32[8,32,128]{2,1,0:T(8,128)S(1)} all-to-all(f32[8,32,128]{2,1,0:T(8,128)S(1)} %broadcast_in_dim.34), channel_id=1, replica_groups=mesh['x'=4,'z'=8,'yh'=2,'yl'=2,'c'=2] {'z'}, dimensions={0} | all-to-all | bytes 262144 | tf_op jit(solution)/shard_map/all_to_all | solution.py:27
  198.0 3.5 %collective-permute-start.6 = (f32[16,640]{1,0:T(8,128)S(1)}, f32[16,640]{1,0:T(8,128)S(1)}, u32[]{:S(2)}, u32[]{:S(2)}) collective-permute-start(f32[16,640]{1,0:T(8,128)S(1)} %constant_dynamic-slice_fusion.1), channel_id=1, source_target_pairs={{0,1},{1,0},{2,3},{3,2},{4,5},{5,4},{6,7},{7,6},{8,9},{9,8},{10,11... | collective-permute-start | bytes 122888 | tf_op jit(solution)/shard_map/ppermute | solution.py:37
  203.5 3.2 collective-permute-done.7
  206.7 9.7 %all_to_all.81 = f32[8,16,640]{2,1,0:T(8,128)} all-to-all(f32[8,16,640]{2,1,0:T(8,128)S(1)} %broadcast_in_dim.35), channel_id=1, replica_groups=mesh['x'=4,'z'=8,'yh'=2,'yl'=2,'c'=2] {'x','yl'}, dimensions={0} | all-to-all | bytes 655360 | tf_op jit(solution)/shard_map/all_to_all | solution.py:27
  217.4 2.7 collective-permute-start.8
  224.2 8.8 %advance.2 = (f32[8,32,128]{2,1,0:T(8,128)S(1)}, f32[8,32,128]{2,1,0:T(8,128)S(1)}, f32[8,32,128]{2,1,0:T(8,128)S(1)}, f32[32,512]{1,0:T(8,128)S(1)}, f32[32,32,128]{2,1,0:T(8,128)S(1)}) custom-call(f32[32,640]{1,0:T(8,128)S(1)} %pad_maximum_fusion.2.packed_ref, f32[8,32,128]{2,1,0:T(8,128)S(1)} %all_to_all.80.image_ref, ...), custom_call_target="tpu_custom_call" | custom-call | flops 10000000000 | bytes 30000000 | tf_op jit(solution)/shard_map/advance/pallas_call | solution.py:379
  234.8 10.7 %all_to_all.82 = f32[16,32,128]{2,1,0:T(8,128)S(1)} all-to-all(f32[16,32,128]{2,1,0:T(8,128)S(1)} %slice_add_fusion.1), channel_id=1, replica_groups=mesh['x'=4,'z'=8,'yh'=2,'yl'=2,'c'=2] {'x','yh','yl'}, dimensions={0} | all-to-all | bytes 524288 | tf_op jit(solution)/shard_map/all_to_all | solution.py:27
  245.6 10.3 %all_to_all.83.image_ref = f32[8,32,128]{2,1,0:T(8,128)S(1)} all-to-all(f32[8,32,128]{2,1,0:T(8,128)S(1)} %broadcast_in_dim.38), channel_id=1, replica_groups=mesh['x'=4,'z'=8,'yh'=2,'yl'=2,'c'=2] {'z'}, dimensions={0} | all-to-all | bytes 262144 | tf_op jit(solution)/shard_map/all_to_all | solution.py:27
  257.8 3.1 collective-permute-start.10
  262.9 3.2 collective-permute-done.11
  266.1 9.7 %all_to_all.84 = f32[8,16,640]{2,1,0:T(8,128)} all-to-all(f32[8,16,640]{2,1,0:T(8,128)S(1)} %broadcast_in_dim.39), channel_id=1, replica_groups=mesh['x'=4,'z'=8,'yh'=2,'yl'=2,'c'=2] {'x','yl'}, dimensions={0} | all-to-all | bytes 655360 | tf_op jit(solution)/shard_map/all_to_all | solution.py:27
  276.8 2.9 collective-permute-start.12
  284.6 8.8 %advance.3 = (f32[8,32,128]{2,1,0:T(8,128)S(1)}, f32[8,32,128]{2,1,0:T(8,128)S(1)}, f32[8,32,128]{2,1,0:T(8,128)S(1)}, f32[32,512]{1,0:T(8,128)}, f32[32,32,128]{2,1,0:T(8,128)S(1)}) custom-call(f32[32,640]{1,0:T(8,128)S(1)} %pad_maximum_fusion.3.packed_ref, f32[8,32,128]{2,1,0:T(8,128)S(1)} %all_to_all.83.image_ref, ...), custom_call_target="tpu_custom_call" | custom-call | flops 10000000000 | bytes 30000000 | tf_op jit(solution)/shard_map/advance/pallas_call | solution.py:379
  295.2 10.7 %all_to_all.85 = f32[16,32,128]{2,1,0:T(8,128)S(1)} all-to-all(f32[16,32,128]{2,1,0:T(8,128)S(1)} %slice_add_fusion), channel_id=1, replica_groups=mesh['x'=4,'z'=8,'yh'=2,'yl'=2,'c'=2] {'x','yh','yl'}, dimensions={0} | all-to-all | bytes 524288 | tf_op jit(solution)/shard_map/all_to_all | solution.py:27
  306.9 6.9 %all-to-all-start.14 = ((f32[256,1,128]{2,1,0:T(1,128)}), f32[256,1,128]{2,1,0:T(1,128)S(1)}, u32[]{:S(2)}, u32[]{:S(2)}) async-start(f32[256,1,128]{2,1,0:T(1,128)} %broadcast_in_dim.41), calls=%async_computation.14 | async-start | bytes 262144 | tf_op jit(solution)/shard_map/all_to_all | solution.py:27
  314.4 12.3 %all-to-all-done.14 = f32[256,1,128]{2,1,0:T(1,128)S(1)} async-done(((f32[256,1,128]{2,1,0:T(1,128)}), f32[256,1,128]{2,1,0:T(1,128)S(1)}, u32[]{:S(2)}, u32[]{:S(2)}) %all-to-all-start.14) | async-done | bytes 131104 | tf_op jit(solution)/shard_map/all_to_all | solution.py:27
  (141 shorter events, 52.8 us)
Async XLA Ops:
  2.4 4.2 %collective-permute-start = (bf16[256,128]{1,0:T(8,128)(2,1)S(1)}, bf16[256,128]{1,0:T(8,128)(2,1)S(1)}, u32[]{:S(2)}, u32[]{:S(2)}) collective-permute-start(bf16[256,128]{1,0:T(8,128)(2,1)S(1)} %constant_dynamic-slice_fusion.4), channel_id=1, source_target_pairs={{0,1},{1,0},{2,3},{3,2},{4,5},{5,4},{6,7},{7,6},{8,9},{9,8},{10,11... | collective-permute-start | bytes 196616 | tf_op jit(solution)/shard_map/ppermute | solution.py:37
  42.7 5.2 %collective-permute-start.1 = (bf16[16,16,128]{2,1,0:T(8,128)(2,1)S(1)}, bf16[16,16,128]{2,1,0:T(8,128)(2,1)S(1)}, u32[]{:S(2)}, u32[]{:S(2)}) collective-permute-start(bf16[16,16,128]{2,1,0:T(8,128)(2,1)S(1)} %all_to_all.77), channel_id=1, source_target_pairs={{0,1},{1,0},{2,3},{3,2},{4,5},{5,4},{6,7},{7,6},{8,9},{9,8},{10,11... | collective-permute-start | bytes 196616 | tf_op jit(solution)/shard_map/ppermute | solution.py:37
  50.3 26.8 %all-to-all-start.3 = ((bf16[8,224,128]{2,1,0:T(8,128)(2,1)}), bf16[8,224,128]{2,1,0:T(8,128)(2,1)S(1)}, u32[]{:S(2)}, u32[]{:S(2)}) async-start(bf16[8,224,128]{2,1,0:T(8,128)(2,1)} %broadcast_in_dim.30), calls=%async_computation.3 | async-start | bytes 917504 | tf_op jit(solution)/shard_map/all_to_all | solution.py:27
  77.2 1.2 copy-start.5
  89.1 2.1 collective-permute-start.3
  92.2 26.5 %copy-start.27 = (bf16[128,128]{1,0:T(8,128)(2,1)S(1)}, bf16[128,128]{1,0:T(8,128)(2,1)}, u32[]{:S(2)}) copy-start(bf16[128,128]{1,0:T(8,128)(2,1)} %param.3) | copy-start | bytes 98308
  115.8 4.3 %collective-permute-start.4 = (f32[16,48,128]{2,1,0:T(8,128)S(1)}, f32[16,48,128]{2,1,0:T(8,128)S(1)}, u32[]{:S(2)}, u32[]{:S(2)}) collective-permute-start(f32[16,48,128]{2,1,0:T(8,128)S(1)} %all_to_all.79), channel_id=1, source_target_pairs={{0,1},{1,0},{2,3},{3,2},{4,5},{5,4},{6,7},{7,6},{8,9},{9,8},{10,11... | collective-permute-start | bytes 1179656 | tf_op jit(solution)/shard_map/ppermute | solution.py:37
  118.6 1.4 collective-permute-start.2
  121.4 29.1 %all-to-all-start.6 = ((bf16[16,256,128]{2,1,0:T(8,128)(2,1)}), bf16[16,256,128]{2,1,0:T(8,128)(2,1)}, u32[]{:S(2)}, u32[]{:S(2)}) async-start(bf16[16,256,128]{2,1,0:T(8,128)(2,1)} %broadcast_in_dim.32), calls=%async_computation.6 | async-start | bytes 2097152 | tf_op jit(solution)/shard_map/all_to_all | solution.py:27
  150.5 1.2 copy-start.1
  151.7 1.0 copy-start.7
  152.7 1.0 copy-start.11
  153.8 1.0 copy-start.15
  164.5 1.6 collective-permute-start.5
  166.8 14.5 %all-to-all-start.7 = ((f32[16,32,128]{2,1,0:T(8,128)}), f32[16,32,128]{2,1,0:T(8,128)S(1)}, u32[]{:S(2)}, u32[]{:S(2)}) async-start(f32[16,32,128]{2,1,0:T(8,128)} %slice_add_fusion.2), calls=%async_computation.7 | async-start | bytes 524288 | tf_op jit(solution)/shard_map/all_to_all | solution.py:27
  196.1 1.2 copy-start.2
  198.0 23.1 %copy-start.24 = (f32[32,512]{1,0:T(8,128)S(1)}, f32[32,512]{1,0:T(8,128)}, u32[]{:S(2)}) copy-start(f32[32,512]{1,0:T(8,128)} %copy-done.22) | copy-start | bytes 196612
  198.0 4.4 %collective-permute-start.6 = (f32[16,640]{1,0:T(8,128)S(1)}, f32[16,640]{1,0:T(8,128)S(1)}, u32[]{:S(2)}, u32[]{:S(2)}) collective-permute-start(f32[16,640]{1,0:T(8,128)S(1)} %constant_dynamic-slice_fusion.1), channel_id=1, source_target_pairs={{0,1},{1,0},{2,3},{3,2},{4,5},{5,4},{6,7},{7,6},{8,9},{9,8},{10,11... | collective-permute-start | bytes 122888 | tf_op jit(solution)/shard_map/ppermute | solution.py:37
  202.4 4.4 %collective-permute-start.7 = (f32[16,640]{1,0:T(8,128)S(1)}, f32[16,640]{1,0:T(8,128)S(1)}, u32[]{:S(2)}, u32[]{:S(2)}) collective-permute-start(f32[16,640]{1,0:T(8,128)S(1)} %dynamic-slice_add_fusion.3), channel_id=1, source_target_pairs={{0,4},{4,0},{1,5},{5,1},{2,6},{6,2},{3,7},{7,3},{8,12},{12,8},{9,1... | collective-permute-start | bytes 122888 | tf_op jit(solution)/shard_map/ppermute | solution.py:37
  217.4 3.6 %collective-permute-start.8 = (f32[16,640]{1,0:T(8,128)S(1)}, f32[16,640]{1,0:T(8,128)S(1)}, u32[]{:S(2)}, u32[]{:S(2)}) collective-permute-start(f32[16,640]{1,0:T(8,128)S(1)} %reduce_sum.114), channel_id=1, source_target_pairs={{0,1},{1,0},{2,3},{3,2},{4,5},{5,4},{6,7},{7,6},{8,9},{9,8},{10,11... | collective-permute-start | bytes 122888 | tf_op jit(solution)/shard_map/ppermute | solution.py:37
  221.1 1.0 copy-start.8
  233.1 1.7 copy-start.20
  233.1 24.7 %copy-start.25 = (f32[32,512]{1,0:T(8,128)}, f32[32,512]{1,0:T(8,128)S(1)}, u32[]{:S(2)}) copy-start(f32[32,512]{1,0:T(8,128)S(1)} %get-tuple-element.54.proj_ref) | copy-start | bytes 196612
  233.1 1.6 collective-permute-start.9
  255.9 1.2 copy-start.3
  257.1 23.5 %copy-start.21 = (f32[8,32,128]{2,1,0:T(8,128)S(1)}, f32[8,32,128]{2,1,0:T(8,128)}, u32[]{:S(2)}) copy-start(f32[8,32,128]{2,1,0:T(8,128)} %copy-done.20) | copy-start | bytes 393220
  257.8 4.0 %collective-permute-start.10 = (f32[16,640]{1,0:T(8,128)S(1)}, f32[16,640]{1,0:T(8,128)S(1)}, u32[]{:S(2)}, u32[]{:S(2)}) collective-permute-start(f32[16,640]{1,0:T(8,128)S(1)} %constant_dynamic-slice_fusion), channel_id=1, source_target_pairs={{0,1},{1,0},{2,3},{3,2},{4,5},{5,4},{6,7},{7,6},{8,9},{9,8},{10,11... | collective-permute-start | bytes 122888 | tf_op jit(solution)/shard_map/ppermute | solution.py:37
  261.7 4.4 %collective-permute-start.11 = (f32[16,640]{1,0:T(8,128)S(1)}, f32[16,640]{1,0:T(8,128)S(1)}, u32[]{:S(2)}, u32[]{:S(2)}) collective-permute-start(f32[16,640]{1,0:T(8,128)S(1)} %dynamic-slice_add_fusion.2), channel_id=1, source_target_pairs={{0,4},{4,0},{1,5},{5,1},{2,6},{6,2},{3,7},{7,3},{8,12},{12,8},{9,1... | collective-permute-start | bytes 122888 | tf_op jit(solution)/shard_map/ppermute | solution.py:37
  276.8 3.8 %collective-permute-start.12 = (f32[16,640]{1,0:T(8,128)S(1)}, f32[16,640]{1,0:T(8,128)S(1)}, u32[]{:S(2)}, u32[]{:S(2)}) collective-permute-start(f32[16,640]{1,0:T(8,128)S(1)} %reduce_sum.117), channel_id=1, source_target_pairs={{0,1},{1,0},{2,3},{3,2},{4,5},{5,4},{6,7},{7,6},{8,9},{9,8},{10,11... | collective-permute-start | bytes 122888 | tf_op jit(solution)/shard_map/ppermute | solution.py:37
  280.7 1.0 copy-start.9
  293.5 1.6 collective-permute-start.13
  306.9 19.8 %all-to-all-start.14 = ((f32[256,1,128]{2,1,0:T(1,128)}), f32[256,1,128]{2,1,0:T(1,128)S(1)}, u32[]{:S(2)}, u32[]{:S(2)}) async-start(f32[256,1,128]{2,1,0:T(1,128)} %broadcast_in_dim.41), calls=%async_computation.14 | async-start | bytes 262144 | tf_op jit(solution)/shard_map/all_to_all | solution.py:27
  (14 other events, 12.6 us)

commit v2 on v1

--- a/solution.py
+++ b/solution.py
@@ -123,7 +123,15 @@
         rows, inverses, steps = [], [], []
         for j in range(STRIDE):
             r = first % GROUP + j
-            inverse = 1.0 / jnp.broadcast_to(own[j][r:r + 1, :], (GROUP, order))
+            if j % 2 == 0:
+                pivot = jnp.broadcast_to(own[j][r:r + 1, :], (GROUP, order))
+                below = jnp.broadcast_to(own[j][r + 1:r + 2, :], (GROUP, order))
+                beside = jnp.broadcast_to(own[j + 1][r:r + 1, :], (GROUP, order))
+                corner = jnp.broadcast_to(own[j + 1][r + 1:r + 2, :], (GROUP, order))
+                inverse = 1.0 / pivot
+                following = pivot * (1.0 / (pivot * corner - below * beside))
+            else:
+                inverse = following
             mult = jnp.where(sub > r, own[j] * inverse, 0.0)
             steps.append(
                 [
@@ -376,8 +384,11 @@
 
 
 def call(body, name, outs, scratch, *args, seconds=10e-6):
+    spec = pl.BlockSpec(memory_space=pltpu.VMEM)
     return pl.pallas_call(
         body,
+        in_specs=[spec] * len(args),
+        out_specs=[spec] * len(outs),
         out_shape=[jax.ShapeDtypeStruct(shape, dtype) for shape, dtype in outs],
         scratch_shapes=scratch,
         compiler_params=pltpu.CompilerParams(vmem_limit_bytes=48 << 20),
@@ -464,8 +475,7 @@
             image, residual, direction, *wide,
         )[0]
         packed = half(packed, core) + partner(half(packed, 1 - core))
-        packed = packed + other_of_two(packed, CHIPS[1])
-        packed = jnp.sum(share(packed, (CHIPS[0], CHIPS[2])), axis=0)
+        packed = jnp.sum(share(packed, CHIPS), axis=0)
         packed = core_first(packed, partner(packed))
         residual, direction, solution_now, projection, partial = call(
             advance_body, "advance",

time: 332 us -> 336 us (1.012)
  blocking collectives: 125 us -> 136 us
  waiting for transfers between devices: 38.1 us -> 31.8 us
  starting transfers between devices: 49.1 us -> 44.7 us
    all_to_all x11, blocking collectives: 125 us -> 136 us  [swap(): return lax.all_to_all(blocks, axes, 0, 0, tiled=False)]
    ppermute x14 -> x12, waiting for transfers between devices: 18.3 us -> 11.9 us  [other_of_two(): lax.ppermute(values, axis, [(i, (i + 1) % count) for i in range(count)])]
    ppermute x14 -> x12, starting transfers between devices: 26.9 us -> 23 us  [other_of_two(): lax.ppermute(values, axis, [(i, (i + 1) % count) for i in range(count)])]
  transfers between devices with their start and end apart: 18 -> 16, of which waited for: 15 -> 13; matrix products, arithmetic and copies ran while one was open for 0% -> 0% of each run, Pallas kernels for 13% -> 14%
where the time goes in v2:
time: 336 us; the launch traced here: 331 us
  blocking collectives  136 us (40%)
  Pallas kernels  81 us (24%)
  starting transfers between devices  44.7 us (13%)
  waiting for transfers between devices  31.8 us (9%)
  local copies, waits for them, and re-layouts  27.9 us (8%)
  other arithmetic  7.04 us (2%)
    all_to_all x11, blocking collectives, swap(): return lax.all_to_all(blocks, axes, 0, 0, tiled=False)  136 us
    pallas_call x8, Pallas kernels, call(): pl.pallas_call(body, in_specs=[spec] * len(args), out_specs=[spec] * len(...  81 us
    unnamed x57, local copies, waits for them, and re-layouts  23.3 us
    ppermute x12, starting transfers between devices, other_of_two(): lax.ppermute(values, axis, [(i, (i + 1) % count) for i in range(count)])  23 us
    all_to_all x4, starting transfers between devices, swap(): return lax.all_to_all(blocks, axes, 0, 0, tiled=False)  21.7 us
    all_to_all x4, waiting for transfers between devices, swap(): return lax.all_to_all(blocks, axes, 0, 0, tiled=False)  19.9 us
    ppermute x12, waiting for transfers between devices, other_of_two(): lax.ppermute(values, axis, [(i, (i + 1) % count) for i in range(count)])  11.9 us
  transfers between devices with their start and end apart: 16, of which 13 were waited for; matrix products, arithmetic and copies ran while one was open for 0% of the time, Pallas kernels for 14%

profile of v2, /device:TPU:1, one launch (start us, length us, event | category | flops | bytes accessed | tf_op | source)
XLA Modules:
  0.0 331.1 jit_solution(11841724299682850715)
XLA Ops:
  2.4 3.3 %collective-permute-start = (bf16[256,128]{1,0:T(8,128)(2,1)S(1)}, bf16[256,128]{1,0:T(8,128)(2,1)S(1)}, u32[]{:S(2)}, u32[]{:S(2)}) collective-permute-start(bf16[256,128]{1,0:T(8,128)(2,1)S(1)} %constant_dynamic-slice_fusion.4), channel_id=1, source_target_pairs={{0,1},{1,0},{2,3},{3,2},{4,5},{5,4},{6,7},{7,6},{8,9},{9,8},{10,11... | collective-permute-start | bytes 196616 | tf_op jit(solution)/shard_map/ppermute | solution.py:37
  6.6 11.3 %all_to_all.75 = bf16[16,16,128]{2,1,0:T(8,128)(2,1)S(1)} all-to-all(bf16[16,16,128]{2,1,0:T(8,128)(2,1)S(1)} %bitcast.80), channel_id=1, replica_groups=mesh['x'=4,'z'=8,'yh'=2,'yl'=2,'c'=2] {'x','yh','yl'}, dimensions={0} | all-to-all | bytes 131072 | tf_op jit(solution)/shard_map/all_to_all | solution.py:27
  18.0 14.9 %all_to_all.76 = bf16[8,16,128]{2,1,0:T(8,128)(2,1)S(1)} all-to-all(bf16[8,16,128]{2,1,0:T(8,128)(2,1)S(1)} %broadcast_in_dim.28), channel_id=1, replica_groups=mesh['x'=4,'z'=8,'yh'=2,'yl'=2,'c'=2] {'z'}, dimensions={0} | all-to-all | bytes 65536 | tf_op jit(solution)/shard_map/all_to_all | solution.py:27
  32.9 9.8 %all_to_all.77 = bf16[16,16,128]{2,1,0:T(8,128)(2,1)S(1)} all-to-all(bf16[16,16,128]{2,1,0:T(8,128)(2,1)S(1)} %broadcast_in_dim.29), channel_id=1, replica_groups=mesh['x'=4,'z'=8,'yh'=2,'yl'=2,'c'=2] {'x','yh','yl'}, dimensions={0} | all-to-all | bytes 131072 | tf_op jit(solution)/shard_map/all_to_all | solution.py:27
  42.7 4.3 %collective-permute-start.1 = (bf16[16,16,128]{2,1,0:T(8,128)(2,1)S(1)}, bf16[16,16,128]{2,1,0:T(8,128)(2,1)S(1)}, u32[]{:S(2)}, u32[]{:S(2)}) collective-permute-start(bf16[16,16,128]{2,1,0:T(8,128)(2,1)S(1)} %all_to_all.77), channel_id=1, source_target_pairs={{0,1},{1,0},{2,3},{3,2},{4,5},{5,4},{6,7},{7,6},{8,9},{9,8},{10,11... | collective-permute-start | bytes 196616 | tf_op jit(solution)/shard_map/ppermute | solution.py:37
  50.3 3.6 %all-to-all-start.3 = ((bf16[8,224,128]{2,1,0:T(8,128)(2,1)}), bf16[8,224,128]{2,1,0:T(8,128)(2,1)S(1)}, u32[]{:S(2)}, u32[]{:S(2)}) async-start(bf16[8,224,128]{2,1,0:T(8,128)(2,1)} %broadcast_in_dim.30), calls=%async_computation.3 | async-start | bytes 917504 | tf_op jit(solution)/shard_map/all_to_all | solution.py:27
  53.9 22.7 %pivots_factor.1 = (f32[512,512]{1,0:T(8,128)S(1)}, bf16[512,256]{1,0:T(8,128)(2,1)S(1)}) custom-call(bf16[512,128]{1,0:T(8,128)(2,1)S(1)} %bitcast.77), custom_call_target="tpu_custom_call" | custom-call | flops 22000001024 | bytes 66000000 | tf_op jit(solution)/shard_map/pivots_factor/pallas_call | solution.py:388
  80.7 7.9 %setup_factor.1 = (bf16[1024,512]{1,0:T(8,128)(2,1)S(1)}, bf16[1024,512]{1,0:T(8,128)(2,1)S(1)}, bf16[1024,512]{1,0:T(8,128)(2,1)S(1)}, bf16[1024,256]{1,0:T(8,128)(2,1)S(1)}, f32[32,48,128]{2,1,0:T(8,128)S(1)}) custom-call(f32[512,512]{1,0:T(8,128)S(1)} %copy-done.5, bf16[512,256]{1,0:T(8,128)(2,1)S(1)} %copy-done.19, bf16[1024,128]{1,0:T(8,128)(2,1)S(1)} %bitcast.76, ...), custom_call_target="tpu_custom_call" | custom-call | flops 10000000000 | bytes 30000000 | tf_op jit(solution)/shard_map/setup_factor/pallas_call | solution.py:388
  91.1 1.7 collective-permute-done.3
  93.9 12.2 %all_to_all.78 = f32[16,48,128]{2,1,0:T(8,128)S(1)} all-to-all(f32[16,48,128]{2,1,0:T(8,128)S(1)} %dynamic-slice_add_fusion), channel_id=1, replica_groups=mesh['x'=4,'z'=8,'yh'=2,'yl'=2,'c'=2] {'x','yh','yl'}, dimensions={0} | all-to-all | bytes 786432 | tf_op jit(solution)/shard_map/all_to_all | solution.py:27
  106.1 11.3 %all_to_all.79 = f32[16,48,128]{2,1,0:T(8,128)S(1)} all-to-all(f32[16,48,128]{2,1,0:T(8,128)S(1)} %broadcast_in_dim.31), channel_id=1, replica_groups=mesh['x'=4,'z'=8,'yh'=2,'yl'=2,'c'=2] {'x','yh','yl'}, dimensions={0} | all-to-all | bytes 786432 | tf_op jit(solution)/shard_map/all_to_all | solution.py:27
  117.4 2.9 collective-permute-start.4
  120.3 1.4 collective-permute-done.2
  123.1 4.3 %all-to-all-start.6 = ((bf16[16,256,128]{2,1,0:T(8,128)(2,1)}), bf16[16,256,128]{2,1,0:T(8,128)(2,1)}, u32[]{:S(2)}, u32[]{:S(2)}) async-start(bf16[16,256,128]{2,1,0:T(8,128)(2,1)} %broadcast_in_dim.32), calls=%async_computation.6 | async-start | bytes 2097152 | tf_op jit(solution)/shard_map/all_to_all | solution.py:27
  127.4 22.6 %gram_factor.1 = (bf16[512,512]{1,0:T(8,128)(2,1)S(1)}, bf16[512,512]{1,0:T(8,128)(2,1)S(1)}, bf16[512,512]{1,0:T(8,128)(2,1)S(1)}, f32[32,512]{1,0:T(8,128)S(1)}) custom-call(f32[32,48,128]{2,1,0:T(8,128)S(1)} %pad_maximum_fusion.packed_ref), custom_call_target="tpu_custom_call" | custom-call | flops 22000001024 | bytes 66000000 | tf_op jit(solution)/shard_map/gram_factor/pallas_call | solution.py:388
  158.3 8.8 %begin.1 = (f32[8,32,128]{2,1,0:T(8,128)S(1)}, bf16[4096,256]{1,0:T(8,128)(2,1)}, f32[32,32,128]{2,1,0:T(8,128)S(1)}) custom-call(f32[32,512]{1,0:T(8,128)S(1)} %copy-done.23, bf16[512,512]{1,0:T(8,128)(2,1)S(1)} %copy-done.7, bf16[512,512]{1,0:T(8,128)(2,1)S(1)} %copy-done.11, bf16[512,512]{1,0:T(8,128)(2,1)S(1)} %copy-done.15, ...), custom_call_target="tpu_custom_call" | custom-call | flops 10000000000 | bytes 30000000 | tf_op jit(solution)/shard_map/begin/pallas_call | solution.py:388
  169.5 6.8 %all-to-all-start.7 = ((f32[16,32,128]{2,1,0:T(8,128)}), f32[16,32,128]{2,1,0:T(8,128)S(1)}, u32[]{:S(2)}, u32[]{:S(2)}) async-start(f32[16,32,128]{2,1,0:T(8,128)} %slice_add_fusion.2), calls=%async_computation.7 | async-start | bytes 524288 | tf_op jit(solution)/shard_map/all_to_all | solution.py:27
  176.3 7.6 %all-to-all-done.7 = f32[16,32,128]{2,1,0:T(8,128)S(1)} async-done(((f32[16,32,128]{2,1,0:T(8,128)}), f32[16,32,128]{2,1,0:T(8,128)S(1)}, u32[]{:S(2)}, u32[]{:S(2)}) %all-to-all-start.7) | async-done | bytes 262176 | tf_op jit(solution)/shard_map/all_to_all | solution.py:27
  183.9 14.7 %all_to_all.80.image_ref = f32[8,32,128]{2,1,0:T(8,128)S(1)} all-to-all(f32[8,32,128]{2,1,0:T(8,128)S(1)} %broadcast_in_dim.34), channel_id=1, replica_groups=mesh['x'=4,'z'=8,'yh'=2,'yl'=2,'c'=2] {'z'}, dimensions={0} | all-to-all | bytes 262144 | tf_op jit(solution)/shard_map/all_to_all | solution.py:27
  200.5 3.5 %collective-permute-start.6 = (f32[16,640]{1,0:T(8,128)S(1)}, f32[16,640]{1,0:T(8,128)S(1)}, u32[]{:S(2)}, u32[]{:S(2)}) collective-permute-start(f32[16,640]{1,0:T(8,128)S(1)} %constant_dynamic-slice_fusion.1), channel_id=1, source_target_pairs={{0,1},{1,0},{2,3},{3,2},{4,5},{5,4},{6,7},{7,6},{8,9},{9,8},{10,11... | collective-permute-start | bytes 122888 | tf_op jit(solution)/shard_map/ppermute | solution.py:37
  204.9 15.3 %all_to_all.81 = f32[16,16,640]{2,1,0:T(8,128)} all-to-all(f32[16,16,640]{2,1,0:T(8,128)S(1)} %broadcast_in_dim.35), channel_id=1, replica_groups=mesh['x'=4,'z'=8,'yh'=2,'yl'=2,'c'=2] {'x','yh','yl'}, dimensions={0} | all-to-all | bytes 1310720 | tf_op jit(solution)/shard_map/all_to_all | solution.py:27
  221.3 1.8 collective-permute-start.7
  227.1 8.8 %advance.2 = (f32[8,32,128]{2,1,0:T(8,128)S(1)}, f32[8,32,128]{2,1,0:T(8,128)S(1)}, f32[8,32,128]{2,1,0:T(8,128)S(1)}, f32[32,512]{1,0:T(8,128)S(1)}, f32[32,32,128]{2,1,0:T(8,128)S(1)}) custom-call(f32[32,640]{1,0:T(8,128)S(1)} %pad_maximum_fusion.2.packed_ref, f32[8,32,128]{2,1,0:T(8,128)S(1)} %all_to_all.80.image_ref, ...), custom_call_target="tpu_custom_call" | custom-call | flops 10000000000 | bytes 30000000 | tf_op jit(solution)/shard_map/advance/pallas_call | solution.py:388
  237.7 10.7 %all_to_all.82 = f32[16,32,128]{2,1,0:T(8,128)S(1)} all-to-all(f32[16,32,128]{2,1,0:T(8,128)S(1)} %slice_add_fusion.1), channel_id=1, replica_groups=mesh['x'=4,'z'=8,'yh'=2,'yl'=2,'c'=2] {'x','yh','yl'}, dimensions={0} | all-to-all | bytes 524288 | tf_op jit(solution)/shard_map/all_to_all | solution.py:27
  248.5 10.3 %all_to_all.83.image_ref = f32[8,32,128]{2,1,0:T(8,128)S(1)} all-to-all(f32[8,32,128]{2,1,0:T(8,128)S(1)} %broadcast_in_dim.38), channel_id=1, replica_groups=mesh['x'=4,'z'=8,'yh'=2,'yl'=2,'c'=2] {'z'}, dimensions={0} | all-to-all | bytes 262144 | tf_op jit(solution)/shard_map/all_to_all | solution.py:27
  260.7 3.1 collective-permute-start.9
  264.7 15.3 %all_to_all.84 = f32[16,16,640]{2,1,0:T(8,128)} all-to-all(f32[16,16,640]{2,1,0:T(8,128)S(1)} %broadcast_in_dim.39), channel_id=1, replica_groups=mesh['x'=4,'z'=8,'yh'=2,'yl'=2,'c'=2] {'x','yh','yl'}, dimensions={0} | all-to-all | bytes 1310720 | tf_op jit(solution)/shard_map/all_to_all | solution.py:27
  281.1 2.0 collective-permute-start.10
  288.0 8.8 %advance.3 = (f32[8,32,128]{2,1,0:T(8,128)S(1)}, f32[8,32,128]{2,1,0:T(8,128)S(1)}, f32[8,32,128]{2,1,0:T(8,128)S(1)}, f32[32,512]{1,0:T(8,128)}, f32[32,32,128]{2,1,0:T(8,128)S(1)}) custom-call(f32[32,640]{1,0:T(8,128)S(1)} %pad_maximum_fusion.3.packed_ref, f32[8,32,128]{2,1,0:T(8,128)S(1)} %all_to_all.83.image_ref, ...), custom_call_target="tpu_custom_call" | custom-call | flops 10000000000 | bytes 30000000 | tf_op jit(solution)/shard_map/advance/pallas_call | solution.py:388
  298.5 10.7 %all_to_all.85 = f32[16,32,128]{2,1,0:T(8,128)S(1)} all-to-all(f32[16,32,128]{2,1,0:T(8,128)S(1)} %slice_add_fusion), channel_id=1, replica_groups=mesh['x'=4,'z'=8,'yh'=2,'yl'=2,'c'=2] {'x','yh','yl'}, dimensions={0} | all-to-all | bytes 524288 | tf_op jit(solution)/shard_map/all_to_all | solution.py:27
  310.2 6.9 %all-to-all-start.14 = ((f32[256,1,128]{2,1,0:T(1,128)}), f32[256,1,128]{2,1,0:T(1,128)S(1)}, u32[]{:S(2)}, u32[]{:S(2)}) async-start(f32[256,1,128]{2,1,0:T(1,128)} %broadcast_in_dim.41), calls=%async_computation.14 | async-start | bytes 262144 | tf_op jit(solution)/shard_map/all_to_all | solution.py:27
  317.8 12.3 %all-to-all-done.14 = f32[256,1,128]{2,1,0:T(1,128)S(1)} async-done(((f32[256,1,128]{2,1,0:T(1,128)}), f32[256,1,128]{2,1,0:T(1,128)S(1)}, u32[]{:S(2)}, u32[]{:S(2)}) %all-to-all-start.14) | async-done | bytes 131104 | tf_op jit(solution)/shard_map/all_to_all | solution.py:27
  (135 shorter events, 48.1 us)
Async XLA Ops:
  2.4 4.2 %collective-permute-start = (bf16[256,128]{1,0:T(8,128)(2,1)S(1)}, bf16[256,128]{1,0:T(8,128)(2,1)S(1)}, u32[]{:S(2)}, u32[]{:S(2)}) collective-permute-start(bf16[256,128]{1,0:T(8,128)(2,1)S(1)} %constant_dynamic-slice_fusion.4), channel_id=1, source_target_pairs={{0,1},{1,0},{2,3},{3,2},{4,5},{5,4},{6,7},{7,6},{8,9},{9,8},{10,11... | collective-permute-start | bytes 196616 | tf_op jit(solution)/shard_map/ppermute | solution.py:37
  42.7 5.2 %collective-permute-start.1 = (bf16[16,16,128]{2,1,0:T(8,128)(2,1)S(1)}, bf16[16,16,128]{2,1,0:T(8,128)(2,1)S(1)}, u32[]{:S(2)}, u32[]{:S(2)}) collective-permute-start(bf16[16,16,128]{2,1,0:T(8,128)(2,1)S(1)} %all_to_all.77), channel_id=1, source_target_pairs={{0,1},{1,0},{2,3},{3,2},{4,5},{5,4},{6,7},{7,6},{8,9},{9,8},{10,11... | collective-permute-start | bytes 196616 | tf_op jit(solution)/shard_map/ppermute | solution.py:37
  50.3 28.1 %all-to-all-start.3 = ((bf16[8,224,128]{2,1,0:T(8,128)(2,1)}), bf16[8,224,128]{2,1,0:T(8,128)(2,1)S(1)}, u32[]{:S(2)}, u32[]{:S(2)}) async-start(bf16[8,224,128]{2,1,0:T(8,128)(2,1)} %broadcast_in_dim.30), calls=%async_computation.3 | async-start | bytes 917504 | tf_op jit(solution)/shard_map/all_to_all | solution.py:27
  78.5 1.2 copy-start.5
  90.4 2.4 collective-permute-start.3
  93.9 26.5 %copy-start.27 = (bf16[128,128]{1,0:T(8,128)(2,1)S(1)}, bf16[128,128]{1,0:T(8,128)(2,1)}, u32[]{:S(2)}) copy-start(bf16[128,128]{1,0:T(8,128)(2,1)} %param.3) | copy-start | bytes 98308
  117.4 4.3 %collective-permute-start.4 = (f32[16,48,128]{2,1,0:T(8,128)S(1)}, f32[16,48,128]{2,1,0:T(8,128)S(1)}, u32[]{:S(2)}, u32[]{:S(2)}) collective-permute-start(f32[16,48,128]{2,1,0:T(8,128)S(1)} %all_to_all.79), channel_id=1, source_target_pairs={{0,1},{1,0},{2,3},{3,2},{4,5},{5,4},{6,7},{7,6},{8,9},{9,8},{10,11... | collective-permute-start | bytes 1179656 | tf_op jit(solution)/shard_map/ppermute | solution.py:37
  120.3 1.4 collective-permute-start.2
  123.1 30.0 %all-to-all-start.6 = ((bf16[16,256,128]{2,1,0:T(8,128)(2,1)}), bf16[16,256,128]{2,1,0:T(8,128)(2,1)}, u32[]{:S(2)}, u32[]{:S(2)}) async-start(bf16[16,256,128]{2,1,0:T(8,128)(2,1)} %broadcast_in_dim.32), calls=%async_computation.6 | async-start | bytes 2097152 | tf_op jit(solution)/shard_map/all_to_all | solution.py:27
  153.1 1.2 copy-start.1
  154.3 1.0 copy-start.7
  155.4 1.0 copy-start.11
  156.4 1.0 copy-start.15
  167.1 1.6 collective-permute-start.5
  169.5 14.4 %all-to-all-start.7 = ((f32[16,32,128]{2,1,0:T(8,128)}), f32[16,32,128]{2,1,0:T(8,128)S(1)}, u32[]{:S(2)}, u32[]{:S(2)}) async-start(f32[16,32,128]{2,1,0:T(8,128)} %slice_add_fusion.2), calls=%async_computation.7 | async-start | bytes 524288 | tf_op jit(solution)/shard_map/all_to_all | solution.py:27
  198.6 1.2 copy-start.2
  200.4 23.5 %copy-start.24 = (f32[32,512]{1,0:T(8,128)S(1)}, f32[32,512]{1,0:T(8,128)}, u32[]{:S(2)}) copy-start(f32[32,512]{1,0:T(8,128)} %copy-done.22) | copy-start | bytes 196612
  200.5 4.4 %collective-permute-start.6 = (f32[16,640]{1,0:T(8,128)S(1)}, f32[16,640]{1,0:T(8,128)S(1)}, u32[]{:S(2)}, u32[]{:S(2)}) collective-permute-start(f32[16,640]{1,0:T(8,128)S(1)} %constant_dynamic-slice_fusion.1), channel_id=1, source_target_pairs={{0,1},{1,0},{2,3},{3,2},{4,5},{5,4},{6,7},{7,6},{8,9},{9,8},{10,11... | collective-permute-start | bytes 122888 | tf_op jit(solution)/shard_map/ppermute | solution.py:37
  221.3 2.6 collective-permute-start.7
  224.0 1.0 copy-start.8
  225.0 1.0 copy-start.12
  226.1 1.0 copy-start.16
  235.9 1.7 copy-start.20
  236.0 24.7 %copy-start.25 = (f32[32,512]{1,0:T(8,128)}, f32[32,512]{1,0:T(8,128)S(1)}, u32[]{:S(2)}) copy-start(f32[32,512]{1,0:T(8,128)S(1)} %get-tuple-element.54.proj_ref) | copy-start | bytes 196612
  236.0 1.6 collective-permute-start.8
  258.8 1.2 copy-start.3
  260.7 23.3 %copy-start.21 = (f32[8,32,128]{2,1,0:T(8,128)S(1)}, f32[8,32,128]{2,1,0:T(8,128)}, u32[]{:S(2)}) copy-start(f32[8,32,128]{2,1,0:T(8,128)} %copy-done.20) | copy-start | bytes 393220
  260.7 4.0 %collective-permute-start.9 = (f32[16,640]{1,0:T(8,128)S(1)}, f32[16,640]{1,0:T(8,128)S(1)}, u32[]{:S(2)}, u32[]{:S(2)}) collective-permute-start(f32[16,640]{1,0:T(8,128)S(1)} %constant_dynamic-slice_fusion), channel_id=1, source_target_pairs={{0,1},{1,0},{2,3},{3,2},{4,5},{5,4},{6,7},{7,6},{8,9},{9,8},{10,11... | collective-permute-start | bytes 122888 | tf_op jit(solution)/shard_map/ppermute | solution.py:37
  281.1 2.9 collective-permute-start.10
  284.0 1.0 copy-start.9
  296.9 1.6 collective-permute-start.11
  310.2 19.9 %all-to-all-start.14 = ((f32[256,1,128]{2,1,0:T(1,128)}), f32[256,1,128]{2,1,0:T(1,128)S(1)}, u32[]{:S(2)}, u32[]{:S(2)}) async-start(f32[256,1,128]{2,1,0:T(1,128)} %broadcast_in_dim.41), calls=%async_computation.14 | async-start | bytes 262144 | tf_op jit(solution)/shard_map/all_to_all | solution.py:27
  (12 other events, 10.5 us)

commit v3 on v1

--- a/solution.py
+++ b/solution.py
@@ -208,10 +208,9 @@
     return jnp.concatenate([ref[i] for i in range(ref.shape[0])], axis=1)
 
 
-def pivots_body(picked_ref, inv_ref, right_ref, work_ref):
+def pivots_body(picked_ref, inv_ref, work_ref):
     picked = picked_ref[...]
     right = extended(picked, False)
-    right_ref[...] = right
     work_ref[...] = (
         jnp.exp(dot_nt(extended(picked, True), right)) + unit_matrix(picked.shape[0], JITTER)
     )
@@ -219,12 +218,12 @@
 
 
 def setup_body(
-    inv_ref, right_ref, keys_ref, targets_ref,
+    inv_ref, picked_ref, keys_ref, targets_ref,
     high_ref, mid_ref, low_ref, key_ref, out_ref, pack_ref,
 ):
     piv = inv_ref.shape[0]
     chunks = out_ref.shape[0]
-    right = right_ref[...]
+    right = extended(picked_ref[...], False)
     inverse = inv_ref[...]
     key_ref[...] = extended(keys_ref[...], True)
     wide = dot_nt(jnp.exp(dot_nt(key_ref[...], right)), inverse, HIGHEST)
@@ -283,7 +282,7 @@
     return (residual - stacked_dot(dot_nt, coef, wide)) * (1.0 / NOISE)
 
 
-def gram_body(packed_ref, inv_high, inv_mid, inv_low, proj_ref, work_ref, pack_ref):
+def gram_body(packed_ref, inv_ref, proj_ref, work_ref, pack_ref):
     piv = work_ref.shape[0]
     chunks = packed_ref.shape[0]
     split_by = piv // BLOCK
@@ -304,15 +303,11 @@
                 work_ref[j * BLOCK:(j + 1) * BLOCK, i * BLOCK:(i + 1) * BLOCK] = piece.T
             at += BLOCK
     work_ref[...] = work_ref[...] + unit_matrix(piv, NOISE)
-    inverse = inverse_factor(work_ref)
-    inverse = split(inverse)
-    inv_high[...] = inverse[0]
-    inv_mid[...] = inverse[1]
-    inv_low[...] = inverse[2]
+    inv_ref[...] = inverse_factor(work_ref)
 
 
 def begin_body(
-    proj_ref, inv_high, inv_mid, inv_low, res_ref, high_ref, mid_ref, low_ref, key_ref,
+    proj_ref, inv_ref, res_ref, high_ref, mid_ref, low_ref, key_ref,
     points_ref, dir_ref, row_ref, out_ref,
 ):
     chips = points_ref.shape[0]
@@ -320,7 +315,7 @@
         for k in range(2):
             at = (k * chips + i) * BLOCK
             row_ref[at:at + BLOCK, :] = extended(points_ref[i, k * BLOCK:(k + 1) * BLOCK, :], False)
-    coef = gram_solve(proj_ref[...], (inv_high[...], inv_mid[...], inv_low[...]))
+    coef = gram_solve(proj_ref[...], split(inv_ref[...]))
     direction = next_direction(joined(res_ref), coef, (high_ref[...], mid_ref[...], low_ref[...]))
     for i in range(dir_ref.shape[0]):
         dir_ref[i] = direction[:, i * BLOCK:(i + 1) * BLOCK]
@@ -345,7 +340,7 @@
 
 def advance_body(
     packed_ref, image_ref, res_ref, dir_ref, sol_ref, proj_ref,
-    inv_high, inv_mid, inv_low, high_ref, mid_ref, low_ref, key_ref, row_ref,
+    inv_ref, high_ref, mid_ref, low_ref, key_ref, row_ref,
     new_res, new_dir, new_sol, new_proj, out_ref,
 ):
     piv = proj_ref.shape[1]
@@ -357,7 +352,7 @@
         + alpha * alpha * total[:, piv + 2:piv + 3]
     )
     proj = proj_ref[...] - alpha * total[:, :piv]
-    coef = gram_solve(proj, (inv_high[...], inv_mid[...], inv_low[...]))
+    coef = gram_solve(proj, split(inv_ref[...]))
     inner_next = (squares - jnp.sum(proj * coef, axis=1, keepdims=True)) * (1.0 / NOISE)
     beta = inner_next / inner
     new_proj[...] = proj
@@ -406,12 +401,10 @@
     own_ids = place * own + jnp.arange(own, dtype=jnp.int32)
     owned = (flat_pivots[:, None] == own_ids[None, :]).astype(BF16)
     held = jnp.dot(owned, points, preferred_element_type=F32).astype(BF16)
-    held = half(held, core) + partner(half(held, 1 - core))
-    picked = swap(held.reshape(chips, part, -1), CHIPS)
+    total = u_size * v_size
+    picked = swap(held.reshape(total, piv // total, -1), ALL)
     picked = jnp.sum(picked.astype(F32), axis=0).astype(BF16)
-    picked = jnp.sum(share(picked, U).astype(F32), axis=0).astype(BF16)
-    picked = share(picked, CHIPS)
-    picked = core_first(picked, partner(picked)).reshape(piv, -1)
+    picked = share(picked, ALL).reshape(piv, -1)
 
     both_points = jnp.concatenate([points, partner(points)], axis=0)
     points, targets, picked = lax.optimization_barrier((points, targets, picked))
@@ -419,10 +412,10 @@
     key_points = packed[:, :own].reshape(u_size * own, -1)
     parts = packed[:, own:].astype(F32).reshape(u_size, 3, columns, own)
     residual = parts[:, 0] + parts[:, 1] + parts[:, 2]
-    piv_inverse, piv_right = call(
-        pivots_body, "pivots_factor", [((piv, piv), F32), ((piv, 2 * BLOCK), BF16)],
-        [pltpu.VMEM((piv, piv), F32)], picked, seconds=22e-6,
-    )
+    piv_inverse = call(
+        pivots_body, "pivots_factor", [((piv, piv), F32)], [pltpu.VMEM((piv, piv), F32)], picked,
+        seconds=22e-6,
+    )[0]
 
     keys = key_points.shape[0]
     lower = piv // BLOCK * (piv // BLOCK + 1) // 2 * BLOCK
@@ -432,7 +425,7 @@
         setup_body, "setup_factor",
         [((keys, piv), BF16)] * 3
         + [((keys, 2 * BLOCK), BF16), ((v_size, height, BLOCK), F32)],
-        work[1:], piv_inverse, piv_right, key_points, residual,
+        work[1:], piv_inverse, picked, key_points, residual,
     )
     factor = lax.dynamic_slice_in_dim(wide[0], u_at * own, own, 0)
     packed = jnp.sum(swap(half(packed, core) + partner(half(packed, 1 - core)), CHIPS), axis=0)
@@ -443,13 +436,13 @@
     partial_shape = ((v_size, columns, own), F32)
     both_points, packed = lax.optimization_barrier((both_points, packed))
     row_points = share(both_points, CHIPS)
-    *inverse, projection = call(
-        gram_body, "gram_factor", [((piv, piv), BF16)] * 3 + [((columns, piv), F32)], work, packed,
+    inverse, projection = call(
+        gram_body, "gram_factor", [((piv, piv), F32), ((columns, piv), F32)], work, packed,
         seconds=22e-6,
     )
     direction, row_right, partial = call(
         begin_body, "begin", [state, ((v_size * own, 2 * BLOCK), BF16), partial_shape], [],
-        projection, *inverse, residual, *wide, key_left, row_points,
+        projection, inverse, residual, *wide, key_left, row_points,
     )
     solution_now = jnp.zeros(state[0], F32)
     for step in range(ITERS):
@@ -471,7 +464,7 @@
             advance_body, "advance",
             [state, state, state, ((columns, piv), F32), partial_shape], [],
             packed, image, residual, direction, solution_now, projection,
-            *inverse, *wide, key_left, row_right,
+            inverse, *wide, key_left, row_right,
         )
     solution_own = lax.dynamic_index_in_dim(solution_now, u_at, 0, keepdims=False)
     residual_own = lax.dynamic_index_in_dim(residual, u_at, 0, keepdims=False)

time: 332 us -> 324 us (0.976)
  waiting for transfers between devices: 38.1 us -> 49.4 us
  blocking collectives: 125 us -> 117 us
  local copies, waits for them, and re-layouts: 27.8 us -> 21.3 us
    all_to_all x4 -> x5, waiting for transfers between devices: 19.9 us -> 32.8 us  [swap(): return lax.all_to_all(blocks, axes, 0, 0, tiled=False)]
    all_to_all x11 -> x9, blocking collectives: 125 us -> 117 us  [swap(): return lax.all_to_all(blocks, axes, 0, 0, tiled=False)]
    ppermute x14 -> x12, starting transfers between devices: 26.9 us -> 19.1 us  [other_of_two(): lax.ppermute(values, axis, [(i, (i + 1) % count) for i in range(count)])]
    unnamed x57 -> x29, local copies, waits for them, and re-layouts: 23.3 us -> 16.1 us
    all_to_all x4 -> x5, starting transfers between devices: 22.2 us -> 27.4 us  [swap(): return lax.all_to_all(blocks, axes, 0, 0, tiled=False)]
    ppermute x14 -> x12, waiting for transfers between devices: 18.3 us -> 16.6 us  [other_of_two(): lax.ppermute(values, axis, [(i, (i + 1) % count) for i in range(count)])]
  transfers between devices with their start and end apart: 18 -> 17, of which waited for: 15 -> 14; matrix products, arithmetic and copies ran while one was open for 0% -> 0% of each run, Pallas kernels for 13% -> 13%
where the time goes in v3:
time: 324 us; the launch traced here: 320 us
  blocking collectives  117 us (36%)
  Pallas kernels  78.2 us (24%)
  waiting for transfers between devices  49.4 us (15%)
  starting transfers between devices  46.5 us (14%)
  local copies, waits for them, and re-layouts  21.3 us (7%)
  other arithmetic  4.79 us (1%)
    all_to_all x9, blocking collectives, swap(): return lax.all_to_all(blocks, axes, 0, 0, tiled=False)  117 us
    pallas_call x8, Pallas kernels, call(): pl.pallas_call(body, out_shape=[jax.ShapeDtypeStruct(shape, dtype) for sh...  78.2 us
    all_to_all x5, waiting for transfers between devices, swap(): return lax.all_to_all(blocks, axes, 0, 0, tiled=False)  32.8 us
    all_to_all x5, starting transfers between devices, swap(): return lax.all_to_all(blocks, axes, 0, 0, tiled=False)  27.4 us
    ppermute x12, starting transfers between devices, other_of_two(): lax.ppermute(values, axis, [(i, (i + 1) % count) for i in range(count)])  19.1 us
    ppermute x12, waiting for transfers between devices, other_of_two(): lax.ppermute(values, axis, [(i, (i + 1) % count) for i in range(count)])  16.6 us
    unnamed x29, local copies, waits for them, and re-layouts  16.1 us
  transfers between devices with their start and end apart: 17, of which 14 were waited for; matrix products, arithmetic and copies ran while one was open for 0% of the time, Pallas kernels for 13%

profile of v3, /device:TPU:1, one launch (start us, length us, event | category | flops | bytes accessed | tf_op | source)
XLA Modules:
  0.0 319.6 jit_solution(8834598175444098636)
XLA Ops:
  2.4 28.3 %all_to_all.70 = bf16[256,2,128]{2,1,0:T(2,128)(2,1)S(1)} all-to-all(bf16[256,2,128]{2,1,0:T(2,128)(2,1)S(1)} %bitcast.81), channel_id=1, replica_groups=mesh['x'=4,'z'=8,'yh'=2,'yl'=2,'c'=2] {'x','z','yh','yl','c'}, dimensions={0} | all-to-all | bytes 262144 | tf_op jit(solution)/shard_map/all_to_all | solution.py:27
  31.7 5.5 %all-to-all-start.1 = ((bf16[256,2,128]{2,1,0:T(2,128)(2,1)}), bf16[256,2,128]{2,1,0:T(2,128)(2,1)S(1)}, u32[]{:S(2)}, u32[]{:S(2)}) async-start(bf16[256,2,128]{2,1,0:T(2,128)(2,1)} %broadcast_in_dim.26), calls=%async_computation.1 | async-start | bytes 262144 | tf_op jit(solution)/shard_map/all_to_all | solution.py:27
  37.1 12.9 %all-to-all-done.1 = bf16[256,2,128]{2,1,0:T(2,128)(2,1)S(1)} async-done(((bf16[256,2,128]{2,1,0:T(2,128)(2,1)}), bf16[256,2,128]{2,1,0:T(2,128)(2,1)S(1)}, u32[]{:S(2)}, u32[]{:S(2)}) %all-to-all-start.1) | async-done | bytes 131104 | tf_op jit(solution)/shard_map/all_to_all | solution.py:27
  52.4 3.6 %all-to-all-start.2 = ((bf16[8,224,128]{2,1,0:T(8,128)(2,1)}), bf16[8,224,128]{2,1,0:T(8,128)(2,1)S(1)}, u32[]{:S(2)}, u32[]{:S(2)}) async-start(bf16[8,224,128]{2,1,0:T(8,128)(2,1)} %broadcast_in_dim.27), calls=%async_computation.2 | async-start | bytes 917504 | tf_op jit(solution)/shard_map/all_to_all | solution.py:27
  56.1 21.4 %pivots_factor.1.inv_ref = f32[512,512]{1,0:T(8,128)S(1)} custom-call(bf16[512,128]{1,0:T(8,128)(2,1)S(1)} %bitcast.77), custom_call_target="tpu_custom_call" | custom-call | flops 22000001024 | bytes 66000000 | tf_op jit(solution)/shard_map/pivots_factor/pallas_call | solution.py:374
  79.8 8.0 %setup_factor.1 = (bf16[1024,512]{1,0:T(8,128)(2,1)S(1)}, bf16[1024,512]{1,0:T(8,128)(2,1)S(1)}, bf16[1024,512]{1,0:T(8,128)(2,1)S(1)}, bf16[1024,256]{1,0:T(8,128)(2,1)S(1)}, f32[32,48,128]{2,1,0:T(8,128)S(1)}) custom-call(f32[512,512]{1,0:T(8,128)S(1)} %copy-done.9, bf16[512,128]{1,0:T(8,128)(2,1)S(1)} %bitcast.78, bf16[1024,128]{1,0:T(8,128)(2,1)S(1)} %bitcast.76, ...), custom_call_target="tpu_custom_call" | custom-call | flops 10000000000 | bytes 30000000 | tf_op jit(solution)/shard_map/setup_factor/pallas_call | solution.py:374
  90.8 1.6 collective-permute-done.1
  92.4 12.4 %all_to_all.71 = f32[16,48,128]{2,1,0:T(8,128)S(1)} all-to-all(f32[16,48,128]{2,1,0:T(8,128)S(1)} %dynamic-slice_add_fusion), channel_id=1, replica_groups=mesh['x'=4,'z'=8,'yh'=2,'yl'=2,'c'=2] {'x','yh','yl'}, dimensions={0} | all-to-all | bytes 786432 | tf_op jit(solution)/shard_map/all_to_all | solution.py:27
  104.9 11.2 %all_to_all.72 = f32[16,48,128]{2,1,0:T(8,128)S(1)} all-to-all(f32[16,48,128]{2,1,0:T(8,128)S(1)} %broadcast_in_dim.28), channel_id=1, replica_groups=mesh['x'=4,'z'=8,'yh'=2,'yl'=2,'c'=2] {'x','yh','yl'}, dimensions={0} | all-to-all | bytes 786432 | tf_op jit(solution)/shard_map/all_to_all | solution.py:27
  116.1 3.0 collective-permute-start.2
  119.1 1.5 collective-permute-done
  122.6 4.7 %all-to-all-start.5 = ((bf16[16,256,128]{2,1,0:T(8,128)(2,1)}), bf16[16,256,128]{2,1,0:T(8,128)(2,1)}, u32[]{:S(2)}, u32[]{:S(2)}) async-start(bf16[16,256,128]{2,1,0:T(8,128)(2,1)} %broadcast_in_dim.29), calls=%async_computation.5 | async-start | bytes 2097152 | tf_op jit(solution)/shard_map/all_to_all | solution.py:27
  127.4 21.1 %gram_factor.1 = (f32[512,512]{1,0:T(8,128)S(1)}, f32[32,512]{1,0:T(8,128)S(1)}) custom-call(f32[32,48,128]{2,1,0:T(8,128)S(1)} %pad_maximum_fusion.packed_ref), custom_call_target="tpu_custom_call" | custom-call | flops 22000001024 | bytes 66000000 | tf_op jit(solution)/shard_map/gram_factor/pallas_call | solution.py:374
  153.0 8.8 %begin.1 = (f32[8,32,128]{2,1,0:T(8,128)S(1)}, bf16[4096,256]{1,0:T(8,128)(2,1)}, f32[32,32,128]{2,1,0:T(8,128)S(1)}) custom-call(f32[32,512]{1,0:T(8,128)S(1)} %get-tuple-element.33.proj_ref, f32[512,512]{1,0:T(8,128)S(1)} %copy-done.5, f32[8,32,128]{2,1,0:T(8,128)S(1)} %fusion.2.targets_ref.res_ref, bf16[1024,512]{1,0:T(8,128)(2,1)S(1)} %get-tuple-element.30.high_ref, ...), custom_call_target="tpu_custom_call" | custom-call | flops 10000000000 | bytes 30000000 | tf_op jit(solution)/shard_map/begin/pallas_call | solution.py:374
  164.2 6.7 %all-to-all-start.6 = ((f32[16,32,128]{2,1,0:T(8,128)}), f32[16,32,128]{2,1,0:T(8,128)S(1)}, u32[]{:S(2)}, u32[]{:S(2)}) async-start(f32[16,32,128]{2,1,0:T(8,128)} %slice_add_fusion.2), calls=%async_computation.6 | async-start | bytes 524288 | tf_op jit(solution)/shard_map/all_to_all | solution.py:27
  171.0 7.6 %all-to-all-done.6 = f32[16,32,128]{2,1,0:T(8,128)S(1)} async-done(((f32[16,32,128]{2,1,0:T(8,128)}), f32[16,32,128]{2,1,0:T(8,128)S(1)}, u32[]{:S(2)}, u32[]{:S(2)}) %all-to-all-start.6) | async-done | bytes 262176 | tf_op jit(solution)/shard_map/all_to_all | solution.py:27
  178.6 14.7 %all_to_all.73.image_ref = f32[8,32,128]{2,1,0:T(8,128)S(1)} all-to-all(f32[8,32,128]{2,1,0:T(8,128)S(1)} %broadcast_in_dim.31), channel_id=1, replica_groups=mesh['x'=4,'z'=8,'yh'=2,'yl'=2,'c'=2] {'z'}, dimensions={0} | all-to-all | bytes 262144 | tf_op jit(solution)/shard_map/all_to_all | solution.py:27
  195.1 3.5 %collective-permute-start.4 = (f32[16,640]{1,0:T(8,128)S(1)}, f32[16,640]{1,0:T(8,128)S(1)}, u32[]{:S(2)}, u32[]{:S(2)}) collective-permute-start(f32[16,640]{1,0:T(8,128)S(1)} %constant_dynamic-slice_fusion.1), channel_id=1, source_target_pairs={{0,1},{1,0},{2,3},{3,2},{4,5},{5,4},{6,7},{7,6},{8,9},{9,8},{10,11... | collective-permute-start | bytes 122888 | tf_op jit(solution)/shard_map/ppermute | solution.py:37
  200.7 3.2 collective-permute-done.5
  203.9 9.0 %all_to_all.74 = f32[8,16,640]{2,1,0:T(8,128)S(1)} all-to-all(f32[8,16,640]{2,1,0:T(8,128)S(1)} %broadcast_in_dim.32), channel_id=1, replica_groups=mesh['x'=4,'z'=8,'yh'=2,'yl'=2,'c'=2] {'x','yl'}, dimensions={0} | all-to-all | bytes 655360 | tf_op jit(solution)/shard_map/all_to_all | solution.py:27
  212.9 2.7 collective-permute-start.6
  218.8 8.8 %advance.2 = (f32[8,32,128]{2,1,0:T(8,128)S(1)}, f32[8,32,128]{2,1,0:T(8,128)S(1)}, f32[8,32,128]{2,1,0:T(8,128)S(1)}, f32[32,512]{1,0:T(8,128)S(1)}, f32[32,32,128]{2,1,0:T(8,128)S(1)}) custom-call(f32[32,640]{1,0:T(8,128)S(1)} %pad_maximum_fusion.1.packed_ref, f32[8,32,128]{2,1,0:T(8,128)S(1)} %all_to_all.73.image_ref, ...), custom_call_target="tpu_custom_call" | custom-call | flops 10000000000 | bytes 30000000 | tf_op jit(solution)/shard_map/advance/pallas_call | solution.py:374
  229.4 11.0 %all_to_all.75 = f32[16,32,128]{2,1,0:T(8,128)S(1)} all-to-all(f32[16,32,128]{2,1,0:T(8,128)S(1)} %slice_add_fusion.1), channel_id=1, replica_groups=mesh['x'=4,'z'=8,'yh'=2,'yl'=2,'c'=2] {'x','yh','yl'}, dimensions={0} | all-to-all | bytes 524288 | tf_op jit(solution)/shard_map/all_to_all | solution.py:27
  240.5 10.3 %all_to_all.76.image_ref = f32[8,32,128]{2,1,0:T(8,128)S(1)} all-to-all(f32[8,32,128]{2,1,0:T(8,128)S(1)} %broadcast_in_dim.35), channel_id=1, replica_groups=mesh['x'=4,'z'=8,'yh'=2,'yl'=2,'c'=2] {'z'}, dimensions={0} | all-to-all | bytes 262144 | tf_op jit(solution)/shard_map/all_to_all | solution.py:27
  252.7 3.1 collective-permute-start.8
  257.8 3.2 collective-permute-done.9
  261.0 9.0 %all_to_all.77 = f32[8,16,640]{2,1,0:T(8,128)S(1)} all-to-all(f32[8,16,640]{2,1,0:T(8,128)S(1)} %broadcast_in_dim.36), channel_id=1, replica_groups=mesh['x'=4,'z'=8,'yh'=2,'yl'=2,'c'=2] {'x','yl'}, dimensions={0} | all-to-all | bytes 655360 | tf_op jit(solution)/shard_map/all_to_all | solution.py:27
  270.0 2.9 collective-permute-start.10
  276.2 8.9 %advance.3 = (f32[8,32,128]{2,1,0:T(8,128)S(1)}, f32[8,32,128]{2,1,0:T(8,128)S(1)}, f32[8,32,128]{2,1,0:T(8,128)S(1)}, f32[32,512]{1,0:T(8,128)}, f32[32,32,128]{2,1,0:T(8,128)S(1)}) custom-call(f32[32,640]{1,0:T(8,128)S(1)} %pad_maximum_fusion.2.packed_ref, f32[8,32,128]{2,1,0:T(8,128)S(1)} %all_to_all.76.image_ref, ...), custom_call_target="tpu_custom_call" | custom-call | flops 10000000000 | bytes 30000000 | tf_op jit(solution)/shard_map/advance/pallas_call | solution.py:374
  286.7 11.0 %all_to_all.78 = f32[16,32,128]{2,1,0:T(8,128)S(1)} all-to-all(f32[16,32,128]{2,1,0:T(8,128)S(1)} %slice_add_fusion), channel_id=1, replica_groups=mesh['x'=4,'z'=8,'yh'=2,'yl'=2,'c'=2] {'x','yh','yl'}, dimensions={0} | all-to-all | bytes 524288 | tf_op jit(solution)/shard_map/all_to_all | solution.py:27
  298.7 6.8 %all-to-all-start.13 = ((f32[256,1,128]{2,1,0:T(1,128)}), f32[256,1,128]{2,1,0:T(1,128)S(1)}, u32[]{:S(2)}, u32[]{:S(2)}) async-start(f32[256,1,128]{2,1,0:T(1,128)} %broadcast_in_dim.38), calls=%async_computation.13 | async-start | bytes 262144 | tf_op jit(solution)/shard_map/all_to_all | solution.py:27
  306.2 12.3 %all-to-all-done.13 = f32[256,1,128]{2,1,0:T(1,128)S(1)} async-done(((f32[256,1,128]{2,1,0:T(1,128)}), f32[256,1,128]{2,1,0:T(1,128)S(1)}, u32[]{:S(2)}, u32[]{:S(2)}) %all-to-all-start.13) | async-done | bytes 131104 | tf_op jit(solution)/shard_map/all_to_all | solution.py:27
  (103 shorter events, 39.5 us)
Async XLA Ops:
  31.7 18.4 %all-to-all-start.1 = ((bf16[256,2,128]{2,1,0:T(2,128)(2,1)}), bf16[256,2,128]{2,1,0:T(2,128)(2,1)S(1)}, u32[]{:S(2)}, u32[]{:S(2)}) async-start(bf16[256,2,128]{2,1,0:T(2,128)(2,1)} %broadcast_in_dim.26), calls=%async_computation.1 | async-start | bytes 262144 | tf_op jit(solution)/shard_map/all_to_all | solution.py:27
  52.4 26.0 %all-to-all-start.2 = ((bf16[8,224,128]{2,1,0:T(8,128)(2,1)}), bf16[8,224,128]{2,1,0:T(8,128)(2,1)S(1)}, u32[]{:S(2)}, u32[]{:S(2)}) async-start(bf16[8,224,128]{2,1,0:T(8,128)(2,1)} %broadcast_in_dim.27), calls=%async_computation.2 | async-start | bytes 917504 | tf_op jit(solution)/shard_map/all_to_all | solution.py:27
  77.5 1.0 copy-start.8
  78.6 1.2 copy-start.9
  87.8 1.0 copy-start
  88.8 0.8 copy-start.10
  90.4 2.0 collective-permute-start.1
  116.1 5.2 %collective-permute-start.2 = (f32[16,48,128]{2,1,0:T(8,128)S(1)}, f32[16,48,128]{2,1,0:T(8,128)S(1)}, u32[]{:S(2)}, u32[]{:S(2)}) collective-permute-start(f32[16,48,128]{2,1,0:T(8,128)S(1)} %all_to_all.72), channel_id=1, source_target_pairs={{0,1},{1,0},{2,3},{3,2},{4,5},{5,4},{6,7},{7,6},{8,9},{9,8},{10,11... | collective-permute-start | bytes 1179656 | tf_op jit(solution)/shard_map/ppermute | solution.py:37
  119.1 1.5 collective-permute-start
  122.6 26.9 %all-to-all-start.5 = ((bf16[16,256,128]{2,1,0:T(8,128)(2,1)}), bf16[16,256,128]{2,1,0:T(8,128)(2,1)}, u32[]{:S(2)}, u32[]{:S(2)}) async-start(bf16[16,256,128]{2,1,0:T(8,128)(2,1)} %broadcast_in_dim.29), calls=%async_computation.5 | async-start | bytes 2097152 | tf_op jit(solution)/shard_map/all_to_all | solution.py:27
  148.5 1.0 copy-start.4
  149.5 1.2 copy-start.1
  150.8 1.2 copy-start.5
  152.0 1.0 copy-start.11
  161.8 1.6 collective-permute-start.3
  164.2 14.3 %all-to-all-start.6 = ((f32[16,32,128]{2,1,0:T(8,128)}), f32[16,32,128]{2,1,0:T(8,128)S(1)}, u32[]{:S(2)}, u32[]{:S(2)}) async-start(f32[16,32,128]{2,1,0:T(8,128)} %slice_add_fusion.2), calls=%async_computation.6 | async-start | bytes 524288 | tf_op jit(solution)/shard_map/all_to_all | solution.py:27
  193.3 1.2 copy-start.2
  195.1 4.4 %collective-permute-start.4 = (f32[16,640]{1,0:T(8,128)S(1)}, f32[16,640]{1,0:T(8,128)S(1)}, u32[]{:S(2)}, u32[]{:S(2)}) collective-permute-start(f32[16,640]{1,0:T(8,128)S(1)} %constant_dynamic-slice_fusion.1), channel_id=1, source_target_pairs={{0,1},{1,0},{2,3},{3,2},{4,5},{5,4},{6,7},{7,6},{8,9},{9,8},{10,11... | collective-permute-start | bytes 122888 | tf_op jit(solution)/shard_map/ppermute | solution.py:37
  199.5 4.4 %collective-permute-start.5 = (f32[16,640]{1,0:T(8,128)S(1)}, f32[16,640]{1,0:T(8,128)S(1)}, u32[]{:S(2)}, u32[]{:S(2)}) collective-permute-start(f32[16,640]{1,0:T(8,128)S(1)} %dynamic-slice_add_fusion.2), channel_id=1, source_target_pairs={{0,4},{4,0},{1,5},{5,1},{2,6},{6,2},{3,7},{7,3},{8,12},{12,8},{9,1... | collective-permute-start | bytes 122888 | tf_op jit(solution)/shard_map/ppermute | solution.py:37
  212.9 3.6 %collective-permute-start.6 = (f32[16,640]{1,0:T(8,128)S(1)}, f32[16,640]{1,0:T(8,128)S(1)}, u32[]{:S(2)}, u32[]{:S(2)}) collective-permute-start(f32[16,640]{1,0:T(8,128)S(1)} %reduce_sum.101), channel_id=1, source_target_pairs={{0,1},{1,0},{2,3},{3,2},{4,5},{5,4},{6,7},{7,6},{8,9},{9,8},{10,11... | collective-permute-start | bytes 122888 | tf_op jit(solution)/shard_map/ppermute | solution.py:37
  216.6 1.2 copy-start.6
  217.8 1.0 copy-start.12
  227.7 1.6 collective-permute-start.7
  250.8 1.2 copy-start.3
  252.7 4.0 %collective-permute-start.8 = (f32[16,640]{1,0:T(8,128)S(1)}, f32[16,640]{1,0:T(8,128)S(1)}, u32[]{:S(2)}, u32[]{:S(2)}) collective-permute-start(f32[16,640]{1,0:T(8,128)S(1)} %constant_dynamic-slice_fusion), channel_id=1, source_target_pairs={{0,1},{1,0},{2,3},{3,2},{4,5},{5,4},{6,7},{7,6},{8,9},{9,8},{10,11... | collective-permute-start | bytes 122888 | tf_op jit(solution)/shard_map/ppermute | solution.py:37
  256.7 4.4 %collective-permute-start.9 = (f32[16,640]{1,0:T(8,128)S(1)}, f32[16,640]{1,0:T(8,128)S(1)}, u32[]{:S(2)}, u32[]{:S(2)}) collective-permute-start(f32[16,640]{1,0:T(8,128)S(1)} %dynamic-slice_add_fusion.1), channel_id=1, source_target_pairs={{0,4},{4,0},{1,5},{5,1},{2,6},{6,2},{3,7},{7,3},{8,12},{12,8},{9,1... | collective-permute-start | bytes 122888 | tf_op jit(solution)/shard_map/ppermute | solution.py:37
  270.0 3.8 %collective-permute-start.10 = (f32[16,640]{1,0:T(8,128)S(1)}, f32[16,640]{1,0:T(8,128)S(1)}, u32[]{:S(2)}, u32[]{:S(2)}) collective-permute-start(f32[16,640]{1,0:T(8,128)S(1)} %reduce_sum.104), channel_id=1, source_target_pairs={{0,1},{1,0},{2,3},{3,2},{4,5},{5,4},{6,7},{7,6},{8,9},{9,8},{10,11... | collective-permute-start | bytes 122888 | tf_op jit(solution)/shard_map/ppermute | solution.py:37
  273.9 1.2 copy-start.7
  275.1 1.0 copy-start.13
  285.0 1.6 collective-permute-start.11
  298.7 19.8 %all-to-all-start.13 = ((f32[256,1,128]{2,1,0:T(1,128)}), f32[256,1,128]{2,1,0:T(1,128)S(1)}, u32[]{:S(2)}, u32[]{:S(2)}) async-start(f32[256,1,128]{2,1,0:T(1,128)} %broadcast_in_dim.38), calls=%async_computation.13 | async-start | bytes 262144 | tf_op jit(solution)/shard_map/all_to_all | solution.py:27

commit v4 on v3

--- a/solution.py
+++ b/solution.py
@@ -401,13 +401,17 @@
     own_ids = place * own + jnp.arange(own, dtype=jnp.int32)
     owned = (flat_pivots[:, None] == own_ids[None, :]).astype(BF16)
     held = jnp.dot(owned, points, preferred_element_type=F32).astype(BF16)
-    total = u_size * v_size
-    picked = swap(held.reshape(total, piv // total, -1), ALL)
+    held = half(held, core) + partner(half(held, 1 - core))
+    picked = swap(held.reshape(chips, part, -1), CHIPS)
     picked = jnp.sum(picked.astype(F32), axis=0).astype(BF16)
-    picked = share(picked, ALL).reshape(piv, -1)
+    picked = jnp.sum(share(picked, U).astype(F32), axis=0).astype(BF16)
+    picked = share(picked, CHIPS)
+    picked = core_first(picked, partner(picked)).reshape(piv, -1)
 
     both_points = jnp.concatenate([points, partner(points)], axis=0)
-    points, targets, picked = lax.optimization_barrier((points, targets, picked))
+    points, targets, picked, both_points = lax.optimization_barrier(
+        (points, targets, picked, both_points)
+    )
     packed = share(jnp.concatenate([points] + three_parts(targets.T), axis=0), U)
     key_points = packed[:, :own].reshape(u_size * own, -1)
     parts = packed[:, own:].astype(F32).reshape(u_size, 3, columns, own)

time: 324 us -> 322 us (level)
  starting transfers between devices: 46.5 us -> 55.4 us
  waiting for transfers between devices: 49.4 us -> 40.6 us
    ppermute x12 -> x14, starting transfers between devices: 19.1 us -> 29.6 us  [other_of_two(): lax.ppermute(values, axis, [(i, (i + 1) % count) for i in range(count)])]
    all_to_all x5, waiting for transfers between devices: 32.8 us -> 23 us  [swap(): return lax.all_to_all(blocks, axes, 0, 0, tiled=False)]
    all_to_all x9 -> x10, blocking collectives: 117 us -> 115 us  [swap(): return lax.all_to_all(blocks, axes, 0, 0, tiled=False)]
    ppermute x12 -> x14, waiting for transfers between devices: 16.6 us -> 17.5 us  [other_of_two(): lax.ppermute(values, axis, [(i, (i + 1) % count) for i in range(count)])]
    unnamed x29 -> x31, local copies, waits for them, and re-layouts: 16.1 us -> 16.1 us
  transfers between devices with their start and end apart: 17 -> 19, of which waited for: 14 -> 15; matrix products, arithmetic and copies ran while one was open for 0% -> 1% of each run, Pallas kernels for 13% -> 13%
where the time goes in v4:
time: 322 us; the launch traced here: 318 us
  blocking collectives  115 us (36%)
  Pallas kernels  78.2 us (24%)
  starting transfers between devices  55.4 us (17%)
  waiting for transfers between devices  40.6 us (13%)
  local copies, waits for them, and re-layouts  21.2 us (7%)
  other arithmetic  5.22 us (2%)
    all_to_all x10, blocking collectives, swap(): return lax.all_to_all(blocks, axes, 0, 0, tiled=False)  115 us
    pallas_call x8, Pallas kernels, call(): pl.pallas_call(body, out_shape=[jax.ShapeDtypeStruct(shape, dtype) for sh...  78.2 us
    ppermute x14, starting transfers between devices, other_of_two(): lax.ppermute(values, axis, [(i, (i + 1) % count) for i in range(count)])  29.6 us
    all_to_all x5, starting transfers between devices, swap(): return lax.all_to_all(blocks, axes, 0, 0, tiled=False)  25.8 us
    all_to_all x5, waiting for transfers between devices, swap(): return lax.all_to_all(blocks, axes, 0, 0, tiled=False)  23 us
    ppermute x14, waiting for transfers between devices, other_of_two(): lax.ppermute(values, axis, [(i, (i + 1) % count) for i in range(count)])  17.5 us
    unnamed x31, local copies, waits for them, and re-layouts  16.1 us
  transfers between devices with their start and end apart: 19, of which 15 were waited for; matrix products, arithmetic and copies ran while one was open for 1% of the time, Pallas kernels for 13%

profile of v4, /device:TPU:1, one launch (start us, length us, event | category | flops | bytes accessed | tf_op | source)
XLA Modules:
  0.0 317.7 jit_solution(13834797548856900165)
XLA Ops:
  2.4 3.3 %collective-permute-start = (bf16[256,128]{1,0:T(8,128)(2,1)S(1)}, bf16[256,128]{1,0:T(8,128)(2,1)S(1)}, u32[]{:S(2)}, u32[]{:S(2)}) collective-permute-start(bf16[256,128]{1,0:T(8,128)(2,1)S(1)} %constant_dynamic-slice_fusion.4), channel_id=1, source_target_pairs={{0,1},{1,0},{2,3},{3,2},{4,5},{5,4},{6,7},{7,6},{8,9},{9,8},{10,11... | collective-permute-start | bytes 196616 | tf_op jit(solution)/shard_map/ppermute | solution.py:37
  6.6 11.3 %all_to_all.75 = bf16[16,16,128]{2,1,0:T(8,128)(2,1)S(1)} all-to-all(bf16[16,16,128]{2,1,0:T(8,128)(2,1)S(1)} %bitcast.81), channel_id=1, replica_groups=mesh['x'=4,'z'=8,'yh'=2,'yl'=2,'c'=2] {'x','yh','yl'}, dimensions={0} | all-to-all | bytes 131072 | tf_op jit(solution)/shard_map/all_to_all | solution.py:27
  18.0 14.9 %all_to_all.76 = bf16[8,16,128]{2,1,0:T(8,128)(2,1)S(1)} all-to-all(bf16[8,16,128]{2,1,0:T(8,128)(2,1)S(1)} %broadcast_in_dim.28), channel_id=1, replica_groups=mesh['x'=4,'z'=8,'yh'=2,'yl'=2,'c'=2] {'z'}, dimensions={0} | all-to-all | bytes 65536 | tf_op jit(solution)/shard_map/all_to_all | solution.py:27
  33.5 3.5 %all-to-all-start.2 = ((bf16[16,16,128]{2,1,0:T(8,128)(2,1)}), bf16[16,16,128]{2,1,0:T(8,128)(2,1)S(1)}, u32[]{:S(2)}, u32[]{:S(2)}) async-start(bf16[16,16,128]{2,1,0:T(8,128)(2,1)} %broadcast_in_dim.29), calls=%async_computation.2 | async-start | bytes 131072 | tf_op jit(solution)/shard_map/all_to_all | solution.py:27
  37.0 3.3 %collective-permute-start.2 = (bf16[128,128]{1,0:T(8,128)(2,1)}, bf16[128,128]{1,0:T(8,128)(2,1)S(1)}, u32[]{:S(2)}, u32[]{:S(2)}) collective-permute-start(bf16[128,128]{1,0:T(8,128)(2,1)} %param.3), channel_id=1, source_target_pairs={{0,1},{1,0},{2,3},{3,2},{4,5},{5,4},{6,7},{7,6},{8,9},{9,8},{10,11... | collective-permute-start | bytes 98312 | tf_op jit(solution)/shard_map/ppermute | solution.py:37
  40.3 3.2 all-to-all-done.2
  43.5 4.4 %collective-permute-start.1 = (bf16[16,16,128]{2,1,0:T(8,128)(2,1)S(1)}, bf16[16,16,128]{2,1,0:T(8,128)(2,1)S(1)}, u32[]{:S(2)}, u32[]{:S(2)}) collective-permute-start(bf16[16,16,128]{2,1,0:T(8,128)(2,1)S(1)} %all-to-all-done.2), channel_id=1, source_target_pairs={{0,1},{1,0},{2,3},{3,2},{4,5},{5,4},{6,7},{7,6},{8,9},{9,8},{10,11... | collective-permute-start | bytes 196616 | tf_op jit(solution)/shard_map/ppermute | solution.py:37
  51.7 3.6 %all-to-all-start.3 = ((bf16[8,224,128]{2,1,0:T(8,128)(2,1)}), bf16[8,224,128]{2,1,0:T(8,128)(2,1)S(1)}, u32[]{:S(2)}, u32[]{:S(2)}) async-start(bf16[8,224,128]{2,1,0:T(8,128)(2,1)} %broadcast_in_dim.30), calls=%async_computation.3 | async-start | bytes 917504 | tf_op jit(solution)/shard_map/all_to_all | solution.py:27
  55.3 21.4 %pivots_factor.1.inv_ref = f32[512,512]{1,0:T(8,128)S(1)} custom-call(bf16[512,128]{1,0:T(8,128)(2,1)S(1)} %bitcast.77), custom_call_target="tpu_custom_call" | custom-call | flops 22000001024 | bytes 66000000 | tf_op jit(solution)/shard_map/pivots_factor/pallas_call | solution.py:374
  79.0 8.0 %setup_factor.1 = (bf16[1024,512]{1,0:T(8,128)(2,1)S(1)}, bf16[1024,512]{1,0:T(8,128)(2,1)S(1)}, bf16[1024,512]{1,0:T(8,128)(2,1)S(1)}, bf16[1024,256]{1,0:T(8,128)(2,1)S(1)}, f32[32,48,128]{2,1,0:T(8,128)S(1)}) custom-call(f32[512,512]{1,0:T(8,128)S(1)} %copy-done.9, bf16[512,128]{1,0:T(8,128)(2,1)S(1)} %bitcast.78, bf16[1024,128]{1,0:T(8,128)(2,1)S(1)} %bitcast.76, ...), custom_call_target="tpu_custom_call" | custom-call | flops 10000000000 | bytes 30000000 | tf_op jit(solution)/shard_map/setup_factor/pallas_call | solution.py:374
  91.6 12.3 %all_to_all.77 = f32[16,48,128]{2,1,0:T(8,128)S(1)} all-to-all(f32[16,48,128]{2,1,0:T(8,128)S(1)} %dynamic-slice_add_fusion), channel_id=1, replica_groups=mesh['x'=4,'z'=8,'yh'=2,'yl'=2,'c'=2] {'x','yh','yl'}, dimensions={0} | all-to-all | bytes 786432 | tf_op jit(solution)/shard_map/all_to_all | solution.py:27
  103.9 11.6 %all_to_all.78 = f32[16,48,128]{2,1,0:T(8,128)S(1)} all-to-all(f32[16,48,128]{2,1,0:T(8,128)S(1)} %broadcast_in_dim.31), channel_id=1, replica_groups=mesh['x'=4,'z'=8,'yh'=2,'yl'=2,'c'=2] {'x','yh','yl'}, dimensions={0} | all-to-all | bytes 786432 | tf_op jit(solution)/shard_map/all_to_all | solution.py:27
  120.8 4.8 %all-to-all-start.6 = ((bf16[16,256,128]{2,1,0:T(8,128)(2,1)}), bf16[16,256,128]{2,1,0:T(8,128)(2,1)}, u32[]{:S(2)}, u32[]{:S(2)}) async-start(bf16[16,256,128]{2,1,0:T(8,128)(2,1)} %broadcast_in_dim.32), calls=%async_computation.6 | async-start | bytes 2097152 | tf_op jit(solution)/shard_map/all_to_all | solution.py:27
  125.6 21.1 %gram_factor.1 = (f32[512,512]{1,0:T(8,128)S(1)}, f32[32,512]{1,0:T(8,128)S(1)}) custom-call(f32[32,48,128]{2,1,0:T(8,128)S(1)} %pad_maximum_fusion.packed_ref), custom_call_target="tpu_custom_call" | custom-call | flops 22000001024 | bytes 66000000 | tf_op jit(solution)/shard_map/gram_factor/pallas_call | solution.py:374
  151.2 8.8 %begin.1 = (f32[8,32,128]{2,1,0:T(8,128)S(1)}, bf16[4096,256]{1,0:T(8,128)(2,1)}, f32[32,32,128]{2,1,0:T(8,128)S(1)}) custom-call(f32[32,512]{1,0:T(8,128)S(1)} %get-tuple-element.35.proj_ref, f32[512,512]{1,0:T(8,128)S(1)} %copy-done.5, f32[8,32,128]{2,1,0:T(8,128)S(1)} %fusion.2.targets_ref.res_ref, bf16[1024,512]{1,0:T(8,128)(2,1)S(1)} %get-tuple-element.31.high_ref, ...), custom_call_target="tpu_custom_call" | custom-call | flops 10000000000 | bytes 30000000 | tf_op jit(solution)/shard_map/begin/pallas_call | solution.py:374
  162.4 7.0 %all-to-all-start.7 = ((f32[16,32,128]{2,1,0:T(8,128)}), f32[16,32,128]{2,1,0:T(8,128)S(1)}, u32[]{:S(2)}, u32[]{:S(2)}) async-start(f32[16,32,128]{2,1,0:T(8,128)} %slice_add_fusion.2), calls=%async_computation.7 | async-start | bytes 524288 | tf_op jit(solution)/shard_map/all_to_all | solution.py:27
  169.4 7.6 %all-to-all-done.7 = f32[16,32,128]{2,1,0:T(8,128)S(1)} async-done(((f32[16,32,128]{2,1,0:T(8,128)}), f32[16,32,128]{2,1,0:T(8,128)S(1)}, u32[]{:S(2)}, u32[]{:S(2)}) %all-to-all-start.7) | async-done | bytes 262176 | tf_op jit(solution)/shard_map/all_to_all | solution.py:27
  177.0 14.3 %all_to_all.79.image_ref = f32[8,32,128]{2,1,0:T(8,128)S(1)} all-to-all(f32[8,32,128]{2,1,0:T(8,128)S(1)} %broadcast_in_dim.34), channel_id=1, replica_groups=mesh['x'=4,'z'=8,'yh'=2,'yl'=2,'c'=2] {'z'}, dimensions={0} | all-to-all | bytes 262144 | tf_op jit(solution)/shard_map/all_to_all | solution.py:27
  193.2 3.5 %collective-permute-start.6 = (f32[16,640]{1,0:T(8,128)S(1)}, f32[16,640]{1,0:T(8,128)S(1)}, u32[]{:S(2)}, u32[]{:S(2)}) collective-permute-start(f32[16,640]{1,0:T(8,128)S(1)} %constant_dynamic-slice_fusion.1), channel_id=1, source_target_pairs={{0,1},{1,0},{2,3},{3,2},{4,5},{5,4},{6,7},{7,6},{8,9},{9,8},{10,11... | collective-permute-start | bytes 122888 | tf_op jit(solution)/shard_map/ppermute | solution.py:37
  198.7 3.2 collective-permute-done.7
  201.9 9.0 %all_to_all.80 = f32[8,16,640]{2,1,0:T(8,128)S(1)} all-to-all(f32[8,16,640]{2,1,0:T(8,128)S(1)} %broadcast_in_dim.35), channel_id=1, replica_groups=mesh['x'=4,'z'=8,'yh'=2,'yl'=2,'c'=2] {'x','yl'}, dimensions={0} | all-to-all | bytes 655360 | tf_op jit(solution)/shard_map/all_to_all | solution.py:27
  216.9 8.8 %advance.2 = (f32[8,32,128]{2,1,0:T(8,128)S(1)}, f32[8,32,128]{2,1,0:T(8,128)S(1)}, f32[8,32,128]{2,1,0:T(8,128)S(1)}, f32[32,512]{1,0:T(8,128)S(1)}, f32[32,32,128]{2,1,0:T(8,128)S(1)}) custom-call(f32[32,640]{1,0:T(8,128)S(1)} %pad_maximum_fusion.2.packed_ref, f32[8,32,128]{2,1,0:T(8,128)S(1)} %all_to_all.79.image_ref, ...), custom_call_target="tpu_custom_call" | custom-call | flops 10000000000 | bytes 30000000 | tf_op jit(solution)/shard_map/advance/pallas_call | solution.py:374
  227.4 11.1 %all_to_all.81 = f32[16,32,128]{2,1,0:T(8,128)S(1)} all-to-all(f32[16,32,128]{2,1,0:T(8,128)S(1)} %slice_add_fusion.1), channel_id=1, replica_groups=mesh['x'=4,'z'=8,'yh'=2,'yl'=2,'c'=2] {'x','yh','yl'}, dimensions={0} | all-to-all | bytes 524288 | tf_op jit(solution)/shard_map/all_to_all | solution.py:27
  238.5 10.3 %all_to_all.82.image_ref = f32[8,32,128]{2,1,0:T(8,128)S(1)} all-to-all(f32[8,32,128]{2,1,0:T(8,128)S(1)} %broadcast_in_dim.38), channel_id=1, replica_groups=mesh['x'=4,'z'=8,'yh'=2,'yl'=2,'c'=2] {'z'}, dimensions={0} | all-to-all | bytes 262144 | tf_op jit(solution)/shard_map/all_to_all | solution.py:27
  250.7 3.1 collective-permute-start.10
  255.9 3.2 collective-permute-done.11
  259.1 9.0 %all_to_all.83 = f32[8,16,640]{2,1,0:T(8,128)S(1)} all-to-all(f32[8,16,640]{2,1,0:T(8,128)S(1)} %broadcast_in_dim.39), channel_id=1, replica_groups=mesh['x'=4,'z'=8,'yh'=2,'yl'=2,'c'=2] {'x','yl'}, dimensions={0} | all-to-all | bytes 655360 | tf_op jit(solution)/shard_map/all_to_all | solution.py:27
  268.1 2.9 collective-permute-start.12
  274.2 8.9 %advance.3 = (f32[8,32,128]{2,1,0:T(8,128)S(1)}, f32[8,32,128]{2,1,0:T(8,128)S(1)}, f32[8,32,128]{2,1,0:T(8,128)S(1)}, f32[32,512]{1,0:T(8,128)}, f32[32,32,128]{2,1,0:T(8,128)S(1)}) custom-call(f32[32,640]{1,0:T(8,128)S(1)} %pad_maximum_fusion.3.packed_ref, f32[8,32,128]{2,1,0:T(8,128)S(1)} %all_to_all.82.image_ref, ...), custom_call_target="tpu_custom_call" | custom-call | flops 10000000000 | bytes 30000000 | tf_op jit(solution)/shard_map/advance/pallas_call | solution.py:374
  284.7 11.0 %all_to_all.84 = f32[16,32,128]{2,1,0:T(8,128)S(1)} all-to-all(f32[16,32,128]{2,1,0:T(8,128)S(1)} %slice_add_fusion), channel_id=1, replica_groups=mesh['x'=4,'z'=8,'yh'=2,'yl'=2,'c'=2] {'x','yh','yl'}, dimensions={0} | all-to-all | bytes 524288 | tf_op jit(solution)/shard_map/all_to_all | solution.py:27
  296.8 6.9 %all-to-all-start.14 = ((f32[256,1,128]{2,1,0:T(1,128)}), f32[256,1,128]{2,1,0:T(1,128)S(1)}, u32[]{:S(2)}, u32[]{:S(2)}) async-start(f32[256,1,128]{2,1,0:T(1,128)} %broadcast_in_dim.41), calls=%async_computation.14 | async-start | bytes 262144 | tf_op jit(solution)/shard_map/all_to_all | solution.py:27
  304.4 12.3 %all-to-all-done.14 = f32[256,1,128]{2,1,0:T(1,128)S(1)} async-done(((f32[256,1,128]{2,1,0:T(1,128)}), f32[256,1,128]{2,1,0:T(1,128)S(1)}, u32[]{:S(2)}, u32[]{:S(2)}) %all-to-all-start.14) | async-done | bytes 131104 | tf_op jit(solution)/shard_map/all_to_all | solution.py:27
  (116 shorter events, 49.0 us)
Async XLA Ops:
  2.4 4.2 %collective-permute-start = (bf16[256,128]{1,0:T(8,128)(2,1)S(1)}, bf16[256,128]{1,0:T(8,128)(2,1)S(1)}, u32[]{:S(2)}, u32[]{:S(2)}) collective-permute-start(bf16[256,128]{1,0:T(8,128)(2,1)S(1)} %constant_dynamic-slice_fusion.4), channel_id=1, source_target_pairs={{0,1},{1,0},{2,3},{3,2},{4,5},{5,4},{6,7},{7,6},{8,9},{9,8},{10,11... | collective-permute-start | bytes 196616 | tf_op jit(solution)/shard_map/ppermute | solution.py:37
  33.5 10.0 %all-to-all-start.2 = ((bf16[16,16,128]{2,1,0:T(8,128)(2,1)}), bf16[16,16,128]{2,1,0:T(8,128)(2,1)S(1)}, u32[]{:S(2)}, u32[]{:S(2)}) async-start(bf16[16,16,128]{2,1,0:T(8,128)(2,1)} %broadcast_in_dim.29), calls=%async_computation.2 | async-start | bytes 131072 | tf_op jit(solution)/shard_map/all_to_all | solution.py:27
  37.0 10.8 %collective-permute-start.2 = (bf16[128,128]{1,0:T(8,128)(2,1)}, bf16[128,128]{1,0:T(8,128)(2,1)S(1)}, u32[]{:S(2)}, u32[]{:S(2)}) collective-permute-start(bf16[128,128]{1,0:T(8,128)(2,1)} %param.3), channel_id=1, source_target_pairs={{0,1},{1,0},{2,3},{3,2},{4,5},{5,4},{6,7},{7,6},{8,9},{9,8},{10,11... | collective-permute-start | bytes 98312 | tf_op jit(solution)/shard_map/ppermute | solution.py:37
  43.5 5.8 %collective-permute-start.1 = (bf16[16,16,128]{2,1,0:T(8,128)(2,1)S(1)}, bf16[16,16,128]{2,1,0:T(8,128)(2,1)S(1)}, u32[]{:S(2)}, u32[]{:S(2)}) collective-permute-start(bf16[16,16,128]{2,1,0:T(8,128)(2,1)S(1)} %all-to-all-done.2), channel_id=1, source_target_pairs={{0,1},{1,0},{2,3},{3,2},{4,5},{5,4},{6,7},{7,6},{8,9},{9,8},{10,11... | collective-permute-start | bytes 196616 | tf_op jit(solution)/shard_map/ppermute | solution.py:37
  51.7 26.0 %all-to-all-start.3 = ((bf16[8,224,128]{2,1,0:T(8,128)(2,1)}), bf16[8,224,128]{2,1,0:T(8,128)(2,1)S(1)}, u32[]{:S(2)}, u32[]{:S(2)}) async-start(bf16[8,224,128]{2,1,0:T(8,128)(2,1)} %broadcast_in_dim.30), calls=%async_computation.3 | async-start | bytes 917504 | tf_op jit(solution)/shard_map/all_to_all | solution.py:27
  76.7 1.0 copy-start.8
  77.8 1.2 copy-start.9
  89.6 1.9 collective-permute-start.3
  103.9 15.7 %copy-start.14 = (bf16[256,128]{1,0:T(8,128)(2,1)S(1)}, bf16[256,128]{1,0:T(8,128)(2,1)}, u32[]{:S(2)}) copy-start(bf16[256,128]{1,0:T(8,128)(2,1)} %pad_maximum_fusion.4) | copy-start | bytes 196612
  115.5 4.0 %collective-permute-start.4 = (f32[16,48,128]{2,1,0:T(8,128)S(1)}, f32[16,48,128]{2,1,0:T(8,128)S(1)}, u32[]{:S(2)}, u32[]{:S(2)}) collective-permute-start(f32[16,48,128]{2,1,0:T(8,128)S(1)} %all_to_all.78), channel_id=1, source_target_pairs={{0,1},{1,0},{2,3},{3,2},{4,5},{5,4},{6,7},{7,6},{8,9},{9,8},{10,11... | collective-permute-start | bytes 1179656 | tf_op jit(solution)/shard_map/ppermute | solution.py:37
  120.8 26.9 %all-to-all-start.6 = ((bf16[16,256,128]{2,1,0:T(8,128)(2,1)}), bf16[16,256,128]{2,1,0:T(8,128)(2,1)}, u32[]{:S(2)}, u32[]{:S(2)}) async-start(bf16[16,256,128]{2,1,0:T(8,128)(2,1)} %broadcast_in_dim.32), calls=%async_computation.6 | async-start | bytes 2097152 | tf_op jit(solution)/shard_map/all_to_all | solution.py:27
  146.7 1.0 copy-start.4
  147.7 1.2 copy-start.1
  149.0 1.2 copy-start.5
  150.2 1.0 copy-start.11
  160.0 1.6 collective-permute-start.5
  162.4 14.5 %all-to-all-start.7 = ((f32[16,32,128]{2,1,0:T(8,128)}), f32[16,32,128]{2,1,0:T(8,128)S(1)}, u32[]{:S(2)}, u32[]{:S(2)}) async-start(f32[16,32,128]{2,1,0:T(8,128)} %slice_add_fusion.2), calls=%async_computation.7 | async-start | bytes 524288 | tf_op jit(solution)/shard_map/all_to_all | solution.py:27
  191.3 1.2 copy-start.2
  193.2 4.4 %collective-permute-start.6 = (f32[16,640]{1,0:T(8,128)S(1)}, f32[16,640]{1,0:T(8,128)S(1)}, u32[]{:S(2)}, u32[]{:S(2)}) collective-permute-start(f32[16,640]{1,0:T(8,128)S(1)} %constant_dynamic-slice_fusion.1), channel_id=1, source_target_pairs={{0,1},{1,0},{2,3},{3,2},{4,5},{5,4},{6,7},{7,6},{8,9},{9,8},{10,11... | collective-permute-start | bytes 122888 | tf_op jit(solution)/shard_map/ppermute | solution.py:37
  197.5 4.4 %collective-permute-start.7 = (f32[16,640]{1,0:T(8,128)S(1)}, f32[16,640]{1,0:T(8,128)S(1)}, u32[]{:S(2)}, u32[]{:S(2)}) collective-permute-start(f32[16,640]{1,0:T(8,128)S(1)} %dynamic-slice_add_fusion.3), channel_id=1, source_target_pairs={{0,4},{4,0},{1,5},{5,1},{2,6},{6,2},{3,7},{7,3},{8,12},{12,8},{9,1... | collective-permute-start | bytes 122888 | tf_op jit(solution)/shard_map/ppermute | solution.py:37
  210.9 3.6 %collective-permute-start.8 = (f32[16,640]{1,0:T(8,128)S(1)}, f32[16,640]{1,0:T(8,128)S(1)}, u32[]{:S(2)}, u32[]{:S(2)}) collective-permute-start(f32[16,640]{1,0:T(8,128)S(1)} %reduce_sum.114), channel_id=1, source_target_pairs={{0,1},{1,0},{2,3},{3,2},{4,5},{5,4},{6,7},{7,6},{8,9},{9,8},{10,11... | collective-permute-start | bytes 122888 | tf_op jit(solution)/shard_map/ppermute | solution.py:37
  214.6 1.2 copy-start.6
  215.8 1.0 copy-start.12
  225.7 1.6 collective-permute-start.9
  248.9 1.2 copy-start.3
  250.7 4.0 %collective-permute-start.10 = (f32[16,640]{1,0:T(8,128)S(1)}, f32[16,640]{1,0:T(8,128)S(1)}, u32[]{:S(2)}, u32[]{:S(2)}) collective-permute-start(f32[16,640]{1,0:T(8,128)S(1)} %constant_dynamic-slice_fusion), channel_id=1, source_target_pairs={{0,1},{1,0},{2,3},{3,2},{4,5},{5,4},{6,7},{7,6},{8,9},{9,8},{10,11... | collective-permute-start | bytes 122888 | tf_op jit(solution)/shard_map/ppermute | solution.py:37
  254.7 4.4 %collective-permute-start.11 = (f32[16,640]{1,0:T(8,128)S(1)}, f32[16,640]{1,0:T(8,128)S(1)}, u32[]{:S(2)}, u32[]{:S(2)}) collective-permute-start(f32[16,640]{1,0:T(8,128)S(1)} %dynamic-slice_add_fusion.2), channel_id=1, source_target_pairs={{0,4},{4,0},{1,5},{5,1},{2,6},{6,2},{3,7},{7,3},{8,12},{12,8},{9,1... | collective-permute-start | bytes 122888 | tf_op jit(solution)/shard_map/ppermute | solution.py:37
  268.1 3.8 %collective-permute-start.12 = (f32[16,640]{1,0:T(8,128)S(1)}, f32[16,640]{1,0:T(8,128)S(1)}, u32[]{:S(2)}, u32[]{:S(2)}) collective-permute-start(f32[16,640]{1,0:T(8,128)S(1)} %reduce_sum.117), channel_id=1, source_target_pairs={{0,1},{1,0},{2,3},{3,2},{4,5},{5,4},{6,7},{7,6},{8,9},{9,8},{10,11... | collective-permute-start | bytes 122888 | tf_op jit(solution)/shard_map/ppermute | solution.py:37
  271.9 1.2 copy-start.7
  273.2 1.0 copy-start.13
  283.1 1.6 collective-permute-start.13
  296.8 19.9 %all-to-all-start.14 = ((f32[256,1,128]{2,1,0:T(1,128)}), f32[256,1,128]{2,1,0:T(1,128)S(1)}, u32[]{:S(2)}, u32[]{:S(2)}) async-start(f32[256,1,128]{2,1,0:T(1,128)} %broadcast_in_dim.41), calls=%async_computation.14 | async-start | bytes 262144 | tf_op jit(solution)/shard_map/all_to_all | solution.py:27
  (2 other events, 1.8 us)

commit v5 on v4

--- a/solution.py
+++ b/solution.py
@@ -409,10 +409,11 @@
     picked = core_first(picked, partner(picked)).reshape(piv, -1)
 
     both_points = jnp.concatenate([points, partner(points)], axis=0)
-    points, targets, picked, both_points = lax.optimization_barrier(
-        (points, targets, picked, both_points)
-    )
-    packed = share(jnp.concatenate([points] + three_parts(targets.T), axis=0), U)
+    both_points = jnp.broadcast_to(both_points[None], (chips,) + both_points.shape)
+    packed = jnp.concatenate([points] + three_parts(targets.T), axis=0)
+    packed = jnp.broadcast_to(packed[None], (u_size,) + packed.shape)
+    picked, packed, both_points = lax.optimization_barrier((picked, packed, both_points))
+    packed = swap(packed, U)
     key_points = packed[:, :own].reshape(u_size * own, -1)
     parts = packed[:, own:].astype(F32).reshape(u_size, 3, columns, own)
     residual = parts[:, 0] + parts[:, 1] + parts[:, 2]
@@ -439,7 +440,7 @@
     state = ((u_size, columns, own), F32)
     partial_shape = ((v_size, columns, own), F32)
     both_points, packed = lax.optimization_barrier((both_points, packed))
-    row_points = share(both_points, CHIPS)
+    row_points = swap(both_points, CHIPS)
     inverse, projection = call(
         gram_body, "gram_factor", [((piv, piv), F32), ((columns, piv), F32)], work, packed,
         seconds=22e-6,

time: 322 us -> 322 us (level)
  blocking collectives: 115 us -> 88.6 us
  waiting for transfers between devices: 40.6 us -> 54.8 us
  starting transfers between devices: 55.4 us -> 66.4 us
    all_to_all x10 -> x8, blocking collectives: 115 us -> 88.6 us  [swap(): return lax.all_to_all(blocks, axes, 0, 0, tiled=False)]
    all_to_all x5 -> x7, waiting for transfers between devices: 23 us -> 37.5 us  [swap(): return lax.all_to_all(blocks, axes, 0, 0, tiled=False)]
    all_to_all x5 -> x7, starting transfers between devices: 25.8 us -> 38.4 us  [swap(): return lax.all_to_all(blocks, axes, 0, 0, tiled=False)]
    unnamed x31 -> x29, local copies, waits for them, and re-layouts: 16.1 us -> 16.1 us
  transfers between devices with their start and end apart: 19 -> 21, of which waited for: 15 -> 18; matrix products, arithmetic and copies ran while one was open for 1% -> 1% of each run, Pallas kernels for 13% -> 13%
where the time goes in v5:
time: 322 us; the launch traced here: 317 us
  blocking collectives  88.6 us (28%)
  Pallas kernels  78.2 us (24%)
  starting transfers between devices  66.4 us (21%)
  waiting for transfers between devices  54.8 us (17%)
  local copies, waits for them, and re-layouts  21.8 us (7%)
  other arithmetic  5.24 us (2%)
    all_to_all x8, blocking collectives, swap(): return lax.all_to_all(blocks, axes, 0, 0, tiled=False)  88.6 us
    pallas_call x8, Pallas kernels, call(): pl.pallas_call(body, out_shape=[jax.ShapeDtypeStruct(shape, dtype) for sh...  78.2 us
    all_to_all x7, starting transfers between devices, swap(): return lax.all_to_all(blocks, axes, 0, 0, tiled=False)  38.4 us
    all_to_all x7, waiting for transfers between devices, swap(): return lax.all_to_all(blocks, axes, 0, 0, tiled=False)  37.5 us
    ppermute x14, starting transfers between devices, other_of_two(): lax.ppermute(values, axis, [(i, (i + 1) % count) for i in range(count)])  28 us
    ppermute x14, waiting for transfers between devices, other_of_two(): lax.ppermute(values, axis, [(i, (i + 1) % count) for i in range(count)])  17.3 us
    unnamed x29, local copies, waits for them, and re-layouts  16.1 us
  transfers between devices with their start and end apart: 21, of which 18 were waited for; matrix products, arithmetic and copies ran while one was open for 1% of the time, Pallas kernels for 13%

profile of v5, /device:TPU:1, one launch (start us, length us, event | category | flops | bytes accessed | tf_op | source)
XLA Modules:
  0.0 317.4 jit_solution(5544673424295180904)
XLA Ops:
  2.4 3.3 %collective-permute-start = (bf16[256,128]{1,0:T(8,128)(2,1)S(1)}, bf16[256,128]{1,0:T(8,128)(2,1)S(1)}, u32[]{:S(2)}, u32[]{:S(2)}) collective-permute-start(bf16[256,128]{1,0:T(8,128)(2,1)S(1)} %constant_dynamic-slice_fusion.4), channel_id=1, source_target_pairs={{0,1},{1,0},{2,3},{3,2},{4,5},{5,4},{6,7},{7,6},{8,9},{9,8},{10,11... | collective-permute-start | bytes 196616 | tf_op jit(solution)/shard_map/ppermute | solution.py:37
  7.3 5.0 %all-to-all-start = ((bf16[16,16,128]{2,1,0:T(8,128)(2,1)}), bf16[16,16,128]{2,1,0:T(8,128)(2,1)S(1)}, u32[]{:S(2)}, u32[]{:S(2)}) async-start(bf16[16,16,128]{2,1,0:T(8,128)(2,1)} %bitcast), calls=%async_computation | async-start | bytes 131072 | tf_op jit(solution)/shard_map/all_to_all | solution.py:27
  13.0 5.8 %all-to-all-done = bf16[16,16,128]{2,1,0:T(8,128)(2,1)S(1)} async-done(((bf16[16,16,128]{2,1,0:T(8,128)(2,1)}), bf16[16,16,128]{2,1,0:T(8,128)(2,1)S(1)}, u32[]{:S(2)}, u32[]{:S(2)}) %all-to-all-start) | async-done | bytes 65568 | tf_op jit(solution)/shard_map/all_to_all | solution.py:27
  19.4 8.2 %all-to-all-start.1 = ((bf16[8,16,128]{2,1,0:T(8,128)(2,1)}), bf16[8,16,128]{2,1,0:T(8,128)(2,1)S(1)}, u32[]{:S(2)}, u32[]{:S(2)}) async-start(bf16[8,16,128]{2,1,0:T(8,128)(2,1)} %broadcast_in_dim.28), calls=%async_computation.1 | async-start | bytes 65536 | tf_op jit(solution)/shard_map/all_to_all | solution.py:27
  28.4 6.2 %all-to-all-done.1 = bf16[8,16,128]{2,1,0:T(8,128)(2,1)S(1)} async-done(((bf16[8,16,128]{2,1,0:T(8,128)(2,1)}), bf16[8,16,128]{2,1,0:T(8,128)(2,1)S(1)}, u32[]{:S(2)}, u32[]{:S(2)}) %all-to-all-start.1) | async-done | bytes 32800 | tf_op jit(solution)/shard_map/all_to_all | solution.py:27
  35.2 3.5 %all-to-all-start.2 = ((bf16[16,16,128]{2,1,0:T(8,128)(2,1)}), bf16[16,16,128]{2,1,0:T(8,128)(2,1)S(1)}, u32[]{:S(2)}, u32[]{:S(2)}) async-start(bf16[16,16,128]{2,1,0:T(8,128)(2,1)} %broadcast_in_dim.29), calls=%async_computation.2 | async-start | bytes 131072 | tf_op jit(solution)/shard_map/all_to_all | solution.py:27
  39.4 5.7 %all-to-all-done.2 = bf16[16,16,128]{2,1,0:T(8,128)(2,1)S(1)} async-done(((bf16[16,16,128]{2,1,0:T(8,128)(2,1)}), bf16[16,16,128]{2,1,0:T(8,128)(2,1)S(1)}, u32[]{:S(2)}, u32[]{:S(2)}) %all-to-all-start.2) | async-done | bytes 65568 | tf_op jit(solution)/shard_map/all_to_all | solution.py:27
  45.1 4.4 %collective-permute-start.1 = (bf16[16,16,128]{2,1,0:T(8,128)(2,1)S(1)}, bf16[16,16,128]{2,1,0:T(8,128)(2,1)S(1)}, u32[]{:S(2)}, u32[]{:S(2)}) collective-permute-start(bf16[16,16,128]{2,1,0:T(8,128)(2,1)S(1)} %all-to-all-done.2), channel_id=1, source_target_pairs={{0,1},{1,0},{2,3},{3,2},{4,5},{5,4},{6,7},{7,6},{8,9},{9,8},{10,11... | collective-permute-start | bytes 196616 | tf_op jit(solution)/shard_map/ppermute | solution.py:37
  52.5 3.6 %all-to-all-start.3 = ((bf16[8,224,128]{2,1,0:T(8,128)(2,1)}), bf16[8,224,128]{2,1,0:T(8,128)(2,1)S(1)}, u32[]{:S(2)}, u32[]{:S(2)}) async-start(bf16[8,224,128]{2,1,0:T(8,128)(2,1)} %broadcast_in_dim.30), calls=%async_computation.3 | async-start | bytes 917504 | tf_op jit(solution)/shard_map/all_to_all | solution.py:27
  56.1 21.4 %pivots_factor.1.inv_ref = f32[512,512]{1,0:T(8,128)S(1)} custom-call(bf16[512,128]{1,0:T(8,128)(2,1)S(1)} %bitcast.77), custom_call_target="tpu_custom_call" | custom-call | flops 22000001024 | bytes 66000000 | tf_op jit(solution)/shard_map/pivots_factor/pallas_call | solution.py:374
  79.8 8.0 %setup_factor.1 = (bf16[1024,512]{1,0:T(8,128)(2,1)S(1)}, bf16[1024,512]{1,0:T(8,128)(2,1)S(1)}, bf16[1024,512]{1,0:T(8,128)(2,1)S(1)}, bf16[1024,256]{1,0:T(8,128)(2,1)S(1)}, f32[32,48,128]{2,1,0:T(8,128)S(1)}) custom-call(f32[512,512]{1,0:T(8,128)S(1)} %copy-done.9, bf16[512,128]{1,0:T(8,128)(2,1)S(1)} %bitcast.78, bf16[1024,128]{1,0:T(8,128)(2,1)S(1)} %bitcast.76, ...), custom_call_target="tpu_custom_call" | custom-call | flops 10000000000 | bytes 30000000 | tf_op jit(solution)/shard_map/setup_factor/pallas_call | solution.py:374
  92.8 12.2 %all_to_all.75 = f32[16,48,128]{2,1,0:T(8,128)S(1)} all-to-all(f32[16,48,128]{2,1,0:T(8,128)S(1)} %dynamic-slice_add_fusion), channel_id=1, replica_groups=mesh['x'=4,'z'=8,'yh'=2,'yl'=2,'c'=2] {'x','yh','yl'}, dimensions={0} | all-to-all | bytes 786432 | tf_op jit(solution)/shard_map/all_to_all | solution.py:27
  105.1 11.3 %all_to_all.76 = f32[16,48,128]{2,1,0:T(8,128)S(1)} all-to-all(f32[16,48,128]{2,1,0:T(8,128)S(1)} %broadcast_in_dim.32), channel_id=1, replica_groups=mesh['x'=4,'z'=8,'yh'=2,'yl'=2,'c'=2] {'x','yh','yl'}, dimensions={0} | all-to-all | bytes 786432 | tf_op jit(solution)/shard_map/all_to_all | solution.py:27
  120.7 4.3 %all-to-all-start.6 = ((bf16[16,256,128]{2,1,0:T(8,128)(2,1)}), bf16[16,256,128]{2,1,0:T(8,128)(2,1)}, u32[]{:S(2)}, u32[]{:S(2)}) async-start(bf16[16,256,128]{2,1,0:T(8,128)(2,1)} %broadcast_in_dim.31), calls=%async_computation.6 | async-start | bytes 2097152 | tf_op jit(solution)/shard_map/all_to_all | solution.py:27
  125.1 21.1 %gram_factor.1 = (f32[512,512]{1,0:T(8,128)S(1)}, f32[32,512]{1,0:T(8,128)S(1)}) custom-call(f32[32,48,128]{2,1,0:T(8,128)S(1)} %pad_maximum_fusion.packed_ref), custom_call_target="tpu_custom_call" | custom-call | flops 22000001024 | bytes 66000000 | tf_op jit(solution)/shard_map/gram_factor/pallas_call | solution.py:374
  150.7 8.8 %begin.1 = (f32[8,32,128]{2,1,0:T(8,128)S(1)}, bf16[4096,256]{1,0:T(8,128)(2,1)}, f32[32,32,128]{2,1,0:T(8,128)S(1)}) custom-call(f32[32,512]{1,0:T(8,128)S(1)} %get-tuple-element.33.proj_ref, f32[512,512]{1,0:T(8,128)S(1)} %copy-done.5, f32[8,32,128]{2,1,0:T(8,128)S(1)} %fusion.2.targets_ref.res_ref, bf16[1024,512]{1,0:T(8,128)(2,1)S(1)} %get-tuple-element.29.high_ref, ...), custom_call_target="tpu_custom_call" | custom-call | flops 10000000000 | bytes 30000000 | tf_op jit(solution)/shard_map/begin/pallas_call | solution.py:374
  162.0 6.8 %all-to-all-start.7 = ((f32[16,32,128]{2,1,0:T(8,128)}), f32[16,32,128]{2,1,0:T(8,128)S(1)}, u32[]{:S(2)}, u32[]{:S(2)}) async-start(f32[16,32,128]{2,1,0:T(8,128)} %slice_add_fusion.2), calls=%async_computation.7 | async-start | bytes 524288 | tf_op jit(solution)/shard_map/all_to_all | solution.py:27
  168.8 7.6 %all-to-all-done.7 = f32[16,32,128]{2,1,0:T(8,128)S(1)} async-done(((f32[16,32,128]{2,1,0:T(8,128)}), f32[16,32,128]{2,1,0:T(8,128)S(1)}, u32[]{:S(2)}, u32[]{:S(2)}) %all-to-all-start.7) | async-done | bytes 262176 | tf_op jit(solution)/shard_map/all_to_all | solution.py:27
  176.5 14.8 %all_to_all.77.image_ref = f32[8,32,128]{2,1,0:T(8,128)S(1)} all-to-all(f32[8,32,128]{2,1,0:T(8,128)S(1)} %broadcast_in_dim.34), channel_id=1, replica_groups=mesh['x'=4,'z'=8,'yh'=2,'yl'=2,'c'=2] {'z'}, dimensions={0} | all-to-all | bytes 262144 | tf_op jit(solution)/shard_map/all_to_all | solution.py:27
  193.1 3.3 %collective-permute-start.6 = (f32[16,640]{1,0:T(8,128)S(1)}, f32[16,640]{1,0:T(8,128)S(1)}, u32[]{:S(2)}, u32[]{:S(2)}) collective-permute-start(f32[16,640]{1,0:T(8,128)S(1)} %constant_dynamic-slice_fusion.1), channel_id=1, source_target_pairs={{0,1},{1,0},{2,3},{3,2},{4,5},{5,4},{6,7},{7,6},{8,9},{9,8},{10,11... | collective-permute-start | bytes 122888 | tf_op jit(solution)/shard_map/ppermute | solution.py:37
  198.5 3.2 collective-permute-done.7
  201.7 9.0 %all_to_all.78 = f32[8,16,640]{2,1,0:T(8,128)S(1)} all-to-all(f32[8,16,640]{2,1,0:T(8,128)S(1)} %broadcast_in_dim.35), channel_id=1, replica_groups=mesh['x'=4,'z'=8,'yh'=2,'yl'=2,'c'=2] {'x','yl'}, dimensions={0} | all-to-all | bytes 655360 | tf_op jit(solution)/shard_map/all_to_all | solution.py:27
  216.6 8.8 %advance.2 = (f32[8,32,128]{2,1,0:T(8,128)S(1)}, f32[8,32,128]{2,1,0:T(8,128)S(1)}, f32[8,32,128]{2,1,0:T(8,128)S(1)}, f32[32,512]{1,0:T(8,128)S(1)}, f32[32,32,128]{2,1,0:T(8,128)S(1)}) custom-call(f32[32,640]{1,0:T(8,128)S(1)} %pad_maximum_fusion.2.packed_ref, f32[8,32,128]{2,1,0:T(8,128)S(1)} %all_to_all.77.image_ref, ...), custom_call_target="tpu_custom_call" | custom-call | flops 10000000000 | bytes 30000000 | tf_op jit(solution)/shard_map/advance/pallas_call | solution.py:374
  227.1 11.0 %all_to_all.79 = f32[16,32,128]{2,1,0:T(8,128)S(1)} all-to-all(f32[16,32,128]{2,1,0:T(8,128)S(1)} %slice_add_fusion.1), channel_id=1, replica_groups=mesh['x'=4,'z'=8,'yh'=2,'yl'=2,'c'=2] {'x','yh','yl'}, dimensions={0} | all-to-all | bytes 524288 | tf_op jit(solution)/shard_map/all_to_all | solution.py:27
  238.2 10.3 %all_to_all.80.image_ref = f32[8,32,128]{2,1,0:T(8,128)S(1)} all-to-all(f32[8,32,128]{2,1,0:T(8,128)S(1)} %broadcast_in_dim.38), channel_id=1, replica_groups=mesh['x'=4,'z'=8,'yh'=2,'yl'=2,'c'=2] {'z'}, dimensions={0} | all-to-all | bytes 262144 | tf_op jit(solution)/shard_map/all_to_all | solution.py:27
  250.4 3.1 collective-permute-start.10
  255.6 3.2 collective-permute-done.11
  258.8 9.0 %all_to_all.81 = f32[8,16,640]{2,1,0:T(8,128)S(1)} all-to-all(f32[8,16,640]{2,1,0:T(8,128)S(1)} %broadcast_in_dim.39), channel_id=1, replica_groups=mesh['x'=4,'z'=8,'yh'=2,'yl'=2,'c'=2] {'x','yl'}, dimensions={0} | all-to-all | bytes 655360 | tf_op jit(solution)/shard_map/all_to_all | solution.py:27
  273.9 8.9 %advance.3 = (f32[8,32,128]{2,1,0:T(8,128)S(1)}, f32[8,32,128]{2,1,0:T(8,128)S(1)}, f32[8,32,128]{2,1,0:T(8,128)S(1)}, f32[32,512]{1,0:T(8,128)}, f32[32,32,128]{2,1,0:T(8,128)S(1)}) custom-call(f32[32,640]{1,0:T(8,128)S(1)} %pad_maximum_fusion.3.packed_ref, f32[8,32,128]{2,1,0:T(8,128)S(1)} %all_to_all.80.image_ref, ...), custom_call_target="tpu_custom_call" | custom-call | flops 10000000000 | bytes 30000000 | tf_op jit(solution)/shard_map/advance/pallas_call | solution.py:374
  284.5 11.0 %all_to_all.82 = f32[16,32,128]{2,1,0:T(8,128)S(1)} all-to-all(f32[16,32,128]{2,1,0:T(8,128)S(1)} %slice_add_fusion), channel_id=1, replica_groups=mesh['x'=4,'z'=8,'yh'=2,'yl'=2,'c'=2] {'x','yh','yl'}, dimensions={0} | all-to-all | bytes 524288 | tf_op jit(solution)/shard_map/all_to_all | solution.py:27
  296.5 6.8 %all-to-all-start.14 = ((f32[256,1,128]{2,1,0:T(1,128)}), f32[256,1,128]{2,1,0:T(1,128)S(1)}, u32[]{:S(2)}, u32[]{:S(2)}) async-start(f32[256,1,128]{2,1,0:T(1,128)} %broadcast_in_dim.41), calls=%async_computation.14 | async-start | bytes 262144 | tf_op jit(solution)/shard_map/all_to_all | solution.py:27
  304.0 12.3 %all-to-all-done.14 = f32[256,1,128]{2,1,0:T(1,128)S(1)} async-done(((f32[256,1,128]{2,1,0:T(1,128)}), f32[256,1,128]{2,1,0:T(1,128)S(1)}, u32[]{:S(2)}, u32[]{:S(2)}) %all-to-all-start.14) | async-done | bytes 131104 | tf_op jit(solution)/shard_map/all_to_all | solution.py:27
  (116 shorter events, 54.2 us)
Async XLA Ops:
  2.4 4.2 %collective-permute-start = (bf16[256,128]{1,0:T(8,128)(2,1)S(1)}, bf16[256,128]{1,0:T(8,128)(2,1)S(1)}, u32[]{:S(2)}, u32[]{:S(2)}) collective-permute-start(bf16[256,128]{1,0:T(8,128)(2,1)S(1)} %constant_dynamic-slice_fusion.4), channel_id=1, source_target_pairs={{0,1},{1,0},{2,3},{3,2},{4,5},{5,4},{6,7},{7,6},{8,9},{9,8},{10,11... | collective-permute-start | bytes 196616 | tf_op jit(solution)/shard_map/ppermute | solution.py:37
  7.3 11.5 %all-to-all-start = ((bf16[16,16,128]{2,1,0:T(8,128)(2,1)}), bf16[16,16,128]{2,1,0:T(8,128)(2,1)S(1)}, u32[]{:S(2)}, u32[]{:S(2)}) async-start(bf16[16,16,128]{2,1,0:T(8,128)(2,1)} %bitcast), calls=%async_computation | async-start | bytes 131072 | tf_op jit(solution)/shard_map/all_to_all | solution.py:27
  12.3 37.2 %collective-permute-start.2 = (bf16[128,128]{1,0:T(8,128)(2,1)}, bf16[128,128]{1,0:T(8,128)(2,1)S(1)}, u32[]{:S(2)}, u32[]{:S(2)}) collective-permute-start(bf16[128,128]{1,0:T(8,128)(2,1)} %param.3), channel_id=1, source_target_pairs={{0,1},{1,0},{2,3},{3,2},{4,5},{5,4},{6,7},{7,6},{8,9},{9,8},{10,11... | collective-permute-start | bytes 98312 | tf_op jit(solution)/shard_map/ppermute | solution.py:37
  19.4 15.1 %all-to-all-start.1 = ((bf16[8,16,128]{2,1,0:T(8,128)(2,1)}), bf16[8,16,128]{2,1,0:T(8,128)(2,1)S(1)}, u32[]{:S(2)}, u32[]{:S(2)}) async-start(bf16[8,16,128]{2,1,0:T(8,128)(2,1)} %broadcast_in_dim.28), calls=%async_computation.1 | async-start | bytes 65536 | tf_op jit(solution)/shard_map/all_to_all | solution.py:27
  35.2 10.0 %all-to-all-start.2 = ((bf16[16,16,128]{2,1,0:T(8,128)(2,1)}), bf16[16,16,128]{2,1,0:T(8,128)(2,1)S(1)}, u32[]{:S(2)}, u32[]{:S(2)}) async-start(bf16[16,16,128]{2,1,0:T(8,128)(2,1)} %broadcast_in_dim.29), calls=%async_computation.2 | async-start | bytes 131072 | tf_op jit(solution)/shard_map/all_to_all | solution.py:27
  45.1 5.3 %collective-permute-start.1 = (bf16[16,16,128]{2,1,0:T(8,128)(2,1)S(1)}, bf16[16,16,128]{2,1,0:T(8,128)(2,1)S(1)}, u32[]{:S(2)}, u32[]{:S(2)}) collective-permute-start(bf16[16,16,128]{2,1,0:T(8,128)(2,1)S(1)} %all-to-all-done.2), channel_id=1, source_target_pairs={{0,1},{1,0},{2,3},{3,2},{4,5},{5,4},{6,7},{7,6},{8,9},{9,8},{10,11... | collective-permute-start | bytes 196616 | tf_op jit(solution)/shard_map/ppermute | solution.py:37
  52.5 26.0 %all-to-all-start.3 = ((bf16[8,224,128]{2,1,0:T(8,128)(2,1)}), bf16[8,224,128]{2,1,0:T(8,128)(2,1)S(1)}, u32[]{:S(2)}, u32[]{:S(2)}) async-start(bf16[8,224,128]{2,1,0:T(8,128)(2,1)} %broadcast_in_dim.30), calls=%async_computation.3 | async-start | bytes 917504 | tf_op jit(solution)/shard_map/all_to_all | solution.py:27
  78.6 1.2 copy-start.9
  90.4 2.3 collective-permute-start.3
  116.4 4.2 %collective-permute-start.4 = (f32[16,48,128]{2,1,0:T(8,128)S(1)}, f32[16,48,128]{2,1,0:T(8,128)S(1)}, u32[]{:S(2)}, u32[]{:S(2)}) collective-permute-start(f32[16,48,128]{2,1,0:T(8,128)S(1)} %all_to_all.76), channel_id=1, source_target_pairs={{0,1},{1,0},{2,3},{3,2},{4,5},{5,4},{6,7},{7,6},{8,9},{9,8},{10,11... | collective-permute-start | bytes 1179656 | tf_op jit(solution)/shard_map/ppermute | solution.py:37
  120.7 26.5 %all-to-all-start.6 = ((bf16[16,256,128]{2,1,0:T(8,128)(2,1)}), bf16[16,256,128]{2,1,0:T(8,128)(2,1)}, u32[]{:S(2)}, u32[]{:S(2)}) async-start(bf16[16,256,128]{2,1,0:T(8,128)(2,1)} %broadcast_in_dim.31), calls=%async_computation.6 | async-start | bytes 2097152 | tf_op jit(solution)/shard_map/all_to_all | solution.py:27
  146.2 1.0 copy-start.4
  147.2 1.2 copy-start.1
  148.4 1.2 copy-start.5
  149.6 1.0 copy-start.11
  159.5 1.8 collective-permute-start.5
  162.0 14.4 %all-to-all-start.7 = ((f32[16,32,128]{2,1,0:T(8,128)}), f32[16,32,128]{2,1,0:T(8,128)S(1)}, u32[]{:S(2)}, u32[]{:S(2)}) async-start(f32[16,32,128]{2,1,0:T(8,128)} %slice_add_fusion.2), calls=%async_computation.7 | async-start | bytes 524288 | tf_op jit(solution)/shard_map/all_to_all | solution.py:27
  191.2 1.2 copy-start.2
  193.1 4.2 %collective-permute-start.6 = (f32[16,640]{1,0:T(8,128)S(1)}, f32[16,640]{1,0:T(8,128)S(1)}, u32[]{:S(2)}, u32[]{:S(2)}) collective-permute-start(f32[16,640]{1,0:T(8,128)S(1)} %constant_dynamic-slice_fusion.1), channel_id=1, source_target_pairs={{0,1},{1,0},{2,3},{3,2},{4,5},{5,4},{6,7},{7,6},{8,9},{9,8},{10,11... | collective-permute-start | bytes 122888 | tf_op jit(solution)/shard_map/ppermute | solution.py:37
  197.3 4.4 %collective-permute-start.7 = (f32[16,640]{1,0:T(8,128)S(1)}, f32[16,640]{1,0:T(8,128)S(1)}, u32[]{:S(2)}, u32[]{:S(2)}) collective-permute-start(f32[16,640]{1,0:T(8,128)S(1)} %dynamic-slice_add_fusion.3), channel_id=1, source_target_pairs={{0,4},{4,0},{1,5},{5,1},{2,6},{6,2},{3,7},{7,3},{8,12},{12,8},{9,1... | collective-permute-start | bytes 122888 | tf_op jit(solution)/shard_map/ppermute | solution.py:37
  210.7 3.6 %collective-permute-start.8 = (f32[16,640]{1,0:T(8,128)S(1)}, f32[16,640]{1,0:T(8,128)S(1)}, u32[]{:S(2)}, u32[]{:S(2)}) collective-permute-start(f32[16,640]{1,0:T(8,128)S(1)} %reduce_sum.114), channel_id=1, source_target_pairs={{0,1},{1,0},{2,3},{3,2},{4,5},{5,4},{6,7},{7,6},{8,9},{9,8},{10,11... | collective-permute-start | bytes 122888 | tf_op jit(solution)/shard_map/ppermute | solution.py:37
  214.3 1.2 copy-start.6
  215.5 1.0 copy-start.12
  225.5 1.6 collective-permute-start.9
  248.6 1.2 copy-start.3
  250.4 4.0 %collective-permute-start.10 = (f32[16,640]{1,0:T(8,128)S(1)}, f32[16,640]{1,0:T(8,128)S(1)}, u32[]{:S(2)}, u32[]{:S(2)}) collective-permute-start(f32[16,640]{1,0:T(8,128)S(1)} %constant_dynamic-slice_fusion), channel_id=1, source_target_pairs={{0,1},{1,0},{2,3},{3,2},{4,5},{5,4},{6,7},{7,6},{8,9},{9,8},{10,11... | collective-permute-start | bytes 122888 | tf_op jit(solution)/shard_map/ppermute | solution.py:37
  254.4 4.4 %collective-permute-start.11 = (f32[16,640]{1,0:T(8,128)S(1)}, f32[16,640]{1,0:T(8,128)S(1)}, u32[]{:S(2)}, u32[]{:S(2)}) collective-permute-start(f32[16,640]{1,0:T(8,128)S(1)} %dynamic-slice_add_fusion.2), channel_id=1, source_target_pairs={{0,4},{4,0},{1,5},{5,1},{2,6},{6,2},{3,7},{7,3},{8,12},{12,8},{9,1... | collective-permute-start | bytes 122888 | tf_op jit(solution)/shard_map/ppermute | solution.py:37
  267.8 3.8 %collective-permute-start.12 = (f32[16,640]{1,0:T(8,128)S(1)}, f32[16,640]{1,0:T(8,128)S(1)}, u32[]{:S(2)}, u32[]{:S(2)}) collective-permute-start(f32[16,640]{1,0:T(8,128)S(1)} %reduce_sum.117), channel_id=1, source_target_pairs={{0,1},{1,0},{2,3},{3,2},{4,5},{5,4},{6,7},{7,6},{8,9},{9,8},{10,11... | collective-permute-start | bytes 122888 | tf_op jit(solution)/shard_map/ppermute | solution.py:37
  271.7 1.2 copy-start.7
  272.9 1.0 copy-start.13
  282.8 1.6 collective-permute-start.13
  296.5 19.8 %all-to-all-start.14 = ((f32[256,1,128]{2,1,0:T(1,128)}), f32[256,1,128]{2,1,0:T(1,128)S(1)}, u32[]{:S(2)}, u32[]{:S(2)}) async-start(f32[256,1,128]{2,1,0:T(1,128)} %broadcast_in_dim.41), calls=%async_computation.14 | async-start | bytes 262144 | tf_op jit(solution)/shard_map/all_to_all | solution.py:27
  (3 other events, 2.8 us)
